TPU v7x, 32 devices: a whole 2x2x4 slice. The times are simulated.
32 devices in a mesh: groups: 2 (over x), img: 16 (over z, y, core).
Axes of the slice: x: 2, y: 2, z: 4, core: 2. Of those that a mesh axis runs over, the one named last changes fastest.
Arguments:
- caches: bfloat16 [32, 768, 1024], P(('groups', 'img')), parts along dimension 0, may hold values from -170 to 170
- owner_slot: int32 [32], P('groups'), parts along dimension 0, may hold values from 0 to 15, each once
- pairs: int32 [32, 2], P('groups'), parts along dimension 0, may hold values from 0 to 15, as said below
- block_mask: int32 [32, 12, 12], P(('groups', 'img')), parts along dimension 0, may hold values from 0 to 1, as said below
- cotangent: bfloat16 [32, 768, 768], P(('groups', 'img')), parts along dimension 0, may hold values from -6 to 6
- embed_weight: bfloat16 [1024, 768], replicated, may hold values from -0.1875 to 0.1875
- query_weight: bfloat16 [768, 512], replicated, may hold values from -2 to 2
- key_weight: bfloat16 [768, 512], replicated, may hold values from -2 to 2
- value_weight: bfloat16 [768, 512], replicated, may hold values from -0.21875 to 0.21875
- out_weight: bfloat16 [768, 512], replicated, may hold values from -0.25 to 0.25
Outputs:
- attended: bfloat16 [32, 768, 768], P(('groups', 'img')), parts along dimension 0
- gradients: float32 [1536, 2048], P(('groups', 'img')), parts along dimension 0
There are 2 independent parts, one for each index of `groups`. A program takes and returns all parts, laid end to end along the dimension named above; an argument that names none is the same for every part. Nothing has to cross between parts.
Inputs may be any that keep to these rules, and one draw needn't show every extreme that they name: `pairs`: each row names two different images. `block_mask`: block (i, i) is live in every pair.
All inputs are finite; a program needn't handle non-finite values.
Results may differ from a plain program's by a relative error of at most 0.012.
Values may be sent and summed in bfloat16 or wider, within the bound.
No kernel may reach another device: no remote copies, remote signals or barrier semaphores. Data moves between devices by JAX's collectives and lax.ppermute only.
A program may use at most 128 MiB of HBM per device.

v0:
```python
import math

import jax
import jax.numpy as jnp
from jax import lax
from jax.sharding import PartitionSpec as P

HEADS = 8
BLOCK = 64


def layer_normed(tokens):
    values_f = tokens.astype(jnp.float32)
    centred = values_f - jnp.mean(values_f, axis=-1, keepdims=True)
    spread_sq = jnp.mean(centred * centred, axis=-1, keepdims=True)
    return (centred * lax.rsqrt(spread_sq + 1e-06)).astype(jnp.bfloat16)


def split_heads(matrix, heads):
    length, width = matrix.shape
    return matrix.reshape(length, heads, width // heads).transpose(1, 0, 2)


def merge_heads(stacked):
    heads, length, hsize = stacked.shape
    return stacked.transpose(1, 0, 2).reshape(length, heads * hsize)


def pair_pass(
    query_tokens,
    key_tokens,
    mask_blocks,
    cotangent,
    query_weight,
    key_weight,
    value_weight,
    out_weight,
    heads,
    block,
):
    query_normed = layer_normed(query_tokens)
    key_normed = layer_normed(key_tokens)
    queries = jnp.dot(query_normed, query_weight, preferred_element_type=jnp.float32).astype(
        jnp.bfloat16
    )
    keys_all = jnp.dot(key_normed, key_weight, preferred_element_type=jnp.float32).astype(
        jnp.bfloat16
    )
    values_all = jnp.dot(key_normed, value_weight, preferred_element_type=jnp.float32).astype(
        jnp.bfloat16
    )
    grad_context = jnp.dot(cotangent, out_weight, preferred_element_type=jnp.float32).astype(
        jnp.bfloat16
    )
    live_mask = jnp.repeat(jnp.repeat(mask_blocks, block, axis=0), block, axis=1) > 0
    scaling = 1.0 / math.sqrt(queries.shape[1] // heads)

    def one_head(operands):
        head_query, head_key, head_value, head_grad = operands
        scores = jnp.dot(head_query, head_key.T, preferred_element_type=jnp.float32) * scaling
        masked = jnp.where(live_mask, scores, -jnp.inf)
        row_max = jnp.max(masked, axis=1, keepdims=True)
        weights = jnp.exp(masked - row_max)
        probability = weights / jnp.sum(weights, axis=1, keepdims=True)
        probability_low = probability.astype(jnp.bfloat16)
        context = jnp.dot(probability_low, head_value, preferred_element_type=jnp.float32).astype(
            jnp.bfloat16
        )
        grad_value = jnp.dot(
            probability_low.T, head_grad, preferred_element_type=jnp.float32
        ).astype(jnp.bfloat16)
        grad_prob = jnp.dot(head_grad, head_value.T, preferred_element_type=jnp.float32)
        inner_sum = jnp.sum(probability * grad_prob, axis=1, keepdims=True)
        grad_score = (probability * (grad_prob - inner_sum) * scaling).astype(jnp.bfloat16)
        grad_query = jnp.dot(grad_score, head_key, preferred_element_type=jnp.float32).astype(
            jnp.bfloat16
        )
        grad_key = jnp.dot(grad_score.T, head_query, preferred_element_type=jnp.float32).astype(
            jnp.bfloat16
        )
        return (context, grad_value, grad_query, grad_key)

    stacked = lax.map(
        one_head,
        (
            split_heads(queries, heads),
            split_heads(keys_all, heads),
            split_heads(values_all, heads),
            split_heads(grad_context, heads),
        ),
    )
    context, grad_value, grad_query, grad_key = [merge_heads(member) for member in stacked]
    attended = (
        query_tokens.astype(jnp.float32)
        + jnp.dot(context, out_weight.T, preferred_element_type=jnp.float32)
    ).astype(jnp.bfloat16)
    return (
        attended,
        (query_normed, key_normed, grad_query, grad_key, grad_value, cotangent, context),
    )


def gradient_rows(kept):
    query_normed, key_normed, grad_query, grad_key, grad_value, cotangent, context = kept
    return jnp.concatenate(
        [
            jnp.dot(query_normed.T, grad_query, preferred_element_type=jnp.float32),
            jnp.dot(key_normed.T, grad_key, preferred_element_type=jnp.float32),
            jnp.dot(key_normed.T, grad_value, preferred_element_type=jnp.float32),
            jnp.dot(cotangent.T, context, preferred_element_type=jnp.float32),
        ],
        axis=1,
    )


def embedded_of(tokens, embed_weight):
    shape_in = tokens.shape
    flat = tokens.reshape(-1, shape_in[-1])
    product = jnp.dot(flat, embed_weight, preferred_element_type=jnp.float32).astype(jnp.bfloat16)
    return product.reshape(shape_in[:-1] + (embed_weight.shape[1],))


def per_device(
    caches,
    owner_slot,
    pairs,
    block_mask,
    cotangent,
    embed_weight,
    query_weight,
    key_weight,
    value_weight,
    out_weight,
):
    devices_img = lax.axis_size("img")
    images_here = caches.shape[0]
    length = caches.shape[1]
    pairs_here = block_mask.shape[0]
    width = caches.shape[-1]
    portion = length // devices_img
    pieces = caches.reshape(images_here, devices_img, portion, width)
    spread = lax.all_to_all(pieces, "img", split_axis=1, concat_axis=0, tiled=True)
    table = spread.reshape(images_here * devices_img, portion, width)
    slots = owner_slot[pairs].reshape(devices_img, pairs_here, 2).transpose(1, 2, 0)
    picked = table[slots]
    arrived = lax.all_to_all(picked, "img", split_axis=2, concat_axis=3, tiled=True)
    tokens = arrived.reshape(pairs_here, 2, length, width)
    tokens = embedded_of(tokens, embed_weight)
    attended, kept = pair_pass(
        tokens[0, 0],
        tokens[0, 1],
        block_mask[0],
        cotangent[0],
        query_weight,
        key_weight,
        value_weight,
        out_weight,
        HEADS,
        BLOCK,
    )
    attended_list = [attended]
    attended_all = jnp.stack(attended_list)
    inverse = 1.0 / (pairs_here * devices_img)
    total = gradient_rows(kept)
    summed = lax.psum_scatter(total, "img", scatter_dimension=0, tiled=True)
    return (attended_all, summed * inverse)


def solution(mesh):
    placed = (
        P(("groups", "img"), None, None),
        P("groups"),
        P("groups", None),
        P(("groups", "img"), None, None),
        P(("groups", "img"), None, None),
        P(),
        P(),
        P(),
        P(),
        P(),
    )
    return jax.shard_map(
        per_device,
        mesh=mesh,
        in_specs=placed,
        out_specs=(P(("groups", "img"), None, None), P(("groups", "img"), None)),
        check_vma=False,
    )
```

profile of v0, /device:TPU:0, one launch (start us, length us, event | category | flops | bytes accessed | tf_op | source)
XLA Modules:
  0.0 350.0 jit_solution(1653082750887615736)
XLA Ops:
  7.2 7.5 %all-to-all-start = ((bf16[1,16,48,1024]{3,2,0,1:T(8,128)(2,1)}), bf16[1,16,48,1024]{3,2,0,1:T(8,128)(2,1)S(1)}, u32[]{:S(2)}, u32[]{:S(2)}) async-start(bf16[1,16,48,1024]{3,2,0,1:T(8,128)(2,1)} %bitcast.197), calls=%async_computation | async-start | bytes 3145728 | tf_op jit(solution)/shard_map/all_to_all | solution.py:142
  15.9 30.8 %all-to-all-done = bf16[1,16,48,1024]{3,2,0,1:T(8,128)(2,1)S(1)} async-done(((bf16[1,16,48,1024]{3,2,0,1:T(8,128)(2,1)}), bf16[1,16,48,1024]{3,2,0,1:T(8,128)(2,1)S(1)}, u32[]{:S(2)}, u32[]{:S(2)}) %all-to-all-start) | async-done | bytes 1572896 | tf_op jit(solution)/shard_map/all_to_all | solution.py:142
  46.7 2.4 gather_fusion.1
  49.1 4.0 %copy.39 = bf16[1,2,16,48,1024]{4,3,1,0,2:T(8,128)(2,1)} copy(bf16[1,2,16,48,1024]{4,3,2,1,0:T(8,128)(2,1)} %bitcast.182) | data formatting | bytes 6291456 | tf_op jit(solution)/shard_map/gather | solution.py:145
  53.2 9.3 %all-to-all-start.1 = ((bf16[1,2,16,48,1024]{4,3,1,0,2:T(8,128)(2,1)}), bf16[1,2,16,48,1024]{4,3,1,0,2:T(8,128)(2,1)}, u32[]{:S(2)}, u32[]{:S(2)}) async-start(bf16[1,2,16,48,1024]{4,3,1,0,2:T(8,128)(2,1)} %copy.39), calls=%async_computation.1 | async-start | bytes 6291456 | tf_op jit(solution)/shard_map/all_to_all | solution.py:146
  66.4 55.5 %all-to-all-done.1 = bf16[1,2,16,48,1024]{4,3,1,0,2:T(8,128)(2,1)} async-done(((bf16[1,2,16,48,1024]{4,3,1,0,2:T(8,128)(2,1)}), bf16[1,2,16,48,1024]{4,3,1,0,2:T(8,128)(2,1)}, u32[]{:S(2)}, u32[]{:S(2)}) %all-to-all-start.1) | async-done | bytes 3145760 | tf_op jit(solution)/shard_map/all_to_all | solution.py:146
  121.9 2.4 copy.40
  124.3 2.8 convolution_convert_fusion.4
  131.5 2.3 convolution_convert_fusion.7
  134.7 3.4 convolution_convert_fusion.8
  139.8 85.0 %while.17 = (s32[]{:T(128)}, bf16[8,768,64]{1,2,0:T(8,128)(2,1)}, bf16[8,768,64]{1,2,0:T(8,128)(2,1)}, bf16[8,768,64]{1,2,0:T(8,128)(2,1)}, bf16[8,768,64]{1,2,0...) while((s32[]{:T(128)}, bf16[8,768,64]{1,2,0:T(8,128)(2,1)}, ...), condition=%wide.region_8.9_spmd.clone, body=%wide.region_4.8_spmd.clone.sunk | while | flops 464385792 | bytes 33088676 | solution.py:83
  146.3 2.2 fusion.115
  156.9 2.2 fusion.115
  167.6 2.2 fusion.115
  178.2 2.2 fusion.115
  199.4 2.2 fusion.115
  210.1 2.2 fusion.115
  220.7 2.2 fusion.115
  224.8 2.6 fusion.58
  232.6 3.1 pad_maximum_fusion
  235.7 6.6 %copy.48 = f32[768,2048]{1,0:T(8,128)} copy(f32[768,2048]{0,1:T(8,128)} %pad_maximum_fusion) | data formatting | bytes 12582912
  243.5 3.5 fusion.55
  246.9 91.5 %reduce-scatter.4.cloned.1.call-done = f32[48,2048]{1,0:T(8,128)} async-done(((f32[768,2048]{1,0:T(8,128)}), f32[48,2048]{1,0:T(8,128)}) %reduce-scatter.4.cloned.1.call-update) | async-done | bytes 393232
  340.9 2.3 copy.46
  (151 shorter events, 90.0 us)
Async XLA Ops:
  7.2 117.1 %copy-start = (bf16[1024,768]{1,0:T(8,128)(2,1)S(1)}, bf16[1024,768]{1,0:T(8,128)(2,1)}, u32[]{:S(2)}) copy-start(bf16[1024,768]{1,0:T(8,128)(2,1)} %param.17) | copy-start | bytes 4718596
  7.2 7.6 %copy-start.8 = (s32[16,2]{0,1:T(2,128)S(1)}, s32[16,2]{0,1:T(2,128)}, u32[]{:S(2)}) copy-start(s32[16,2]{0,1:T(2,128)} %param.14) | copy-start | bytes 388
  7.2 7.8 %copy-start.2 = (s32[16]{0:T(128)S(1)}, s32[16]{0:T(128)}, u32[]{:S(2)}) copy-start(s32[16]{0:T(128)} %param.13) | copy-start | bytes 196
  7.2 39.5 %all-to-all-start = ((bf16[1,16,48,1024]{3,2,0,1:T(8,128)(2,1)}), bf16[1,16,48,1024]{3,2,0,1:T(8,128)(2,1)S(1)}, u32[]{:S(2)}, u32[]{:S(2)}) async-start(bf16[1,16,48,1024]{3,2,0,1:T(8,128)(2,1)} %bitcast.197), calls=%async_computation | async-start | bytes 3145728 | tf_op jit(solution)/shard_map/all_to_all | solution.py:142
  53.2 9.4 %copy-start.9 = (bf16[1,768,768]{2,1,0:T(8,128)(2,1)S(1)}, bf16[1,768,768]{2,1,0:T(8,128)(2,1)}, u32[]{:S(2)}) copy-start(bf16[1,768,768]{2,1,0:T(8,128)(2,1)} %param.16) | copy-start | bytes 3538948
  53.2 68.7 %all-to-all-start.1 = ((bf16[1,2,16,48,1024]{4,3,1,0,2:T(8,128)(2,1)}), bf16[1,2,16,48,1024]{4,3,1,0,2:T(8,128)(2,1)}, u32[]{:S(2)}, u32[]{:S(2)}) async-start(bf16[1,2,16,48,1024]{4,3,1,0,2:T(8,128)(2,1)} %copy.39), calls=%async_computation.1 | async-start | bytes 6291456 | tf_op jit(solution)/shard_map/all_to_all | solution.py:146
  62.5 276.0 %reduce-scatter.4.cloned.1.call-start = ((), (), s32[]{:S(2)}) async-start(), calls=%async_computation.3 | async-start | bytes 6684672
  62.6 3.5 %copy-start.7 = (s32[1,12,12]{2,0,1:T(1,128)S(1)}, s32[1,12,12]{2,0,1:T(1,128)}, u32[]{:S(2)}) copy-start(s32[1,12,12]{2,0,1:T(1,128)} %param.15) | copy-start | bytes 1732
  127.1 1.4 copy-start.3
  127.1 1.7 copy-start.11
  129.9 1.6 copy-start.12
  139.8 1.2 copy-start.5
  146.3 4.2 %copy-start.6 = (bf16[8,768,64]{2,1,0:T(8,128)(2,1)S(1)}, bf16[8,768,64]{2,1,0:T(8,128)(2,1)}, u32[]{:S(2)}) copy-start(bf16[8,768,64]{2,1,0:T(8,128)(2,1)} %copy-done.5) | copy-start | bytes 2359300 | tf_op jit(solution)/shard_map/while
  156.9 4.2 %copy-start.6 = (bf16[8,768,64]{2,1,0:T(8,128)(2,1)S(1)}, bf16[8,768,64]{2,1,0:T(8,128)(2,1)}, u32[]{:S(2)}) copy-start(bf16[8,768,64]{2,1,0:T(8,128)(2,1)} %copy-done.5) | copy-start | bytes 2359300 | tf_op jit(solution)/shard_map/while
  167.6 4.2 %copy-start.6 = (bf16[8,768,64]{2,1,0:T(8,128)(2,1)S(1)}, bf16[8,768,64]{2,1,0:T(8,128)(2,1)}, u32[]{:S(2)}) copy-start(bf16[8,768,64]{2,1,0:T(8,128)(2,1)} %copy-done.5) | copy-start | bytes 2359300 | tf_op jit(solution)/shard_map/while
  178.2 4.2 %copy-start.6 = (bf16[8,768,64]{2,1,0:T(8,128)(2,1)S(1)}, bf16[8,768,64]{2,1,0:T(8,128)(2,1)}, u32[]{:S(2)}) copy-start(bf16[8,768,64]{2,1,0:T(8,128)(2,1)} %copy-done.5) | copy-start | bytes 2359300 | tf_op jit(solution)/shard_map/while
  188.8 4.2 %copy-start.6 = (bf16[8,768,64]{2,1,0:T(8,128)(2,1)S(1)}, bf16[8,768,64]{2,1,0:T(8,128)(2,1)}, u32[]{:S(2)}) copy-start(bf16[8,768,64]{2,1,0:T(8,128)(2,1)} %copy-done.5) | copy-start | bytes 2359300 | tf_op jit(solution)/shard_map/while
  199.4 4.2 %copy-start.6 = (bf16[8,768,64]{2,1,0:T(8,128)(2,1)S(1)}, bf16[8,768,64]{2,1,0:T(8,128)(2,1)}, u32[]{:S(2)}) copy-start(bf16[8,768,64]{2,1,0:T(8,128)(2,1)} %copy-done.5) | copy-start | bytes 2359300 | tf_op jit(solution)/shard_map/while
  210.1 4.2 %copy-start.6 = (bf16[8,768,64]{2,1,0:T(8,128)(2,1)S(1)}, bf16[8,768,64]{2,1,0:T(8,128)(2,1)}, u32[]{:S(2)}) copy-start(bf16[8,768,64]{2,1,0:T(8,128)(2,1)} %copy-done.5) | copy-start | bytes 2359300 | tf_op jit(solution)/shard_map/while
  220.7 4.2 %copy-start.6 = (bf16[8,768,64]{2,1,0:T(8,128)(2,1)S(1)}, bf16[8,768,64]{2,1,0:T(8,128)(2,1)}, u32[]{:S(2)}) copy-start(bf16[8,768,64]{2,1,0:T(8,128)(2,1)} %copy-done.5) | copy-start | bytes 2359300 | tf_op jit(solution)/shard_map/while
  224.8 2.6 copy-start.4
  224.8 2.6 copy-start.14
  228.5 2.2 copy-start.10
  243.5 99.7 %copy-start.1 = (bf16[1024,768]{1,0:T(8,128)(2,1)S(1)}, bf16[1024,768]{1,0:T(8,128)(2,1)}, u32[]{:S(2)}) copy-start(bf16[1024,768]{1,0:T(8,128)(2,1)} %param.17) | copy-start | bytes 4718596
  (8 other events, 9.3 us)
Sparse Core Ops, SparseCore 0:
  242.5 95.9 reduce-scatter.3
where the time goes:
time: 351 us; the launch traced here: 350 us
  waiting for transfers between devices  178 us (51%)
  matrix products  99.2 us (28%)
  local copies, waits for them, and re-layouts  29.2 us (8%)
  starting transfers between devices  16.9 us (5%)
  between operations  14.4 us (4%)
  other arithmetic  12.4 us (4%)
    unnamed x2, waiting for transfers between devices  91.6 us
    all_to_all x1, waiting for transfers between devices, per_device(): lax.all_to_all(picked, 'img', split_axis=2, concat_axis=3, tiled=True)  55.5 us
    all_to_all x1, waiting for transfers between devices, per_device(): lax.all_to_all(pieces, 'img', split_axis=1, concat_axis=0, tiled=True)  30.8 us
    dot_general x8, matrix products, one_head(): jnp.dot(probability_low.T, head_grad, preferred_element_type=jnp.float32)  17.7 us
    dot_general x8, matrix products, one_head(): jnp.dot(grad_score.T, head_query, preferred_element_type=jnp.float32)  16.7 us
    dot_general x8, matrix products, one_head(): jnp.dot(probability_low, head_value, preferred_element_type=jnp.float32)  15.6 us
    dot_general x8, matrix products, one_head(): jnp.dot(head_grad, head_value.T, preferred_element_type=jnp.float32)  14.5 us
    unnamed x29, local copies, waits for them, and re-layouts  11.8 us
  transfers between devices with their start and end apart: 3, of which 3 were waited for; matrix products, arithmetic and copies ran while one was open for 2% of the time, Pallas kernels for 0%

commit v1 on v0

v1 whole, which is shorter than its diff:
```python
import functools
import math

import jax
import jax.numpy as jnp
from jax import lax
from jax.experimental import pallas as pl
from jax.experimental.pallas import tpu as pltpu
from jax.sharding import PartitionSpec as P

HEADS = 8
BLOCK = 64
CHUNK = 256
DEAD = -1e30
F32 = jnp.float32
BF16 = jnp.bfloat16
VMEM = pl.BlockSpec(memory_space=pltpu.VMEM)
SMEM = pl.BlockSpec(memory_space=pltpu.SMEM)


def dot_nn(a, b):
    return lax.dot_general(a, b, (((1,), (0,)), ((), ())), preferred_element_type=F32)


def dot_nt(a, b):
    return lax.dot_general(a, b, (((1,), (1,)), ((), ())), preferred_element_type=F32)


def norm_columns(tokens):
    values_f = tokens.astype(F32)
    width = values_f.shape[0]
    centred = values_f - jnp.sum(values_f, axis=0, keepdims=True) * (1.0 / width)
    spread_sq = jnp.sum(centred * centred, axis=0, keepdims=True) * (1.0 / width)
    return (centred * lax.rsqrt(spread_sq + 1e-06)).astype(BF16)


def pick_body(owner_ref, pairs_ref, shares_ref, query_ref, key_ref):
    count = shares_ref.shape[0]

    def step(p, carry):
        query_ref[p] = shares_ref[owner_ref[pairs_ref[2 * p]]]
        key_ref[p] = shares_ref[owner_ref[pairs_ref[2 * p + 1]]]
        return carry

    lax.fori_loop(0, count, step, 0)


def pick(owner_slot, pairs, shares):
    out = jax.ShapeDtypeStruct(shares.shape, shares.dtype)
    return pl.pallas_call(
        pick_body,
        out_shape=(out, out),
        in_specs=[SMEM, SMEM, VMEM],
        out_specs=(VMEM, VMEM),
        name="pick_shares",
    )(owner_slot, pairs.reshape(-1), shares)


def key_body(heads, token_ref, kw_ref, vw_ref, aug_ref, normed_ref, kt_ref, k_ref, vt_ref, v_ref):
    length = token_ref.shape[1]
    hsize = kw_ref.shape[0] // heads
    for c in range(length // CHUNK):
        cols = pl.ds(c * CHUNK, CHUNK)
        normed = norm_columns(token_ref[:, cols])
        normed_ref[:, cols] = normed
        kt_ref[:, cols] = dot_nn(kw_ref[...], normed).astype(BF16)
        vt_ref[:, cols] = dot_nn(vw_ref[...], normed).astype(BF16)
    for h in range(heads):
        rows = pl.ds(h * hsize, hsize)
        k_ref[h] = jnp.concatenate([kt_ref[rows, :].T, aug_ref[...]], axis=1)
        v_ref[h] = vt_ref[rows, :].T


def key_side(tokens, kw, vw, aug, heads):
    width, length = tokens.shape
    att = kw.shape[0]
    hsize = att // heads
    flat = jax.ShapeDtypeStruct((att, length), BF16)
    return pl.pallas_call(
        functools.partial(key_body, heads),
        out_shape=(
            jax.ShapeDtypeStruct((width, length), BF16),
            flat,
            jax.ShapeDtypeStruct((heads, length, 2 * hsize), BF16),
            flat,
            jax.ShapeDtypeStruct((heads, length, hsize), BF16),
        ),
        in_specs=[VMEM] * 4,
        out_specs=(VMEM,) * 5,
        compiler_params=pltpu.CompilerParams(vmem_limit_bytes=40 * 2**20),
        name="key_side",
    )(tokens, kw, vw, aug)


def chunk_body(
    heads, first, last, token_ref, qw_ref, hot_ref, gt_ref, g_ref, cot_ref, knt_ref,
    kt_ref, k_ref, vt_ref, v_ref, *rest,
):
    if not first:
        gk_in, gv_in, q_in, o_in = rest[:4]
        rest = rest[4:]
    ctx_ref, gk_ref, gv_ref, gradq_ref, grado_ref = rest[:5]
    rest = rest[5:]
    if last:
        gradk_ref, gradv_ref = rest[:2]
        rest = rest[2:]
    qt_ref, qnat_ref, gq_ref = rest
    att = qw_ref.shape[0]
    hsize = att // heads
    normed = norm_columns(token_ref[...])
    qt_ref[...] = dot_nn(qw_ref[...], normed).astype(BF16)
    for h in range(heads):
        qnat_ref[h] = qt_ref[pl.ds(h * hsize, hsize), :].T
    scale = jnp.asarray(1.0 / math.sqrt(hsize), BF16)

    def one_head(h, carry):
        rows = pl.ds(pl.multiple_of(h * hsize, hsize), hsize)
        query_aug = jnp.concatenate([qt_ref[rows, :] * scale, hot_ref[...]], axis=0)
        scores = dot_nn(k_ref[h], query_aug)
        top = jnp.max(scores, axis=0, keepdims=True)
        weights = jnp.exp(scores - top)
        total = jnp.sum(weights, axis=0, keepdims=True)
        prob = weights * (1.0 / total)
        low = prob.astype(BF16)
        ctx_ref[rows, :] = dot_nn(vt_ref[rows, :], low).astype(BF16)
        grad_prob = dot_nn(v_ref[h], gt_ref[rows, :] * scale)
        inner = jnp.sum(prob * grad_prob, axis=0, keepdims=True)
        grad_score = (prob * (grad_prob - inner)).astype(BF16)
        gq_ref[rows, :] = dot_nn(kt_ref[rows, :], grad_score).astype(BF16)
        gv = dot_nn(low, g_ref[h])
        gk = dot_nn(grad_score, qnat_ref[h])
        if first:
            gv_ref[h] = gv
            gk_ref[h] = gk
        else:
            gv_ref[h] = gv_in[h] + gv
            gk_ref[h] = gk_in[h] + gk
        return carry

    lax.fori_loop(0, heads, one_head, 0)
    gradq = dot_nt(normed, gq_ref[...])
    grado = dot_nt(cot_ref[...], ctx_ref[...])
    gradq_ref[...] = gradq if first else q_in[...] + gradq
    grado_ref[...] = grado if first else o_in[...] + grado
    if last:
        for out_ref, acc_ref in ((gradk_ref, gk_ref), (gradv_ref, gv_ref)):
            merged = jnp.concatenate([acc_ref[h].astype(BF16) for h in range(heads)], axis=1)
            out_ref[...] = dot_nn(knt_ref[...], merged)


def chunk_side(index, count, tokens, qw, hot, gt, g, cot, key_state, carried, heads):
    knt, kt, k, vt, v = key_state
    width, chunk = tokens.shape
    length = knt.shape[1]
    att = qw.shape[0]
    hsize = att // heads
    first, last = index == 0, index == count - 1
    acc = jax.ShapeDtypeStruct((heads, length, hsize), F32)
    grad = jax.ShapeDtypeStruct((width, att), F32)
    outs = [jax.ShapeDtypeStruct((att, chunk), BF16), acc, acc, grad, grad]
    if last:
        outs += [grad, grad]
    args = [tokens, qw, hot, gt, g, cot, knt, kt, k, vt, v]
    alias = {}
    if not first:
        alias = {len(args) + n: n + 1 for n in range(4)}
        args += list(carried)
    return pl.pallas_call(
        functools.partial(chunk_body, heads, first, last),
        out_shape=tuple(outs),
        in_specs=[VMEM] * len(args),
        out_specs=(VMEM,) * len(outs),
        scratch_shapes=[
            pltpu.VMEM((att, chunk), BF16),
            pltpu.VMEM((heads, chunk, hsize), BF16),
            pltpu.VMEM((att, chunk), BF16),
        ],
        input_output_aliases=alias,
        compiler_params=pltpu.CompilerParams(vmem_limit_bytes=56 * 2**20),
        name="attend_chunk",
    )(*args)


def scatter_sum(total, axis):
    size = lax.axis_size(axis)
    me = lax.axis_index(axis)
    rows, cols = total.shape
    part = total.reshape(size, rows // size, cols)
    bit = 1
    while bit < size:
        mine = (me // bit) % 2
        halves = part.reshape(part.shape[0] // 2, 2, *part.shape[1:])
        send = lax.dynamic_index_in_dim(halves, 1 - mine, 1, keepdims=False)
        keep = lax.dynamic_index_in_dim(halves, mine, 1, keepdims=False)
        got = lax.ppermute(send, axis, [(d, d ^ bit) for d in range(size)])
        part = keep + got
        bit *= 2
    return part[0]


def per_device(
    caches, owner_slot, pairs, block_mask, cotangent, embed_weight, query_weight,
    key_weight, value_weight, out_weight,
):
    devices_img = lax.axis_size("img")
    length = caches.shape[1]
    width = embed_weight.shape[1]
    att = query_weight.shape[1]
    hsize = att // HEADS
    blocks = block_mask.shape[1]
    cot = cotangent[0]

    embedded = lax.dot_general(
        embed_weight, caches[0], (((0,), (1,)), ((), ())), preferred_element_type=F32
    ).astype(BF16)
    shares = lax.all_to_all(
        embedded.reshape(devices_img, width // devices_img, length), "img", 0, 0, tiled=True
    )
    query_pick, key_pick = pick(owner_slot, pairs, shares)
    key_tokens = lax.all_to_all(key_pick, "img", 0, 0, tiled=True).reshape(width, length)
    query_tokens = lax.all_to_all(query_pick, "img", 0, 0, tiled=True).reshape(width, length)

    bias = jnp.where(block_mask[0] > 0, 0.0, DEAD).astype(BF16)
    aug = jnp.pad(jnp.repeat(bias.T, BLOCK, axis=0), ((0, 0), (0, hsize - blocks)))
    hot = (
        lax.broadcasted_iota(jnp.int32, (hsize, length), 0)
        == lax.broadcasted_iota(jnp.int32, (hsize, length), 1) // BLOCK
    ).astype(BF16)
    grad_context = jnp.dot(cot, out_weight, preferred_element_type=F32).astype(BF16)
    gt = grad_context.T
    g = grad_context.reshape(length, HEADS, hsize).transpose(1, 0, 2)
    cot_t = cot.T

    key_state = key_side(key_tokens, key_weight.T, value_weight.T, aug, HEADS)
    count = length // CHUNK
    carried, contexts = None, []
    for n in range(count):
        cols = slice(n * CHUNK, (n + 1) * CHUNK)
        out = chunk_side(
            n, count, query_tokens[:, cols], query_weight.T, hot[:, cols], gt[:, cols],
            g[:, cols], cot_t[:, cols], key_state, carried, HEADS,
        )
        contexts.append(out[0])
        carried = out[1:5]
    grad_q, grad_o = carried[2], carried[3]
    grad_k, grad_v = out[5], out[6]
    context = jnp.concatenate(contexts, axis=1)
    total = jnp.concatenate([grad_q, grad_k, grad_v, grad_o], axis=1)
    summed = scatter_sum(total, "img")
    attended = (
        query_tokens.T.astype(F32)
        + lax.dot_general(context, out_weight, (((0,), (1,)), ((), ())), preferred_element_type=F32)
    ).astype(BF16)
    return (attended[None], summed * (1.0 / devices_img))


def solution(mesh):
    spread = P(("groups", "img"), None, None)
    placed = (spread, P("groups"), P("groups", None), spread, spread) + (P(),) * 5
    return jax.shard_map(
        per_device,
        mesh=mesh,
        in_specs=placed,
        out_specs=(spread, P(("groups", "img"), None)),
        check_vma=False,
    )
```

time: 351 us -> 284 us (0.81)
  matrix products: 99.2 us -> 9.46 us
  Pallas kernels: 0 us -> 71.2 us
  waiting for transfers between devices: 178 us -> 126 us
  starting transfers between devices: 16.9 us -> 31.6 us
  between operations: 14.4 us -> 0.89 us
  local copies, waits for them, and re-layouts: 29.2 us -> 33.3 us
    unnamed x2 -> x0, waiting for transfers between devices: 91.6 us -> none
    dot_general x58 -> x3, matrix products: 99.2 us -> 9.46 us  [the longest x1 3.85 us: per_device(): lax.dot_general(embed_weight, caches[0], (((0,), (1,)), ((), ())), prefer...]
    pallas_call x0 -> x5, Pallas kernels: none -> 71.2 us  [the longest x3 66.1 us: chunk_side(): pl.pallas_call(functools.partial(chunk_body, heads, first, last), out_sha...]
    ppermute x0 -> x4, waiting for transfers between devices: none -> 69.1 us  [scatter_sum(): got = lax.ppermute(send, axis, [(d, d ^ bit) for d in range(size)])]
    all_to_all x2 -> x3, waiting for transfers between devices: 86.3 us -> 56.7 us  [the longest x1 24.4 us: per_device(): lax.all_to_all(embedded.reshape(devices_img, width // devices_img, length...]
    unnamed x29 -> x44, local copies, waits for them, and re-layouts: 11.8 us -> 21.6 us
    ppermute x0 -> x4, starting transfers between devices: none -> 9.13 us  [scatter_sum(): got = lax.ppermute(send, axis, [(d, d ^ bit) for d in range(size)])]
    gather x3 -> x0, local copies, waits for them, and re-layouts: 7.14 us -> none  [the longest x2 6.45 us: per_device(): picked = table[slots]]
  transfers between devices with their start and end apart: 3 -> 7, of which waited for: 3 -> 7; matrix products, arithmetic and copies ran while one was open for 2% -> 8% of each run, Pallas kernels for 0% -> 0%
where the time goes in v1:
time: 284 us; the launch traced here: 283 us
  waiting for transfers between devices  126 us (44%)
  Pallas kernels  71.2 us (25%)
  local copies, waits for them, and re-layouts  33.3 us (12%)
  starting transfers between devices  31.6 us (11%)
  other arithmetic  11.3 us (4%)
  matrix products  9.46 us (3%)
    ppermute x4, waiting for transfers between devices, scatter_sum(): got = lax.ppermute(send, axis, [(d, d ^ bit) for d in range(size)])  69.1 us
    pallas_call x3, Pallas kernels, chunk_side(): pl.pallas_call(functools.partial(chunk_body, heads, first, last), out_sha...  66.1 us
    all_to_all x1, waiting for transfers between devices, per_device(): lax.all_to_all(embedded.reshape(devices_img, width // devices_img, length...  24.4 us
    all_to_all x1, waiting for transfers between devices, per_device(): lax.all_to_all(query_pick, 'img', 0, 0, tiled=True).reshape(width, length)  23.4 us
    unnamed x44, local copies, waits for them, and re-layouts  21.6 us
    ppermute x4, starting transfers between devices, scatter_sum(): got = lax.ppermute(send, axis, [(d, d ^ bit) for d in range(size)])  9.13 us
    all_to_all x1, waiting for transfers between devices, per_device(): lax.all_to_all(key_pick, 'img', 0, 0, tiled=True).reshape(width, length)  8.83 us
    all_to_all x1, starting transfers between devices, per_device(): lax.all_to_all(embedded.reshape(devices_img, width // devices_img, length...  7.52 us
  transfers between devices with their start and end apart: 7, of which 7 were waited for; matrix products, arithmetic and copies ran while one was open for 8% of the time, Pallas kernels for 0%

profile of v1, /device:TPU:0, one launch (start us, length us, event | category | flops | bytes accessed | tf_op | source)
XLA Modules:
  0.0 283.4 jit_solution(1389610333517522057)
XLA Ops:
  2.0 3.9 %fusion.3 = bf16[768,768]{1,0:T(8,128)(2,1)} fusion(bf16[1024,768]{1,0:T(8,128)(2,1)S(1)} %copy-done, bf16[1,768,1024]{2,1,0:T(8,128)(2,1)} %param.10), kind=kOutput, calls=%fused_computation.9 | convolution fusion | flops 1208549376 | bytes 4325376 | tf_op jit(solution)/shard_map/dot_general | solution.py:213
  5.9 7.5 %all-to-all-start = ((bf16[16,48,768]{2,1,0:T(8,128)(2,1)}), bf16[16,48,768]{2,1,0:T(8,128)(2,1)S(1)}, u32[]{:S(2)}, u32[]{:S(2)}) async-start(bf16[16,48,768]{2,1,0:T(8,128)(2,1)} %bitcast.1), calls=%async_computation | async-start | bytes 2359296 | tf_op jit(solution)/shard_map/all_to_all | solution.py:216
  14.1 24.4 %all-to-all-done.shares_ref = bf16[16,48,768]{2,1,0:T(8,128)(2,1)S(1)} async-done(((bf16[16,48,768]{2,1,0:T(8,128)(2,1)}), bf16[16,48,768]{2,1,0:T(8,128)(2,1)S(1)}, u32[]{:S(2)}, u32[]{:S(2)}) %all-to-all-start) | async-done | bytes 1179680 | tf_op jit(solution)/shard_map/all_to_all | solution.py:216
  39.6 3.0 %pick_shares.1 = (bf16[16,48,768]{2,1,0:T(8,128)(2,1)}, bf16[16,48,768]{2,1,0:T(8,128)(2,1)}) custom-call(s32[16]{0:T(128)} %owner_ref.1, s32[32]{0:T(128)} %reshape.41.pairs_ref, bf16[16,48,768]{2,1,0:T(8,128)(2,1)} %copy-done.14), custom_call_target="tpu_custom_call" | custom-call | tf_op jit(solution)/shard_map/pick_shares/pallas_call | solution.py:50
  42.6 7.5 %all-to-all-start.1 = ((bf16[16,48,768]{2,1,0:T(8,128)(2,1)}), bf16[16,48,768]{2,1,0:T(8,128)(2,1)S(1)}, u32[]{:S(2)}, u32[]{:S(2)}) async-start(bf16[16,48,768]{2,1,0:T(8,128)(2,1)} %get-tuple-element.24), calls=%async_computation.1 | async-start | bytes 2359296 | tf_op jit(solution)/shard_map/all_to_all | solution.py:221
  51.8 23.4 %all-to-all-done.1 = bf16[16,48,768]{2,1,0:T(8,128)(2,1)S(1)} async-done(((bf16[16,48,768]{2,1,0:T(8,128)(2,1)}), bf16[16,48,768]{2,1,0:T(8,128)(2,1)S(1)}, u32[]{:S(2)}, u32[]{:S(2)}) %all-to-all-start.1) | async-done | bytes 1179680 | tf_op jit(solution)/shard_map/all_to_all | solution.py:221
  76.2 7.5 %all-to-all-start.2 = ((bf16[16,48,768]{2,1,0:T(8,128)(2,1)}), bf16[16,48,768]{2,1,0:T(8,128)(2,1)S(1)}, u32[]{:S(2)}, u32[]{:S(2)}) async-start(bf16[16,48,768]{2,1,0:T(8,128)(2,1)} %get-tuple-element.25), calls=%async_computation.2 | async-start | bytes 2359296 | tf_op jit(solution)/shard_map/all_to_all | solution.py:220
  83.8 2.4 copy.39
  86.2 2.3 convolution_convert_fusion
  90.1 2.3 copy.38
  100.0 8.8 %all-to-all-done.2 = bf16[16,48,768]{2,1,0:T(8,128)(2,1)S(1)} async-done(((bf16[16,48,768]{2,1,0:T(8,128)(2,1)}), bf16[16,48,768]{2,1,0:T(8,128)(2,1)S(1)}, u32[]{:S(2)}, u32[]{:S(2)}) %all-to-all-start.2) | async-done | bytes 1179680 | tf_op jit(solution)/shard_map/all_to_all | solution.py:220
  116.1 19.5 %attend_chunk.3 = (bf16[512,256]{1,0:T(8,128)(2,1)}, f32[8,768,64]{2,1,0:T(8,128)}, f32[8,768,64]{2,1,0:T(8,128)}, f32[768,512]{1,0:T(8,128)}, f32[768,512]{1,0:T(8,128)}) custom-call(bf16[768,256]{1,0:T(8,128)(2,1)} %get-tuple-element.58.token_ref, bf16[512,768]{1,0:T(8,128)(2,1)} %bitcast.58, bf16[64,256]{1,0:T(8,128)(2,1)} %get-tuple-element.64.hot_ref, ...), custom_call_target="tpu_custom_call" | custom-call | tf_op jit(solution)/shard_map/attend_chunk/pallas_call | solution.py:168
  135.6 22.3 %attend_chunk.4 = (bf16[512,256]{1,0:T(8,128)(2,1)}, f32[8,768,64]{2,1,0:T(8,128)}, f32[8,768,64]{2,1,0:T(8,128)}, f32[768,512]{1,0:T(8,128)}, f32[768,512]{1,0:T(8,128)}) custom-call(bf16[768,256]{1,0:T(8,128)(2,1)} %get-tuple-element.60.token_ref, ...), custom_call_target="tpu_custom_call", output_to_operand_aliasing={{1}: (11, {}), {2}: (12, {}), {3}: (13, {}), {4}: (14, {})} | custom-call | tf_op jit(solution)/shard_map/attend_chunk/pallas_call | solution.py:168
  157.9 24.3 %attend_chunk.5 = (bf16[512,256]{1,0:T(8,128)(2,1)}, f32[8,768,64]{2,1,0:T(8,128)}, f32[8,768,64]{2,1,0:T(8,128)}, f32[768,512]{1,0:T(8,128)}, f32[768,512]{1,0:...) custom-call(bf16[768,256]{1,0:T(8,128)(2,1)} %get-tuple-element.59.t, ...), custom_call_target="tpu_custom_call", output_to_operand_aliasing={{1}: (11, {}), {2}: (12, {}), {3}: (13, {}), {4}: (14, {})} | custom-call | tf_op jit(solution)/shard_map/attend_chunk/pallas_call | solution.py:168
  182.2 3.1 %pad_maximum_fusion = f32[768,2048]{1,0:T(8,128)S(1)} fusion(f32[768,512]{1,0:T(8,128)} %get-tuple-element.45, f32[768,512]{1,0:T(8,128)} %get-tuple-element.44, f32[768,512]{1,0:T(8,128)} %get-tuple-element.43, f32[768,512]{1,0:T(8,128)} %get-tuple-element.42), kind=kLoop, calls=%fused_computation | loop fusion | flops 4718592 | bytes 12582912 | tf_op jit(solution)/shard_map/concatenate | solution.py:248
  189.7 5.6 %collective-permute-done = f32[8,48,2048]{2,1,0:T(8,128)} collective-permute-done((f32[8,48,2048]{2,1,0:T(8,128)}, f32[8,48,2048]{2,1,0:T(8,128)}, u32[]{:S(2)}, u32[]{:S(2)}) %collective-permute-start) | collective-permute-done | bytes 3145760 | tf_op jit(solution)/shard_map/ppermute | solution.py:195
  195.3 3.5 %bitcast_add_fusion = f32[8,48,2048]{2,1,0:T(8,128)S(1)} fusion(f32[8,48,2048]{2,1,0:T(8,128)} %collective-permute-done, f32[8,2,48,2048]{3,2,1,0:T(8,128)} %bitcast.57, s32[]{:T(128)S(6)} %select_n.75), kind=kLoop, calls=%fused_computation.1 | loop fusion | flops 786432 | bytes 9437188 | tf_op jit(solution)/shard_map/add | solution.py:196
  202.6 34.9 %collective-permute-done.1 = f32[4,48,2048]{2,1,0:T(8,128)S(1)} collective-permute-done((f32[4,48,2048]{2,1,0:T(8,128)S(1)}, f32[4,48,2048]{2,1,0:T(8,128)S(1)}, u32[]{:S(2)}, u32[]{:S(2)}) %collective-permute-start.1) | collective-permute-done | bytes 1572896 | tf_op jit(solution)/shard_map/ppermute | solution.py:195
  239.2 3.4 %collective-permute-start.2 = (f32[2,48,2048]{2,1,0:T(8,128)S(1)}, f32[2,48,2048]{2,1,0:T(8,128)}, u32[]{:S(2)}, u32[]{:S(2)}) collective-permute-start(f32[2,48,2048]{2,1,0:T(8,128)S(1)} %dynamic-slice_bitcast_fusion.2), channel_id=1, source_target_pairs={{0,4},{1,5},{2,6},{3,7},{4,0},{5,1},{6,2},{7,3},{8,12},{9,13},{10,... | collective-permute-start | bytes 2359304 | tf_op jit(solution)/shard_map/ppermute | solution.py:195
  242.6 17.4 %collective-permute-done.2 = f32[2,48,2048]{2,1,0:T(8,128)} collective-permute-done((f32[2,48,2048]{2,1,0:T(8,128)S(1)}, f32[2,48,2048]{2,1,0:T(8,128)}, u32[]{:S(2)}, u32[]{:S(2)}) %collective-permute-start.2) | collective-permute-done | bytes 786464 | tf_op jit(solution)/shard_map/ppermute | solution.py:195
  262.0 2.8 collective-permute-start.3
  264.8 3.3 %fusion.6 = bf16[1,768,768]{1,2,0:T(8,128)(2,1)} fusion(bf16[768,512]{1,0:T(8,128)(2,1)} %param.19, bf16[768,768]{1,0:T(8,128)(2,1)S(1)} %bitcast.67, bf16[512,256]{1,0:T(8,128)(2,1)} %get-tuple-element.41, bf16[512,256]{1,0:T(8,128)(2,1)} %get-tuple-element.36, bf16[512,256]{1,0:T(8,128)(2,1)} %get-tuple-element.31), kind=kOutput, calls=%fused_computation.11 | convolution fusion | flops 608108544 | bytes 3932160 | tf_op jit(solution)/shard_map/dot_general | solution.py:252
  268.1 2.4 copy.45
  270.5 11.1 %collective-permute-done.3 = f32[1,48,2048]{2,1,0:T(8,128)} collective-permute-done((f32[1,48,2048]{2,1,0:T(8,128)}, f32[1,48,2048]{2,1,0:T(8,128)}, u32[]{:S(2)}, u32[]{:S(2)}) %collective-permute-start.3) | collective-permute-done | bytes 393248 | tf_op jit(solution)/shard_map/ppermute | solution.py:195
  (65 shorter events, 35.8 us)
Async XLA Ops:
  0.6 1.4 copy-start
  5.9 7.5 %copy-start.18 = (s32[16,2]{0,1:T(2,128)S(1)}, s32[16,2]{0,1:T(2,128)}, u32[]{:S(2)}) copy-start(s32[16,2]{0,1:T(2,128)} %param.12) | copy-start | bytes 388
  5.9 32.7 %all-to-all-start = ((bf16[16,48,768]{2,1,0:T(8,128)(2,1)}), bf16[16,48,768]{2,1,0:T(8,128)(2,1)S(1)}, u32[]{:S(2)}, u32[]{:S(2)}) async-start(bf16[16,48,768]{2,1,0:T(8,128)(2,1)} %bitcast.1), calls=%async_computation | async-start | bytes 2359296 | tf_op jit(solution)/shard_map/all_to_all | solution.py:216
  14.1 35.9 %copy-start.16 = (bf16[768,512]{1,0:T(8,128)(2,1)S(1)}, bf16[768,512]{1,0:T(8,128)(2,1)}, u32[]{:S(2)}) copy-start(bf16[768,512]{1,0:T(8,128)(2,1)} %param.17) | copy-start | bytes 2359300
  38.6 1.0 copy-start.14
  42.6 32.6 %all-to-all-start.1 = ((bf16[16,48,768]{2,1,0:T(8,128)(2,1)}), bf16[16,48,768]{2,1,0:T(8,128)(2,1)S(1)}, u32[]{:S(2)}, u32[]{:S(2)}) async-start(bf16[16,48,768]{2,1,0:T(8,128)(2,1)} %get-tuple-element.24), calls=%async_computation.1 | async-start | bytes 2359296 | tf_op jit(solution)/shard_map/all_to_all | solution.py:221
  51.8 31.9 %copy-start.17 = (s32[1,12,12]{2,0,1:T(1,128)S(1)}, s32[1,12,12]{2,0,1:T(1,128)}, u32[]{:S(2)}) copy-start(s32[1,12,12]{2,0,1:T(1,128)} %param.13) | copy-start | bytes 1732
  75.2 1.0 copy-start.10
  76.2 32.6 %all-to-all-start.2 = ((bf16[16,48,768]{2,1,0:T(8,128)(2,1)}), bf16[16,48,768]{2,1,0:T(8,128)(2,1)S(1)}, u32[]{:S(2)}, u32[]{:S(2)}) async-start(bf16[16,48,768]{2,1,0:T(8,128)(2,1)} %get-tuple-element.25), calls=%async_computation.2 | async-start | bytes 2359296 | tf_op jit(solution)/shard_map/all_to_all | solution.py:220
  88.5 3.9 %copy-start.15 = (bf16[768,512]{0,1:T(8,128)(2,1)}, bf16[768,512]{0,1:T(8,128)(2,1)S(1)}, u32[]{:S(2)}) copy-start(bf16[768,512]{0,1:T(8,128)(2,1)S(1)} %convolution_convert_fusion) | copy-start | bytes 2359300
  92.5 2.8 copy-start.13
  95.3 1.8 copy-start.9
  97.1 1.8 copy-start.11
  110.9 1.2 copy-start.2
  112.1 1.2 copy-start.3
  113.3 1.0 copy-start.4
  185.3 3.6 %copy-start.7 = (f32[768,2048]{1,0:T(8,128)}, f32[768,2048]{1,0:T(8,128)S(1)}, u32[]{:S(2)}) copy-start(f32[768,2048]{1,0:T(8,128)S(1)} %pad_maximum_fusion) | copy-start | bytes 18874372
  188.9 6.4 %collective-permute-start = (f32[8,48,2048]{2,1,0:T(8,128)}, f32[8,48,2048]{2,1,0:T(8,128)}, u32[]{:S(2)}, u32[]{:S(2)}) collective-permute-start(f32[8,48,2048]{2,1,0:T(8,128)} %dynamic-slice_bitcast_fusion), channel_id=1, source_target_pairs={{0,1},{1,0},{2,3},{3,2},{4,5},{5,4},{6,7},{7,6},{8,9},{9,8},{10,11... | collective-permute-start | bytes 9437192 | tf_op jit(solution)/shard_map/ppermute | solution.py:195
  198.9 1.6 copy-start.8
  200.5 37.0 %collective-permute-start.1 = (f32[4,48,2048]{2,1,0:T(8,128)S(1)}, f32[4,48,2048]{2,1,0:T(8,128)S(1)}, u32[]{:S(2)}, u32[]{:S(2)}) collective-permute-start(f32[4,48,2048]{2,1,0:T(8,128)S(1)} %dynamic-slice_bitcast_fusion.1), channel_id=1, source_target_pairs={{0,2},{1,3},{2,0},{3,1},{4,6},{5,7},{6,4},{7,5},{8,10},{9,11},{10,... | collective-permute-start | bytes 4718600 | tf_op jit(solution)/shard_map/ppermute | solution.py:195
  239.2 20.8 %collective-permute-start.2 = (f32[2,48,2048]{2,1,0:T(8,128)S(1)}, f32[2,48,2048]{2,1,0:T(8,128)}, u32[]{:S(2)}, u32[]{:S(2)}) collective-permute-start(f32[2,48,2048]{2,1,0:T(8,128)S(1)} %dynamic-slice_bitcast_fusion.2), channel_id=1, source_target_pairs={{0,4},{1,5},{2,6},{3,7},{4,0},{5,1},{6,2},{7,3},{8,12},{9,13},{10,... | collective-permute-start | bytes 2359304 | tf_op jit(solution)/shard_map/ppermute | solution.py:195
  242.6 22.2 %copy-start.12 = (bf16[16,48,768]{2,1,0:T(8,128)(2,1)S(1)}, bf16[16,48,768]{2,1,0:T(8,128)(2,1)}, u32[]{:S(2)}) copy-start(bf16[16,48,768]{2,1,0:T(8,128)(2,1)} %copy-done.10) | copy-start | bytes 3538948
  262.0 19.6 %collective-permute-start.3 = (f32[1,48,2048]{2,1,0:T(8,128)}, f32[1,48,2048]{2,1,0:T(8,128)}, u32[]{:S(2)}, u32[]{:S(2)}) collective-permute-start(f32[1,48,2048]{2,1,0:T(8,128)} %constant_dynamic-slice_fusion), channel_id=1, source_target_pairs={{0,8},{1,9},{2,10},{3,11},{4,12},{5,13},{6,14},{7,15},{8,0},{9,1},... | collective-permute-start | bytes 1179656 | tf_op jit(solution)/shard_map/ppermute | solution.py:195
  264.8 18.6 %copy-start.1 = (bf16[1024,768]{1,0:T(8,128)(2,1)S(1)}, bf16[1024,768]{1,0:T(8,128)(2,1)}, u32[]{:S(2)}) copy-start(bf16[1024,768]{1,0:T(8,128)(2,1)} %param.15) | copy-start | bytes 4718596
  (2 other events, 1.8 us)

commit v2 on v1

v2 whole, which is shorter than its diff:
```python
import functools
import math

import jax
import jax.numpy as jnp
from jax import lax
from jax.experimental import pallas as pl
from jax.experimental.pallas import tpu as pltpu
from jax.sharding import PartitionSpec as P

HEADS = 8
BLOCK = 64
CHUNK = 256
DEAD = -1e30
F32 = jnp.float32
F16 = jnp.float16
BF16 = jnp.bfloat16
VMEM = pl.BlockSpec(memory_space=pltpu.VMEM)
SMEM = pl.BlockSpec(memory_space=pltpu.SMEM)


def dot_nn(a, b):
    return lax.dot_general(a, b, (((1,), (0,)), ((), ())), preferred_element_type=F32)


def dot_nt(a, b):
    return lax.dot_general(a, b, (((1,), (1,)), ((), ())), preferred_element_type=F32)


def norm_columns(tokens):
    values_f = tokens.astype(F32)
    width = values_f.shape[0]
    centred = values_f - jnp.sum(values_f, axis=0, keepdims=True) * (1.0 / width)
    spread_sq = jnp.sum(centred * centred, axis=0, keepdims=True) * (1.0 / width)
    return (centred * lax.rsqrt(spread_sq + 1e-06)).astype(BF16)


def pick_body(owner_ref, pairs_ref, shares_ref, out_ref):
    count = shares_ref.shape[0]

    def step(p, carry):
        for side in range(2):
            out_ref[p, side] = shares_ref[owner_ref[pairs_ref[2 * p + side]]]
        return carry

    lax.fori_loop(0, count, step, 0, unroll=4)


def pick(owner_slot, pairs, shares):
    count = shares.shape[0]
    return pl.pallas_call(
        pick_body,
        out_shape=jax.ShapeDtypeStruct((count, 2) + shares.shape[1:], shares.dtype),
        in_specs=[SMEM, SMEM, VMEM],
        out_specs=VMEM,
        compiler_params=pltpu.CompilerParams(vmem_limit_bytes=16 * 2**20),
        name="pick_shares",
    )(owner_slot, pairs.reshape(-1), shares)


def pair_body(
    heads, core_ref, token_ref, qw_ref, kw_ref, vw_ref, aug_ref, hot_ref, gt_ref, g_ref, cot_ref,
    ctx_ref, keep_qk_ref, send_qk_ref, keep_vo_ref, send_vo_ref,
    qn_ref, kn_ref, qt_ref, kt_ref, vt_ref, q_ref, k_ref, v_ref, gq_ref, gk_ref, gv_ref, val_ref,
):
    count, _, share, length = token_ref.shape
    att = qw_ref.shape[0]
    hsize = att // heads
    scale = jnp.asarray(1.0 / math.sqrt(hsize), BF16)
    for c in range(length // CHUNK):
        cols = pl.ds(c * CHUNK, CHUNK)
        query_n = norm_columns(token_ref[:, 0, :, cols].reshape(count * share, CHUNK))
        key_n = norm_columns(token_ref[:, 1, :, cols].reshape(count * share, CHUNK))
        qn_ref[:, cols] = query_n
        kn_ref[:, cols] = key_n
        qt_ref[:, cols] = dot_nn(qw_ref[...], query_n).astype(BF16)
        kt_ref[:, cols] = dot_nn(kw_ref[...], key_n).astype(BF16)
        vt_ref[:, cols] = dot_nn(vw_ref[...], key_n).astype(BF16)
    for h in range(heads):
        rows = pl.ds(h * hsize, hsize)
        q_ref[h] = qt_ref[rows, :].T
        k_ref[h] = jnp.concatenate([kt_ref[rows, :].T, aug_ref[...]], axis=1)
        v_ref[h] = vt_ref[rows, :].T

    def one_head(h):
        rows = pl.ds(pl.multiple_of(h * hsize, hsize), hsize)
        query_aug = jnp.concatenate([qt_ref[rows, :] * scale, hot_ref[...]], axis=0)
        scores = dot_nn(k_ref[h], query_aug)
        top = jnp.max(scores, axis=0, keepdims=True)
        weights = jnp.exp(scores - top)
        total = jnp.sum(weights, axis=0, keepdims=True)
        prob = weights * (1.0 / total)
        low = prob.astype(BF16)
        ctx_ref[rows, :] = dot_nn(vt_ref[rows, :], low).astype(BF16)
        grad_prob = dot_nn(v_ref[h], gt_ref[rows, :] * scale)
        inner = jnp.sum(prob * grad_prob, axis=0, keepdims=True)
        grad_score = (prob * (grad_prob - inner)).astype(BF16)
        gq_ref[rows, :] = dot_nn(kt_ref[rows, :], grad_score).astype(BF16)
        return (
            dot_nn(grad_score, q_ref[h]).astype(BF16),
            dot_nn(low, g_ref[h]).astype(BF16),
        )

    def two_heads(i, carry):
        gk0, gv0 = one_head(2 * i)
        gk1, gv1 = one_head(2 * i + 1)
        cols = pl.ds(pl.multiple_of(i * 2 * hsize, 2 * hsize), 2 * hsize)
        gk_ref[:, cols] = jnp.concatenate([gk0, gk1], axis=1)
        gv_ref[:, cols] = jnp.concatenate([gv0, gv1], axis=1)
        return carry

    lax.fori_loop(0, heads // 2, two_heads, 0)

    blocks, rows_each, _ = keep_qk_ref.shape
    for n, (left, right, dot) in enumerate(
        (
            (qn_ref, gq_ref, dot_nt),
            (kn_ref, gk_ref, dot_nn),
            (kn_ref, gv_ref, dot_nn),
            (cot_ref, ctx_ref, dot_nt),
        )
    ):
        keep_ref, send_ref = ((keep_qk_ref, send_qk_ref), (keep_vo_ref, send_vo_ref))[n // 2]
        cols = pl.ds((n % 2) * att, att)
        val_ref[...] = dot(left[...], right[...])
        for core, targets in ((0, (keep_ref, send_ref)), (1, (send_ref, keep_ref))):

            @pl.when(core_ref[0] == core)
            def _():
                for b in range(2 * blocks):
                    targets[b % 2][b // 2, :, cols] = val_ref[pl.ds(b * rows_each, rows_each), :]


def pair_side(core, arrived, qw, kw, vw, aug, hot, gt, g, cot, heads, rows_each):
    length = arrived.shape[-1]
    width = cot.shape[0]
    att = qw.shape[0]
    hsize = att // heads
    part = jax.ShapeDtypeStruct((width // rows_each // 2, rows_each, 2 * att), F32)
    flat = pltpu.VMEM((att, length), BF16)
    each = pltpu.VMEM((heads, length, hsize), BF16)
    side = pltpu.VMEM((length, att), BF16)
    return pl.pallas_call(
        functools.partial(pair_body, heads),
        out_shape=(jax.ShapeDtypeStruct((att, length), BF16), part, part, part, part),
        in_specs=[SMEM] + [VMEM] * 9,
        out_specs=(VMEM,) * 5,
        scratch_shapes=[
            pltpu.VMEM((width, length), BF16),
            pltpu.VMEM((width, length), BF16),
            flat,
            flat,
            flat,
            each,
            pltpu.VMEM((heads, length, 2 * hsize), BF16),
            each,
            flat,
            side,
            side,
            pltpu.VMEM((width, att), F32),
        ],
        compiler_params=pltpu.CompilerParams(vmem_limit_bytes=58 * 2**20),
        name="pair_pass",
    )(core, arrived, qw, kw, vw, aug, hot, gt, g, cot)


def exchange(array, axis, bit):
    size = lax.axis_size(axis)
    return lax.ppermute(array, axis, [(d, d ^ (1 << bit)) for d in range(size)])


def scatter_sum(keep, send, axis, order):
    bits = lax.axis_size(axis).bit_length() - 1
    me = lax.axis_index(axis)
    part = keep + exchange(send, axis, 0)
    rows, cols = part.shape[1:]
    part = part.reshape((2,) * (bits - 1) + (rows, cols))
    left = list(reversed(range(1, bits)))
    for bit in order:
        at = left.index(bit)
        left.pop(at)
        mine = (me >> bit) & 1
        send = lax.dynamic_index_in_dim(part, 1 - mine, at, keepdims=False)
        keep = lax.dynamic_index_in_dim(part, mine, at, keepdims=False)
        top = jnp.max(jnp.abs(send), axis=tuple(range(send.ndim - 1)), keepdims=True)
        power = jnp.ceil(jnp.log2(jnp.maximum(top, 1e-30)))
        scaled = (send * jnp.exp2(8.0 - power)).astype(F16)
        power = exchange(power, axis, bit)
        part = keep + exchange(scaled, axis, bit).astype(F32) * jnp.exp2(power - 8.0)
    return part


def per_device(
    caches, owner_slot, pairs, block_mask, cotangent, embed_weight, query_weight,
    key_weight, value_weight, out_weight,
):
    devices_img = lax.axis_size("img")
    bits = devices_img.bit_length() - 1
    length = caches.shape[1]
    width = embed_weight.shape[1]
    att = query_weight.shape[1]
    hsize = att // HEADS
    blocks = block_mask.shape[1]
    cot = cotangent[0]
    share = width // devices_img

    embedded = lax.dot_general(
        embed_weight, caches[0], (((0,), (1,)), ((), ())), preferred_element_type=F32
    ).astype(BF16)
    shares = lax.all_to_all(
        embedded.reshape(devices_img, share, length), "img", 0, 0, tiled=True
    )
    picked = pick(owner_slot, pairs, shares)
    arrived = lax.all_to_all(picked, "img", 0, 0, tiled=True)
    query_tokens = arrived[:, 0].reshape(width, length)
    if share % 16:
        arrived = arrived.transpose(1, 0, 2, 3).reshape(1, 2, width, length)

    bias = jnp.where(block_mask[0] > 0, 0.0, DEAD).astype(BF16)
    aug = jnp.pad(jnp.repeat(bias.T, BLOCK, axis=0), ((0, 0), (0, hsize - blocks)))
    hot = (
        lax.broadcasted_iota(jnp.int32, (hsize, length), 0)
        == lax.broadcasted_iota(jnp.int32, (hsize, length), 1) // BLOCK
    ).astype(BF16)
    grad_context = jnp.dot(cot, out_weight, preferred_element_type=F32).astype(BF16)
    g = grad_context.reshape(length, HEADS, hsize).transpose(1, 0, 2)
    core = (lax.axis_index("img") % 2).astype(jnp.int32).reshape(1)

    context, keep_qk, send_qk, keep_vo, send_vo = pair_side(
        core, arrived, query_weight.T, key_weight.T, value_weight.T, aug, hot,
        grad_context.T, g, cot.T, HEADS, share,
    )
    upward = list(range(1, bits))
    qk = scatter_sum(keep_qk, send_qk, "img", upward)
    vo = scatter_sum(keep_vo, send_vo, "img", upward[1:2] + upward[:1] + upward[2:])
    attended = (
        query_tokens.T.astype(F32)
        + lax.dot_general(context, out_weight, (((0,), (1,)), ((), ())), preferred_element_type=F32)
    ).astype(BF16)
    return (attended[None], jnp.concatenate([qk, vo], axis=1) * (1.0 / devices_img))


def solution(mesh):
    spread = P(("groups", "img"), None, None)
    placed = (spread, P("groups"), P("groups", None), spread, spread) + (P(),) * 5
    return jax.shard_map(
        per_device,
        mesh=mesh,
        in_specs=placed,
        out_specs=(spread, P(("groups", "img"), None)),
        check_vma=False,
    )
```

time: 284 us -> 181 us (0.64)
  waiting for transfers between devices: 126 us -> 77 us
  Pallas kernels: 71.2 us -> 33.3 us
  local copies, waits for them, and re-layouts: 33.3 us -> 16.2 us
  starting transfers between devices: 31.6 us -> 36.8 us
  other arithmetic: 11.3 us -> 6.29 us
    ppermute x4 -> x14, waiting for transfers between devices: 69.1 us -> 17.8 us  [exchange(): return lax.ppermute(array, axis, [(d, d ^ 1 << bit) for d in range(size)])]
    pallas_call x5 -> x2, Pallas kernels: 71.2 us -> 33.3 us  [the longest x1 32.6 us: pair_side(): pl.pallas_call(functools.partial(pair_body, heads), out_shape=(jax.ShapeD...]
    ppermute x4 -> x14, starting transfers between devices: 9.13 us -> 21.6 us  [exchange(): return lax.ppermute(array, axis, [(d, d ^ 1 << bit) for d in range(size)])]
    unnamed x44 -> x27, local copies, waits for them, and re-layouts: 21.6 us -> 9.32 us
    all_to_all x3 -> x2, starting transfers between devices: 22.5 us -> 15.2 us  [the longest x1 7.66 us: per_device(): arrived = lax.all_to_all(picked, 'img', 0, 0, tiled=True)]
    slice x5 -> x1, local copies, waits for them, and re-layouts: 6.05 us -> 1.35 us  [per_device(): query_tokens = arrived[:, 0].reshape(width, length)]
    add x3 -> x8, other arithmetic: 6.33 us -> 2.38 us  [the longest x2 1.96 us: scatter_sum(): part = keep + exchange(send, axis, 0)]
    squeeze x4 -> x0, local copies, waits for them, and re-layouts: 3.27 us -> none  [scatter_sum(): send = lax.dynamic_index_in_dim(halves, 1 - mine, 1, keepdims=False)]
  transfers between devices with their start and end apart: 7 -> 16, of which waited for: 7 -> 8; matrix products, arithmetic and copies ran while one was open for 8% -> 14% of each run, Pallas kernels for 0% -> 0%
where the time goes in v2:
time: 181 us; the launch traced here: 180 us
  waiting for transfers between devices  77 us (43%)
  starting transfers between devices  36.8 us (20%)
  Pallas kernels  33.3 us (18%)
  local copies, waits for them, and re-layouts  16.2 us (9%)
  matrix products  9.91 us (5%)
  other arithmetic  6.29 us (3%)
    all_to_all x1, waiting for transfers between devices, per_device(): arrived = lax.all_to_all(picked, 'img', 0, 0, tiled=True)  34.3 us
    pallas_call x1, Pallas kernels, pair_side(): pl.pallas_call(functools.partial(pair_body, heads), out_shape=(jax.ShapeD...  32.6 us
    all_to_all x1, waiting for transfers between devices, per_device(): lax.all_to_all(embedded.reshape(devices_img, share, length), 'img', 0, 0,...  24.9 us
    ppermute x14, starting transfers between devices, exchange(): return lax.ppermute(array, axis, [(d, d ^ 1 << bit) for d in range(size)])  21.6 us
    ppermute x14, waiting for transfers between devices, exchange(): return lax.ppermute(array, axis, [(d, d ^ 1 << bit) for d in range(size)])  17.8 us
    unnamed x27, local copies, waits for them, and re-layouts  9.32 us
    all_to_all x1, starting transfers between devices, per_device(): arrived = lax.all_to_all(picked, 'img', 0, 0, tiled=True)  7.66 us
    all_to_all x1, starting transfers between devices, per_device(): lax.all_to_all(embedded.reshape(devices_img, share, length), 'img', 0, 0,...  7.52 us
  transfers between devices with their start and end apart: 16, of which 8 were waited for; matrix products, arithmetic and copies ran while one was open for 14% of the time, Pallas kernels for 0%

profile of v2, /device:TPU:0, one launch (start us, length us, event | category | flops | bytes accessed | tf_op | source)
XLA Modules:
  0.0 180.5 jit_solution(12086469192891858397)
XLA Ops:
  2.0 3.9 %fusion.3 = bf16[768,768]{1,0:T(8,128)(2,1)} fusion(bf16[1024,768]{1,0:T(8,128)(2,1)S(1)} %copy-done, bf16[1,768,1024]{2,1,0:T(8,128)(2,1)} %param.10), kind=kOutput, calls=%fused_computation.4 | convolution fusion | flops 1208549376 | bytes 4325376 | tf_op jit(solution)/shard_map/dot_general | solution.py:207
  5.9 7.5 %all-to-all-start = ((bf16[16,48,768]{2,1,0:T(8,128)(2,1)}), bf16[16,48,768]{2,1,0:T(8,128)(2,1)S(1)}, u32[]{:S(2)}, u32[]{:S(2)}) async-start(bf16[16,48,768]{2,1,0:T(8,128)(2,1)} %bitcast.120), calls=%async_computation | async-start | bytes 2359296 | tf_op jit(solution)/shard_map/all_to_all | solution.py:210
  13.6 24.9 %all-to-all-done.shares_ref = bf16[16,48,768]{2,1,0:T(8,128)(2,1)S(1)} async-done(((bf16[16,48,768]{2,1,0:T(8,128)(2,1)}), bf16[16,48,768]{2,1,0:T(8,128)(2,1)S(1)}, u32[]{:S(2)}, u32[]{:S(2)}) %all-to-all-start) | async-done | bytes 1179680 | tf_op jit(solution)/shard_map/all_to_all | solution.py:210
  40.7 7.7 %all-to-all-start.1 = ((bf16[16,2,48,768]{3,2,1,0:T(8,128)(2,1)}), bf16[16,2,48,768]{3,2,1,0:T(8,128)(2,1)}, u32[]{:S(2)}, u32[]{:S(2)}) async-start(bf16[16,2,48,768]{3,2,1,0:T(8,128)(2,1)} %copy-done.1), calls=%async_computation.1 | async-start | bytes 4718592 | tf_op jit(solution)/shard_map/all_to_all | solution.py:214
  49.9 2.0 %convolution_convert_fusion = bf16[768,512]{0,1:T(8,128)(2,1)S(1)} fusion(bf16[768,512]{1,0:T(8,128)(2,1)} %param.19, bf16[1,768,768]{2,1,0:T(8,128)(2,1)S(1)} %copy-done.6), kind=kOutput, calls=%fused_computation.6 | convolution fusion | flops 604372992 | bytes 2752512 | tf_op jit(solution)/shard_map/dot_general | solution.py:225
  54.7 2.4 %copy.22 = bf16[768,512]{0,1:T(8,128)(2,1)} copy(bf16[768,512]{1,0:T(8,128)(2,1)} %param.17) | data formatting | bytes 1572864 | tf_op args[7]
  59.9 34.3 %all-to-all-done.1.token_ref = bf16[16,2,48,768]{3,2,1,0:T(8,128)(2,1)} async-done(((bf16[16,2,48,768]{3,2,1,0:T(8,128)(2,1)}), bf16[16,2,48,768]{3,2,1,0:T(8,128)(2,1)}, u32[]{:S(2)}, u32[]{:S(2)}) %all-to-all-start.1) | async-done | bytes 2359328 | tf_op jit(solution)/shard_map/all_to_all | solution.py:214
  94.1 32.6 %pair_pass.1 = (bf16[512,768]{1,0:T(8,128)(2,1)}, f32[8,48,1024]{2,1,0:T(8,128)}, f32[8,48,1024]{2,1,0:T(8,128)}, f32[8,48,1024]{2,1,0:T(8,128)}, f32[8,48,1024]{2,1,0:T(8,128)}) custom-call(s32[1]{0:T(128)} %bitcast.4.core_ref, bf16[16,2,48,768]{3,2,1,0:T(8,128)(2,1)} %all-to-all-done.1.token_ref, bf16[512,768]{1,0:T(8,128)(2,1)} %bitcast.115, ...), custom_call_target="tpu_custom_call" | custom-call | tf_op jit(solution)/shard_map/pair_pass/pallas_call | solution.py:143
  128.8 1.7 bitcast_convert_fusion
  130.6 3.1 %copy.20 = f32[768,768]{0,1:T(8,128)} copy(f32[768,768]{1,0:T(8,128)} %bitcast_convert_fusion) | data formatting | bytes 4718592 | tf_op jit(solution)/shard_map/convert_element_type | solution.py:237
  133.7 4.1 %fusion.6 = bf16[1,768,768]{2,1,0:T(8,128)(2,1)} fusion(bf16[512,768]{1,0:T(8,128)(2,1)} %get-tuple-element.7, bf16[768,512]{1,0:T(8,128)(2,1)} %param.19, f32[768,768]{0,1:T(8,128)} %copy.20), kind=kOutput, calls=%fused_computation.5 | convolution fusion | flops 605159424 | bytes 5111808 | tf_op jit(solution)/shard_map/dot_general | solution.py:238
  137.8 1.7 add.74
  139.6 3.8 %collective-permute-start.1 = (f16[2,2,48,1024]{3,2,1,0:T(8,128)(2,1)S(1)}, f16[2,2,48,1024]{3,2,1,0:T(8,128)(2,1)S(1)}, u32[]{:S(2)}, u32[]{:S(2)}) collective-permute-start(f16[2,2,48,1024]{3,2,1,0:T(8,128)(2,1)S(1)} %fusion.11), channel_id=1, source_target_pairs={{0,2},{1,3},{2,0},{3,1},{4,6},{5,7},{6,4},{7,5},{8,10},{9,11},{10,... | collective-permute-start | bytes 1179656 | tf_op jit(solution)/shard_map/ppermute | solution.py:169
  143.9 6.7 %collective-permute-start.8 = (f16[2,2,48,1024]{3,2,1,0:T(8,128)(2,1)S(1)}, f16[2,2,48,1024]{3,2,1,0:T(8,128)(2,1)S(1)}, u32[]{:S(2)}, u32[]{:S(2)}) collective-permute-start(f16[2,2,48,1024]{3,2,1,0:T(8,128)(2,1)S(1)} %fusion.9), channel_id=1, source_target_pairs={{0,4},{1,5},{2,6},{3,7},{4,0},{5,1},{6,2},{7,3},{8,12},{9,13},{10,... | collective-permute-start | bytes 1179656 | tf_op jit(solution)/shard_map/ppermute | solution.py:169
  150.7 2.6 %collective-permute-done.2 = f32[1,1,1,1024]{3,2,1,0:T(1,128)S(1)} collective-permute-done((f32[1,1,1,1024]{3,2,1,0:T(1,128)S(1)}, f32[1,1,1,1024]{3,2,1,0:T(1,128)S(1)}, u32[]{:S(2)}, u32[]{:S(2)}) %collective-permute-start.2) | collective-permute-done | bytes 4128 | tf_op jit(solution)/shard_map/ppermute | solution.py:169
  153.3 6.8 %collective-permute-done.9 = f32[1,1,1,1024]{3,2,1,0:T(1,128)S(1)} collective-permute-done((f32[1,1,1,1024]{3,2,1,0:T(1,128)S(1)}, f32[1,1,1,1024]{3,2,1,0:T(1,128)S(1)}, u32[]{:S(2)}, u32[]{:S(2)}) %collective-permute-start.9) | collective-permute-done | bytes 4128 | tf_op jit(solution)/shard_map/ppermute | solution.py:169
  160.3 1.8 %collective-permute-start.3 = (f16[2,48,1024]{2,1,0:T(8,128)(2,1)S(1)}, f16[2,48,1024]{2,1,0:T(8,128)(2,1)S(1)}, u32[]{:S(2)}, u32[]{:S(2)}) collective-permute-start(f16[2,48,1024]{2,1,0:T(8,128)(2,1)S(1)} %fusion.15), channel_id=1, source_target_pairs={{0,4},{1,5},{2,6},{3,7},{4,0},{5,1},{6,2},{7,3},{8,12},{9,13},{10,... | collective-permute-start | bytes 589832 | tf_op jit(solution)/shard_map/ppermute | solution.py:169
  162.7 1.7 collective-permute-start.10
  164.8 2.1 %collective-permute-done.4 = f32[1,1,1024]{2,1,0:T(1,128)S(1)} collective-permute-done((f32[1,1,1024]{2,1,0:T(1,128)S(1)}, f32[1,1,1024]{2,1,0:T(1,128)S(1)}, u32[]{:S(2)}, u32[]{:S(2)}) %collective-permute-start.4) | collective-permute-done | bytes 4128 | tf_op jit(solution)/shard_map/ppermute | solution.py:169
  166.8 1.8 collective-permute-done.11
  168.8 2.8 %collective-permute-start.5 = (f16[48,1024]{1,0:T(8,128)(2,1)S(1)}, f16[48,1024]{1,0:T(8,128)(2,1)S(1)}, u32[]{:S(2)}, u32[]{:S(2)}) collective-permute-start(f16[48,1024]{1,0:T(8,128)(2,1)S(1)} %fusion.19), channel_id=1, source_target_pairs={{0,8},{1,9},{2,10},{3,11},{4,12},{5,13},{6,14},{7,15},{8,0},{9,1},... | collective-permute-start | bytes 294920 | tf_op jit(solution)/shard_map/ppermute | solution.py:169
  171.9 2.8 %collective-permute-start.12 = (f16[48,1024]{1,0:T(8,128)(2,1)S(1)}, f16[48,1024]{1,0:T(8,128)(2,1)S(1)}, u32[]{:S(2)}, u32[]{:S(2)}) collective-permute-start(f16[48,1024]{1,0:T(8,128)(2,1)S(1)} %fusion.17), channel_id=1, source_target_pairs={{0,8},{1,9},{2,10},{3,11},{4,12},{5,13},{6,14},{7,15},{8,0},{9,1},... | collective-permute-start | bytes 294920 | tf_op jit(solution)/shard_map/ppermute | solution.py:169
  174.9 2.4 %collective-permute-done.6 = f32[1,1024]{1,0:T(1,128)S(1)} collective-permute-done((f32[1,1024]{1,0:T(1,128)S(1)}, f32[1,1024]{1,0:T(1,128)S(1)}, u32[]{:S(2)}, u32[]{:S(2)}) %collective-permute-start.6) | collective-permute-done | bytes 4128 | tf_op jit(solution)/shard_map/ppermute | solution.py:169
  177.4 2.2 %collective-permute-done.13 = f32[1,1024]{1,0:T(1,128)S(1)} collective-permute-done((f32[1,1024]{1,0:T(1,128)S(1)}, f32[1,1024]{1,0:T(1,128)S(1)}, u32[]{:S(2)}, u32[]{:S(2)}) %collective-permute-start.13) | collective-permute-done | bytes 4128 | tf_op jit(solution)/shard_map/ppermute | solution.py:169
  (85 shorter events, 16.5 us)
Async XLA Ops:
  5.9 7.5 %copy-start.10 = (s32[16,2]{0,1:T(2,128)S(1)}, s32[16,2]{0,1:T(2,128)}, u32[]{:S(2)}) copy-start(s32[16,2]{0,1:T(2,128)} %param.12) | copy-start | bytes 388
  5.9 32.7 %copy-start.2 = (s32[16]{0:T(128)S(1)}, s32[16]{0:T(128)}, u32[]{:S(2)}) copy-start(s32[16]{0:T(128)} %owner_ref.1) | copy-start | bytes 196
  5.9 32.7 %all-to-all-start = ((bf16[16,48,768]{2,1,0:T(8,128)(2,1)}), bf16[16,48,768]{2,1,0:T(8,128)(2,1)S(1)}, u32[]{:S(2)}, u32[]{:S(2)}) async-start(bf16[16,48,768]{2,1,0:T(8,128)(2,1)} %bitcast.120), calls=%async_computation | async-start | bytes 2359296 | tf_op jit(solution)/shard_map/all_to_all | solution.py:210
  40.7 7.7 %copy-start.6 = (bf16[1,768,768]{2,1,0:T(8,128)(2,1)S(1)}, bf16[1,768,768]{2,1,0:T(8,128)(2,1)}, u32[]{:S(2)}) copy-start(bf16[1,768,768]{2,1,0:T(8,128)(2,1)} %param.14) | copy-start | bytes 3538948
  40.7 53.4 %all-to-all-start.1 = ((bf16[16,2,48,768]{3,2,1,0:T(8,128)(2,1)}), bf16[16,2,48,768]{3,2,1,0:T(8,128)(2,1)}, u32[]{:S(2)}, u32[]{:S(2)}) async-start(bf16[16,2,48,768]{3,2,1,0:T(8,128)(2,1)} %copy-done.1), calls=%async_computation.1 | async-start | bytes 4718592 | tf_op jit(solution)/shard_map/all_to_all | solution.py:214
  51.8 2.9 %copy-start.3 = (bf16[768,512]{0,1:T(8,128)(2,1)}, bf16[768,512]{0,1:T(8,128)(2,1)S(1)}, u32[]{:S(2)}) copy-start(bf16[768,512]{0,1:T(8,128)(2,1)S(1)} %convolution_convert_fusion) | copy-start | bytes 2359300
  54.7 2.4 %copy-start.8 = (bf16[768,512]{1,0:T(8,128)(2,1)S(1)}, bf16[768,512]{1,0:T(8,128)(2,1)}, u32[]{:S(2)}) copy-start(bf16[768,512]{1,0:T(8,128)(2,1)} %param.18) | copy-start | bytes 2359300
  54.7 3.6 %copy-start.9 = (s32[1,12,12]{2,0,1:T(1,128)S(1)}, s32[1,12,12]{2,0,1:T(1,128)}, u32[]{:S(2)}) copy-start(s32[1,12,12]{2,0,1:T(1,128)} %param.13) | copy-start | bytes 1732
  126.7 11.1 %collective-permute-start = (f32[8,48,1024]{2,1,0:T(8,128)}, f32[8,48,1024]{2,1,0:T(8,128)}, u32[]{:S(2)}, u32[]{:S(2)}) collective-permute-start(f32[8,48,1024]{2,1,0:T(8,128)} %get-tuple-element.9), channel_id=1, source_target_pairs={{0,1},{1,0},{2,3},{3,2},{4,5},{5,4},{6,7},{7,6},{8,9},{9,8},{10,11... | collective-permute-start | bytes 4718600 | tf_op jit(solution)/shard_map/ppermute | solution.py:169
  127.5 16.0 %collective-permute-start.7 = (f32[8,48,1024]{2,1,0:T(8,128)}, f32[8,48,1024]{2,1,0:T(8,128)S(1)}, u32[]{:S(2)}, u32[]{:S(2)}) collective-permute-start(f32[8,48,1024]{2,1,0:T(8,128)} %get-tuple-element.11), channel_id=1, source_target_pairs={{0,1},{1,0},{2,3},{3,2},{4,5},{5,4},{6,7},{7,6},{8,9},{9,8},{10,11... | collective-permute-start | bytes 4718600 | tf_op jit(solution)/shard_map/ppermute | solution.py:169
  133.7 4.1 %copy-start.5 = (f32[8,48,1024]{2,1,0:T(8,128)S(1)}, f32[8,48,1024]{2,1,0:T(8,128)}, u32[]{:S(2)}) copy-start(f32[8,48,1024]{2,1,0:T(8,128)} %get-tuple-element.8) | copy-start | bytes 4718596
  139.4 4.0 %copy-start.4 = (f32[8,48,1024]{2,1,0:T(8,128)S(1)}, f32[8,48,1024]{2,1,0:T(8,128)}, u32[]{:S(2)}) copy-start(f32[8,48,1024]{2,1,0:T(8,128)} %get-tuple-element.10) | copy-start | bytes 4718596
  139.6 20.5 %collective-permute-start.1 = (f16[2,2,48,1024]{3,2,1,0:T(8,128)(2,1)S(1)}, f16[2,2,48,1024]{3,2,1,0:T(8,128)(2,1)S(1)}, u32[]{:S(2)}, u32[]{:S(2)}) collective-permute-start(f16[2,2,48,1024]{3,2,1,0:T(8,128)(2,1)S(1)} %fusion.11), channel_id=1, source_target_pairs={{0,2},{1,3},{2,0},{3,1},{4,6},{5,7},{6,4},{7,5},{8,10},{9,11},{10,... | collective-permute-start | bytes 1179656 | tf_op jit(solution)/shard_map/ppermute | solution.py:169
  143.4 9.9 %collective-permute-start.2 = (f32[1,1,1,1024]{3,2,1,0:T(1,128)S(1)}, f32[1,1,1,1024]{3,2,1,0:T(1,128)S(1)}, u32[]{:S(2)}, u32[]{:S(2)}) collective-permute-start(f32[1,1,1,1024]{3,2,1,0:T(1,128)S(1)} %bitcast.131), channel_id=1, source_target_pairs={{0,2},{1,3},{2,0},{3,1},{4,6},{5,7},{6,4},{7,5},{8,10},{9,11},{10,... | collective-permute-start | bytes 12296 | tf_op jit(solution)/shard_map/ppermute | solution.py:169
  143.9 18.5 %collective-permute-start.8 = (f16[2,2,48,1024]{3,2,1,0:T(8,128)(2,1)S(1)}, f16[2,2,48,1024]{3,2,1,0:T(8,128)(2,1)S(1)}, u32[]{:S(2)}, u32[]{:S(2)}) collective-permute-start(f16[2,2,48,1024]{3,2,1,0:T(8,128)(2,1)S(1)} %fusion.9), channel_id=1, source_target_pairs={{0,4},{1,5},{2,6},{3,7},{4,0},{5,1},{6,2},{7,3},{8,12},{9,13},{10,... | collective-permute-start | bytes 1179656 | tf_op jit(solution)/shard_map/ppermute | solution.py:169
  150.6 9.4 %collective-permute-start.9 = (f32[1,1,1,1024]{3,2,1,0:T(1,128)S(1)}, f32[1,1,1,1024]{3,2,1,0:T(1,128)S(1)}, u32[]{:S(2)}, u32[]{:S(2)}) collective-permute-start(f32[1,1,1,1024]{3,2,1,0:T(1,128)S(1)} %bitcast.134), channel_id=1, source_target_pairs={{0,4},{1,5},{2,6},{3,7},{4,0},{5,1},{6,2},{7,3},{8,12},{9,13},{10,... | collective-permute-start | bytes 12296 | tf_op jit(solution)/shard_map/ppermute | solution.py:169
  160.3 8.3 %collective-permute-start.3 = (f16[2,48,1024]{2,1,0:T(8,128)(2,1)S(1)}, f16[2,48,1024]{2,1,0:T(8,128)(2,1)S(1)}, u32[]{:S(2)}, u32[]{:S(2)}) collective-permute-start(f16[2,48,1024]{2,1,0:T(8,128)(2,1)S(1)} %fusion.15), channel_id=1, source_target_pairs={{0,4},{1,5},{2,6},{3,7},{4,0},{5,1},{6,2},{7,3},{8,12},{9,13},{10,... | collective-permute-start | bytes 589832 | tf_op jit(solution)/shard_map/ppermute | solution.py:169
  162.1 4.7 %collective-permute-start.4 = (f32[1,1,1024]{2,1,0:T(1,128)S(1)}, f32[1,1,1024]{2,1,0:T(1,128)S(1)}, u32[]{:S(2)}, u32[]{:S(2)}) collective-permute-start(f32[1,1,1024]{2,1,0:T(1,128)S(1)} %bitcast.129), channel_id=1, source_target_pairs={{0,4},{1,5},{2,6},{3,7},{4,0},{5,1},{6,2},{7,3},{8,12},{9,13},{10,... | collective-permute-start | bytes 12296 | tf_op jit(solution)/shard_map/ppermute | solution.py:169
  162.7 9.1 %collective-permute-start.10 = (f16[2,48,1024]{2,1,0:T(8,128)(2,1)S(1)}, f16[2,48,1024]{2,1,0:T(8,128)(2,1)S(1)}, u32[]{:S(2)}, u32[]{:S(2)}) collective-permute-start(f16[2,48,1024]{2,1,0:T(8,128)(2,1)S(1)} %fusion.13), channel_id=1, source_target_pairs={{0,2},{1,3},{2,0},{3,1},{4,6},{5,7},{6,4},{7,5},{8,10},{9,11},{10,... | collective-permute-start | bytes 589832 | tf_op jit(solution)/shard_map/ppermute | solution.py:169
  164.4 4.2 %collective-permute-start.11 = (f32[1,1,1024]{2,1,0:T(1,128)S(1)}, f32[1,1,1024]{2,1,0:T(1,128)S(1)}, u32[]{:S(2)}, u32[]{:S(2)}) collective-permute-start(f32[1,1,1024]{2,1,0:T(1,128)S(1)} %bitcast.132), channel_id=1, source_target_pairs={{0,2},{1,3},{2,0},{3,1},{4,6},{5,7},{6,4},{7,5},{8,10},{9,11},{10,... | collective-permute-start | bytes 12296 | tf_op jit(solution)/shard_map/ppermute | solution.py:169
  168.8 10.8 %collective-permute-start.5 = (f16[48,1024]{1,0:T(8,128)(2,1)S(1)}, f16[48,1024]{1,0:T(8,128)(2,1)S(1)}, u32[]{:S(2)}, u32[]{:S(2)}) collective-permute-start(f16[48,1024]{1,0:T(8,128)(2,1)S(1)} %fusion.19), channel_id=1, source_target_pairs={{0,8},{1,9},{2,10},{3,11},{4,12},{5,13},{6,14},{7,15},{8,0},{9,1},... | collective-permute-start | bytes 294920 | tf_op jit(solution)/shard_map/ppermute | solution.py:169
  171.6 5.8 %collective-permute-start.6 = (f32[1,1024]{1,0:T(1,128)S(1)}, f32[1,1024]{1,0:T(1,128)S(1)}, u32[]{:S(2)}, u32[]{:S(2)}) collective-permute-start(f32[1,1024]{1,0:T(1,128)S(1)} %bitcast.130), channel_id=1, source_target_pairs={{0,8},{1,9},{2,10},{3,11},{4,12},{5,13},{6,14},{7,15},{8,0},{9,1},... | collective-permute-start | bytes 12296 | tf_op jit(solution)/shard_map/ppermute | solution.py:169
  171.9 7.7 %collective-permute-start.12 = (f16[48,1024]{1,0:T(8,128)(2,1)S(1)}, f16[48,1024]{1,0:T(8,128)(2,1)S(1)}, u32[]{:S(2)}, u32[]{:S(2)}) collective-permute-start(f16[48,1024]{1,0:T(8,128)(2,1)S(1)} %fusion.17), channel_id=1, source_target_pairs={{0,8},{1,9},{2,10},{3,11},{4,12},{5,13},{6,14},{7,15},{8,0},{9,1},... | collective-permute-start | bytes 294920 | tf_op jit(solution)/shard_map/ppermute | solution.py:169
  174.7 4.9 %collective-permute-start.13 = (f32[1,1024]{1,0:T(1,128)S(1)}, f32[1,1024]{1,0:T(1,128)S(1)}, u32[]{:S(2)}, u32[]{:S(2)}) collective-permute-start(f32[1,1024]{1,0:T(1,128)S(1)} %bitcast.133), channel_id=1, source_target_pairs={{0,8},{1,9},{2,10},{3,11},{4,12},{5,13},{6,14},{7,15},{8,0},{9,1},... | collective-permute-start | bytes 12296 | tf_op jit(solution)/shard_map/ppermute | solution.py:169
  (3 other events, 4.6 us)

commit v3 on v2

--- a/solution.py
+++ b/solution.py
@@ -60,7 +60,7 @@
 
 def pair_body(
     heads, core_ref, token_ref, qw_ref, kw_ref, vw_ref, aug_ref, hot_ref, gt_ref, g_ref, cot_ref,
-    ctx_ref, keep_qk_ref, send_qk_ref, keep_vo_ref, send_vo_ref,
+    ctx_ref, keep_ref, send_ref,
     qn_ref, kn_ref, qt_ref, kt_ref, vt_ref, q_ref, k_ref, v_ref, gq_ref, gk_ref, gv_ref, val_ref,
 ):
     count, _, share, length = token_ref.shape
@@ -82,36 +82,47 @@
         k_ref[h] = jnp.concatenate([kt_ref[rows, :].T, aug_ref[...]], axis=1)
         v_ref[h] = vt_ref[rows, :].T
 
-    def one_head(h):
-        rows = pl.ds(pl.multiple_of(h * hsize, hsize), hsize)
-        query_aug = jnp.concatenate([qt_ref[rows, :] * scale, hot_ref[...]], axis=0)
-        scores = dot_nn(k_ref[h], query_aug)
-        top = jnp.max(scores, axis=0, keepdims=True)
-        weights = jnp.exp(scores - top)
-        total = jnp.sum(weights, axis=0, keepdims=True)
-        prob = weights * (1.0 / total)
-        low = prob.astype(BF16)
-        ctx_ref[rows, :] = dot_nn(vt_ref[rows, :], low).astype(BF16)
-        grad_prob = dot_nn(v_ref[h], gt_ref[rows, :] * scale)
+    def rows_of(h):
+        return pl.ds(pl.multiple_of(h * hsize, hsize), hsize)
+
+    def scores_of(h):
+        query_aug = jnp.concatenate([qt_ref[rows_of(h), :] * scale, hot_ref[...]], axis=0)
+        return dot_nn(k_ref[h], query_aug)
+
+    def softmax(scores):
+        weights = jnp.exp(scores - jnp.max(scores, axis=0, keepdims=True))
+        return weights * (1.0 / jnp.sum(weights, axis=0, keepdims=True))
+
+    def context_of(h, low):
+        ctx_ref[rows_of(h), :] = dot_nn(vt_ref[rows_of(h), :], low).astype(BF16)
+        return dot_nn(low, g_ref[h]).astype(BF16)
+
+    def grad_score_of(prob, grad_prob):
         inner = jnp.sum(prob * grad_prob, axis=0, keepdims=True)
-        grad_score = (prob * (grad_prob - inner)).astype(BF16)
-        gq_ref[rows, :] = dot_nn(kt_ref[rows, :], grad_score).astype(BF16)
-        return (
-            dot_nn(grad_score, q_ref[h]).astype(BF16),
-            dot_nn(low, g_ref[h]).astype(BF16),
+        return (prob * (grad_prob - inner)).astype(BF16)
+
+    def grads_of(h, grad_score):
+        gq_ref[rows_of(h), :] = dot_nn(kt_ref[rows_of(h), :], grad_score).astype(BF16)
+        return dot_nn(grad_score, q_ref[h]).astype(BF16)
+
+    def two_heads(i, carry):
+        pair = (2 * i, 2 * i + 1)
+        cols = pl.ds(pl.multiple_of(i * 2 * hsize, 2 * hsize), 2 * hsize)
+        scores = [scores_of(h) for h in pair]
+        grad_probs = [dot_nn(v_ref[h], gt_ref[rows_of(h), :] * scale) for h in pair]
+        probs = [softmax(each) for each in scores]
+        gv_ref[:, cols] = jnp.concatenate(
+            [context_of(h, prob.astype(BF16)) for h, prob in zip(pair, probs)], axis=1
         )
-
-    def two_heads(i, carry):
-        gk0, gv0 = one_head(2 * i)
-        gk1, gv1 = one_head(2 * i + 1)
-        cols = pl.ds(pl.multiple_of(i * 2 * hsize, 2 * hsize), 2 * hsize)
-        gk_ref[:, cols] = jnp.concatenate([gk0, gk1], axis=1)
-        gv_ref[:, cols] = jnp.concatenate([gv0, gv1], axis=1)
+        grad_scores = [grad_score_of(*each) for each in zip(probs, grad_probs)]
+        gk_ref[:, cols] = jnp.concatenate(
+            [grads_of(h, each) for h, each in zip(pair, grad_scores)], axis=1
+        )
         return carry
 
     lax.fori_loop(0, heads // 2, two_heads, 0)
 
-    blocks, rows_each, _ = keep_qk_ref.shape
+    blocks, rows_each, _ = keep_ref.shape
     for n, (left, right, dot) in enumerate(
         (
             (qn_ref, gq_ref, dot_nt),
@@ -120,8 +131,7 @@
             (cot_ref, ctx_ref, dot_nt),
         )
     ):
-        keep_ref, send_ref = ((keep_qk_ref, send_qk_ref), (keep_vo_ref, send_vo_ref))[n // 2]
-        cols = pl.ds((n % 2) * att, att)
+        cols = pl.ds(n * att, att)
         val_ref[...] = dot(left[...], right[...])
         for core, targets in ((0, (keep_ref, send_ref)), (1, (send_ref, keep_ref))):
 
@@ -136,15 +146,15 @@
     width = cot.shape[0]
     att = qw.shape[0]
     hsize = att // heads
-    part = jax.ShapeDtypeStruct((width // rows_each // 2, rows_each, 2 * att), F32)
+    part = jax.ShapeDtypeStruct((width // rows_each // 2, rows_each, 4 * att), F32)
     flat = pltpu.VMEM((att, length), BF16)
     each = pltpu.VMEM((heads, length, hsize), BF16)
     side = pltpu.VMEM((length, att), BF16)
     return pl.pallas_call(
         functools.partial(pair_body, heads),
-        out_shape=(jax.ShapeDtypeStruct((att, length), BF16), part, part, part, part),
+        out_shape=(jax.ShapeDtypeStruct((att, length), BF16), part, part),
         in_specs=[SMEM] + [VMEM] * 9,
-        out_specs=(VMEM,) * 5,
+        out_specs=(VMEM,) * 3,
         scratch_shapes=[
             pltpu.VMEM((width, length), BF16),
             pltpu.VMEM((width, length), BF16),
@@ -159,7 +169,7 @@
             side,
             pltpu.VMEM((width, att), F32),
         ],
-        compiler_params=pltpu.CompilerParams(vmem_limit_bytes=58 * 2**20),
+        compiler_params=pltpu.CompilerParams(vmem_limit_bytes=38 * 2**20),
         name="pair_pass",
     )(core, arrived, qw, kw, vw, aug, hot, gt, g, cot)
 
@@ -169,25 +179,52 @@
     return lax.ppermute(array, axis, [(d, d ^ (1 << bit)) for d in range(size)])
 
 
-def scatter_sum(keep, send, axis, order):
-    bits = lax.axis_size(axis).bit_length() - 1
+def out_body(token_ref, ow_ref, ctx_ref, out_ref):
+    count, _, share, length = token_ref.shape
+    for c in range(length // CHUNK):
+        cols = pl.ds(c * CHUNK, CHUNK)
+        tokens = token_ref[:, 0, :, cols].reshape(count * share, CHUNK)
+        summed = tokens.astype(F32) + dot_nn(ow_ref[...], ctx_ref[:, cols])
+        out_ref[cols, :] = summed.astype(BF16).T
+
+
+def out_side(arrived, ow, context):
+    width, att = ow.shape
+    length = context.shape[1]
+    return pl.pallas_call(
+        out_body,
+        out_shape=jax.ShapeDtypeStruct((length, width), BF16),
+        in_specs=[VMEM] * 3,
+        out_specs=VMEM,
+        compiler_params=pltpu.CompilerParams(vmem_limit_bytes=24 * 2**20),
+        cost_estimate=pl.CostEstimate(
+            flops=2 * width * att * length, bytes_accessed=6 * width * length, transcendentals=0
+        ),
+        name="attended_out",
+    )(arrived, ow, context)
+
+
+def halve(parts, axis, left, bits):
     me = lax.axis_index(axis)
-    part = keep + exchange(send, axis, 0)
-    rows, cols = part.shape[1:]
-    part = part.reshape((2,) * (bits - 1) + (rows, cols))
-    left = list(reversed(range(1, bits)))
-    for bit in order:
-        at = left.index(bit)
-        left.pop(at)
+    cut = []
+    for part, lefts, bit in zip(parts, left, bits):
+        at = lefts.index(bit)
+        lefts.pop(at)
         mine = (me >> bit) & 1
         send = lax.dynamic_index_in_dim(part, 1 - mine, at, keepdims=False)
         keep = lax.dynamic_index_in_dim(part, mine, at, keepdims=False)
         top = jnp.max(jnp.abs(send), axis=tuple(range(send.ndim - 1)), keepdims=True)
         power = jnp.ceil(jnp.log2(jnp.maximum(top, 1e-30)))
-        scaled = (send * jnp.exp2(8.0 - power)).astype(F16)
+        cut.append((keep, power, (send * jnp.exp2(8.0 - power)).astype(F16)))
+    return cut
+
+
+def join(cut, axis, bits):
+    out = []
+    for (keep, power, scaled), bit in zip(cut, bits):
         power = exchange(power, axis, bit)
-        part = keep + exchange(scaled, axis, bit).astype(F32) * jnp.exp2(power - 8.0)
-    return part
+        out.append(keep + exchange(scaled, axis, bit).astype(F32) * jnp.exp2(power - 8.0))
+    return out
 
 
 def per_device(
@@ -212,7 +249,6 @@
     )
     picked = pick(owner_slot, pairs, shares)
     arrived = lax.all_to_all(picked, "img", 0, 0, tiled=True)
-    query_tokens = arrived[:, 0].reshape(width, length)
     if share % 16:
         arrived = arrived.transpose(1, 0, 2, 3).reshape(1, 2, width, length)
 
@@ -226,18 +262,26 @@
     g = grad_context.reshape(length, HEADS, hsize).transpose(1, 0, 2)
     core = (lax.axis_index("img") % 2).astype(jnp.int32).reshape(1)
 
-    context, keep_qk, send_qk, keep_vo, send_vo = pair_side(
+    context, keep, send = pair_side(
         core, arrived, query_weight.T, key_weight.T, value_weight.T, aug, hot,
         grad_context.T, g, cot.T, HEADS, share,
     )
-    upward = list(range(1, bits))
-    qk = scatter_sum(keep_qk, send_qk, "img", upward)
-    vo = scatter_sum(keep_vo, send_vo, "img", upward[1:2] + upward[:1] + upward[2:])
-    attended = (
-        query_tokens.T.astype(F32)
-        + lax.dot_general(context, out_weight, (((0,), (1,)), ((), ())), preferred_element_type=F32)
-    ).astype(BF16)
-    return (attended[None], jnp.concatenate([qk, vo], axis=1) * (1.0 / devices_img))
+    part = keep + exchange(send, "img", 0)
+    half = part.shape[-1] // 2
+    dims = (2,) * (bits - 1) + (share, half)
+    parts = [part[:, :, :half].reshape(dims), part[:, :, half:].reshape(dims)]
+    left = [list(reversed(range(1, bits))) for _ in parts]
+    cut = halve(parts, "img", left, (1, 2))
+    context, *kept = lax.optimization_barrier((context, cut[0][2], cut[1][2]))
+    cut = [(keep, power, scaled) for (keep, power, _), scaled in zip(cut, kept)]
+    parts = join(cut, "img", (1, 2))
+    attended = out_side(arrived, out_weight, context)
+    parts = join(halve(parts, "img", left, (2, 1)), "img", (2, 1))
+    parts = [jnp.concatenate(parts, axis=-1)]
+    left = left[:1]
+    for bit in range(3, bits):
+        parts = join(halve(parts, "img", left, (bit,)), "img", (bit,))
+    return (attended[None], parts[0] * (1.0 / devices_img))
 
 
 def solution(mesh):

time: 181 us -> 183 us (1.011)
  local copies, waits for them, and re-layouts: 16.2 us -> 22.1 us
  waiting for transfers between devices: 77 us -> 82.8 us
  matrix products: 9.91 us -> 5.58 us
  starting transfers between devices: 36.8 us -> 33.6 us
    unnamed x27 -> x37, local copies, waits for them, and re-layouts: 9.32 us -> 19.7 us
    ppermute x14 -> x11, waiting for transfers between devices: 17.8 us -> 24.3 us  [exchange(): return lax.ppermute(array, axis, [(d, d ^ 1 << bit) for d in range(size)])]
    pallas_call x1, Pallas kernels: 32.6 us -> 27.6 us  [pair_side(): pl.pallas_call(functools.partial(pair_body, heads), out_shape=(jax.ShapeD...]
    dot_general x1 -> x0, matrix products: 4.1 us -> none  [per_device(): lax.dot_general(context, out_weight, (((0,), (1,)), ((), ())), preferred_...]
    pallas_call x0 -> x1, Pallas kernels: none -> 3.53 us  [out_side(): pl.pallas_call(out_body, out_shape=jax.ShapeDtypeStruct((length, width),...]
    ppermute x14 -> x11, starting transfers between devices: 21.6 us -> 18.4 us  [exchange(): return lax.ppermute(array, axis, [(d, d ^ 1 << bit) for d in range(size)])]
    convert_element_type x1 -> x0, local copies, waits for them, and re-layouts: 3.07 us -> none  [per_device(): query_tokens.T.astype(F32)]
    add x8 -> x5, other arithmetic: 2.38 us -> 3.93 us  [the longest x1 3.52 us: per_device(): part = keep + exchange(send, 'img', 0)]
  transfers between devices with their start and end apart: 16 -> 13, of which waited for: 8 -> 9; matrix products, arithmetic and copies ran while one was open for 14% -> 7% of each run, Pallas kernels for 0% -> 2%
where the time goes in v3:
time: 183 us; the launch traced here: 182 us
  waiting for transfers between devices  82.8 us (45%)
  starting transfers between devices  33.6 us (18%)
  Pallas kernels  31.9 us (17%)
  local copies, waits for them, and re-layouts  22.1 us (12%)
  matrix products  5.58 us (3%)
  other arithmetic  5.43 us (3%)
    all_to_all x1, waiting for transfers between devices, per_device(): arrived = lax.all_to_all(picked, 'img', 0, 0, tiled=True)  33.6 us
    pallas_call x1, Pallas kernels, pair_side(): pl.pallas_call(functools.partial(pair_body, heads), out_shape=(jax.ShapeD...  27.6 us
    all_to_all x1, waiting for transfers between devices, per_device(): lax.all_to_all(embedded.reshape(devices_img, share, length), 'img', 0, 0,...  24.9 us
    ppermute x11, waiting for transfers between devices, exchange(): return lax.ppermute(array, axis, [(d, d ^ 1 << bit) for d in range(size)])  24.3 us
    unnamed x37, local copies, waits for them, and re-layouts  19.7 us
    ppermute x11, starting transfers between devices, exchange(): return lax.ppermute(array, axis, [(d, d ^ 1 << bit) for d in range(size)])  18.4 us
    all_to_all x1, starting transfers between devices, per_device(): arrived = lax.all_to_all(picked, 'img', 0, 0, tiled=True)  7.66 us
    all_to_all x1, starting transfers between devices, per_device(): lax.all_to_all(embedded.reshape(devices_img, share, length), 'img', 0, 0,...  7.52 us
  transfers between devices with their start and end apart: 13, of which 9 were waited for; matrix products, arithmetic and copies ran while one was open for 7% of the time, Pallas kernels for 2%

profile of v3, /device:TPU:0, one launch (start us, length us, event | category | flops | bytes accessed | tf_op | source)
XLA Modules:
  0.0 182.4 jit_solution(8725714686090229378)
XLA Ops:
  2.0 3.9 %fusion.2 = bf16[768,768]{1,0:T(8,128)(2,1)} fusion(bf16[1024,768]{1,0:T(8,128)(2,1)S(1)} %copy-done, bf16[1,768,1024]{2,1,0:T(8,128)(2,1)} %param.10), kind=kOutput, calls=%fused_computation.2 | convolution fusion | flops 1208549376 | bytes 4325376 | tf_op jit(solution)/shard_map/dot_general | solution.py:244
  5.9 7.5 %all-to-all-start = ((bf16[16,48,768]{2,1,0:T(8,128)(2,1)}), bf16[16,48,768]{2,1,0:T(8,128)(2,1)S(1)}, u32[]{:S(2)}, u32[]{:S(2)}) async-start(bf16[16,48,768]{2,1,0:T(8,128)(2,1)} %bitcast.101), calls=%async_computation | async-start | bytes 2359296 | tf_op jit(solution)/shard_map/all_to_all | solution.py:247
  13.6 24.9 %all-to-all-done.shares_ref = bf16[16,48,768]{2,1,0:T(8,128)(2,1)S(1)} async-done(((bf16[16,48,768]{2,1,0:T(8,128)(2,1)}), bf16[16,48,768]{2,1,0:T(8,128)(2,1)S(1)}, u32[]{:S(2)}, u32[]{:S(2)}) %all-to-all-start) | async-done | bytes 1179680 | tf_op jit(solution)/shard_map/all_to_all | solution.py:247
  40.7 7.7 %all-to-all-start.1 = ((bf16[16,2,48,768]{3,2,1,0:T(8,128)(2,1)}), bf16[16,2,48,768]{3,2,1,0:T(8,128)(2,1)}, u32[]{:S(2)}, u32[]{:S(2)}) async-start(bf16[16,2,48,768]{3,2,1,0:T(8,128)(2,1)} %copy-done.1), calls=%async_computation.1 | async-start | bytes 4718592 | tf_op jit(solution)/shard_map/all_to_all | solution.py:251
  51.6 1.8 copy.24
  53.4 2.3 %copy.19 = bf16[768,512]{0,1:T(8,128)(2,1)} copy(bf16[768,512]{1,0:T(8,128)(2,1)} %param.16) | data formatting | bytes 1572864 | tf_op args[6]
  55.7 2.3 %copy.20 = bf16[768,512]{0,1:T(8,128)(2,1)} copy(bf16[768,512]{1,0:T(8,128)(2,1)} %param.17) | data formatting | bytes 1572864 | tf_op args[7]
  58.0 2.3 %copy.21 = bf16[768,512]{0,1:T(8,128)(2,1)} copy(bf16[768,512]{1,0:T(8,128)(2,1)} %param.18) | data formatting | bytes 1572864 | tf_op args[8]
  60.6 33.6 %all-to-all-done.1.token_ref = bf16[16,2,48,768]{3,2,1,0:T(8,128)(2,1)} async-done(((bf16[16,2,48,768]{3,2,1,0:T(8,128)(2,1)}), bf16[16,2,48,768]{3,2,1,0:T(8,128)(2,1)}, u32[]{:S(2)}, u32[]{:S(2)}) %all-to-all-start.1) | async-done | bytes 2359328 | tf_op jit(solution)/shard_map/all_to_all | solution.py:251
  99.9 27.6 %pair_pass.1 = (bf16[512,768]{1,0:T(8,128)(2,1)S(1)}, f32[8,48,2048]{2,1,0:T(8,128)S(1)}, f32[8,48,2048]{2,1,0:T(8,128)}) custom-call(s32[1]{0:T(128)} %bitcast.2.core_ref, bf16[16,2,48,768]{3,2,1,0:T(8,128)(2,1)} %all-to-all-done.1.token_ref, bf16[512,768]{1,0:T(8,128)(2,1)S(1)} %bitcast.89, bf16[512,768]{1,0:T(8,128)(2,1)S(1)} %bitcast.90, ...), custom_call_target="tpu_custom_call" | custom-call | tf_op jit(solution)/shard_map/pair_pass/pallas_call | solution.py:153
  131.0 5.6 %collective-permute-done = f32[8,48,2048]{2,1,0:T(8,128)} collective-permute-done((f32[8,48,2048]{2,1,0:T(8,128)}, f32[8,48,2048]{2,1,0:T(8,128)}, u32[]{:S(2)}, u32[]{:S(2)}) %collective-permute-start) | collective-permute-done | bytes 3145760 | tf_op jit(solution)/shard_map/ppermute | solution.py:179
  136.6 3.5 %add.61 = f32[8,48,2048]{2,1,0:T(8,128)S(1)} add(f32[8,48,2048]{2,1,0:T(8,128)} %copy-done.7, f32[8,48,2048]{2,1,0:T(8,128)} %collective-permute-done) | non-fusion elementwise | flops 786432 | bytes 9437184 | tf_op jit(solution)/shard_map/add | solution.py:269
  140.9 7.3 %collective-permute-start.5 = (f16[2,2,48,1024]{3,2,1,0:T(8,128)(2,1)S(1)}, f16[2,2,48,1024]{3,2,1,0:T(8,128)(2,1)S(1)}, u32[]{:S(2)}, u32[]{:S(2)}) collective-permute-start(f16[2,2,48,1024]{3,2,1,0:T(8,128)(2,1)S(1)} %fusion.7), channel_id=1, source_target_pairs={{0,4},{1,5},{2,6},{3,7},{4,0},{5,1},{6,2},{7,3},{8,12},{9,13},{10,... | collective-permute-start | bytes 1179656 | tf_op jit(solution)/shard_map/ppermute | solution.py:179
  148.3 3.0 %collective-permute-start.1 = (f16[2,2,48,1024]{3,2,1,0:T(8,128)(2,1)S(1)}, f16[2,2,48,1024]{3,2,1,0:T(8,128)(2,1)S(1)}, u32[]{:S(2)}, u32[]{:S(2)}) collective-permute-start(f16[2,2,48,1024]{3,2,1,0:T(8,128)(2,1)S(1)} %fusion.9), channel_id=1, source_target_pairs={{0,2},{1,3},{2,0},{3,1},{4,6},{5,7},{6,4},{7,5},{8,10},{9,11},{10,... | collective-permute-start | bytes 1179656 | tf_op jit(solution)/shard_map/ppermute | solution.py:179
  151.3 3.5 %attended_out.1 = bf16[768,768]{1,0:T(8,128)(2,1)} custom-call(bf16[16,2,48,768]{3,2,1,0:T(8,128)(2,1)} %all-to-all-done.1.token_ref, bf16[768,512]{1,0:T(8,128)(2,1)S(1)} %copy-done.9, bf16[512,768]{1,0:T(8,128)(2,1)S(1)} %copy-done.11), custom_call_target="tpu_custom_call" | custom-call | flops 603979776 | bytes 3538944 | tf_op jit(solution)/shard_map/attended_out/pallas_call | solution.py:194
  154.8 2.9 %collective-permute-done.6 = f32[1,1,1,1024]{3,2,1,0:T(1,128)S(1)} collective-permute-done((f32[1,1,1,1024]{3,2,1,0:T(1,128)S(1)}, f32[1,1,1,1024]{3,2,1,0:T(1,128)S(1)}, u32[]{:S(2)}, u32[]{:S(2)}) %collective-permute-start.6) | collective-permute-done | bytes 4128 | tf_op jit(solution)/shard_map/ppermute | solution.py:179
  157.7 3.0 %collective-permute-done.2 = f32[1,1,1,1024]{3,2,1,0:T(1,128)S(1)} collective-permute-done((f32[1,1,1,1024]{3,2,1,0:T(1,128)S(1)}, f32[1,1,1,1024]{3,2,1,0:T(1,128)S(1)}, u32[]{:S(2)}, u32[]{:S(2)}) %collective-permute-start.2) | collective-permute-done | bytes 4128 | tf_op jit(solution)/shard_map/ppermute | solution.py:179
  161.0 1.8 collective-permute-start.7
  163.3 1.7 collective-permute-start.3
  165.4 2.1 %collective-permute-done.8 = f32[1,1,1024]{2,1,0:T(1,128)S(1)} collective-permute-done((f32[1,1,1024]{2,1,0:T(1,128)S(1)}, f32[1,1,1024]{2,1,0:T(1,128)S(1)}, u32[]{:S(2)}, u32[]{:S(2)}) %collective-permute-start.8) | collective-permute-done | bytes 4128 | tf_op jit(solution)/shard_map/ppermute | solution.py:179
  167.5 1.8 collective-permute-done.4
  169.5 2.9 %collective-permute-start.10 = (f32[1,2048]{1,0:T(1,128)S(1)}, f32[1,2048]{1,0:T(1,128)S(1)}, u32[]{:S(2)}, u32[]{:S(2)}) collective-permute-start(f32[1,2048]{1,0:T(1,128)S(1)} %bitcast.109), channel_id=1, source_target_pairs={{0,8},{1,9},{2,10},{3,11},{4,12},{5,13},{6,14},{7,15},{8,0},{9,1},... | collective-permute-start | bytes 24584 | tf_op jit(solution)/shard_map/ppermute | solution.py:179
  172.6 3.0 %collective-permute-done.10 = f32[1,2048]{1,0:T(1,128)S(1)} collective-permute-done((f32[1,2048]{1,0:T(1,128)S(1)}, f32[1,2048]{1,0:T(1,128)S(1)}, u32[]{:S(2)}, u32[]{:S(2)}) %collective-permute-start.10) | collective-permute-done | bytes 8224 | tf_op jit(solution)/shard_map/ppermute | solution.py:179
  175.6 6.0 %collective-permute-done.9 = f16[48,2048]{1,0:T(8,128)(2,1)S(1)} collective-permute-done((f16[48,2048]{1,0:T(8,128)(2,1)S(1)}, f16[48,2048]{1,0:T(8,128)(2,1)S(1)}, u32[]{:S(2)}, u32[]{:S(2)}) %collective-permute-start.9) | collective-permute-done | bytes 196640 | tf_op jit(solution)/shard_map/ppermute | solution.py:179
  (80 shorter events, 19.5 us)
Async XLA Ops:
  0.6 1.4 copy-start
  5.9 7.5 %copy-start.15 = (s32[16,2]{0,1:T(2,128)S(1)}, s32[16,2]{0,1:T(2,128)}, u32[]{:S(2)}) copy-start(s32[16,2]{0,1:T(2,128)} %param.12) | copy-start | bytes 388
  5.9 32.7 %copy-start.12 = (s32[16]{0:T(128)S(1)}, s32[16]{0:T(128)}, u32[]{:S(2)}) copy-start(s32[16]{0:T(128)} %owner_ref.1) | copy-start | bytes 196
  5.9 32.7 %all-to-all-start = ((bf16[16,48,768]{2,1,0:T(8,128)(2,1)}), bf16[16,48,768]{2,1,0:T(8,128)(2,1)S(1)}, u32[]{:S(2)}, u32[]{:S(2)}) async-start(bf16[16,48,768]{2,1,0:T(8,128)(2,1)} %bitcast.101), calls=%async_computation | async-start | bytes 2359296 | tf_op jit(solution)/shard_map/all_to_all | solution.py:247
  39.3 1.4 copy-start.1
  40.7 7.7 %copy-start.13 = (bf16[1,768,768]{2,1,0:T(8,128)(2,1)S(1)}, bf16[1,768,768]{2,1,0:T(8,128)(2,1)}, u32[]{:S(2)}) copy-start(bf16[1,768,768]{2,1,0:T(8,128)(2,1)} %param.14) | copy-start | bytes 3538948
  40.7 53.4 %all-to-all-start.1 = ((bf16[16,2,48,768]{3,2,1,0:T(8,128)(2,1)}), bf16[16,2,48,768]{3,2,1,0:T(8,128)(2,1)}, u32[]{:S(2)}, u32[]{:S(2)}) async-start(bf16[16,2,48,768]{3,2,1,0:T(8,128)(2,1)} %copy-done.1), calls=%async_computation.1 | async-start | bytes 4718592 | tf_op jit(solution)/shard_map/all_to_all | solution.py:251
  48.4 1.5 copy-start.8
  55.7 4.6 %copy-start.14 = (s32[1,12,12]{2,0,1:T(1,128)S(1)}, s32[1,12,12]{2,0,1:T(1,128)}, u32[]{:S(2)}) copy-start(s32[1,12,12]{2,0,1:T(1,128)} %param.13) | copy-start | bytes 1732
  94.1 1.3 copy-start.2
  127.6 1.7 copy-start.7
  130.2 6.5 %collective-permute-start = (f32[8,48,2048]{2,1,0:T(8,128)}, f32[8,48,2048]{2,1,0:T(8,128)}, u32[]{:S(2)}, u32[]{:S(2)}) collective-permute-start(f32[8,48,2048]{2,1,0:T(8,128)} %get-tuple-element.10), channel_id=1, source_target_pairs={{0,1},{1,0},{2,3},{3,2},{4,5},{5,4},{6,7},{7,6},{8,9},{9,8},{10,11... | collective-permute-start | bytes 9437192 | tf_op jit(solution)/shard_map/ppermute | solution.py:179
  140.6 10.6 %copy-start.9 = (bf16[768,512]{1,0:T(8,128)(2,1)S(1)}, bf16[768,512]{1,0:T(8,128)(2,1)}, u32[]{:S(2)}) copy-start(bf16[768,512]{1,0:T(8,128)(2,1)} %ow_ref.1) | copy-start | bytes 2359300
  140.7 10.6 %copy-start.11 = (bf16[512,768]{1,0:T(8,128)(2,1)S(1)}, bf16[512,768]{1,0:T(8,128)(2,1)}, u32[]{:S(2)}) copy-start(bf16[512,768]{1,0:T(8,128)(2,1)} %copy-done.10) | copy-start | bytes 2359300
  140.9 19.8 %collective-permute-start.5 = (f16[2,2,48,1024]{3,2,1,0:T(8,128)(2,1)S(1)}, f16[2,2,48,1024]{3,2,1,0:T(8,128)(2,1)S(1)}, u32[]{:S(2)}, u32[]{:S(2)}) collective-permute-start(f16[2,2,48,1024]{3,2,1,0:T(8,128)(2,1)S(1)} %fusion.7), channel_id=1, source_target_pairs={{0,4},{1,5},{2,6},{3,7},{4,0},{5,1},{6,2},{7,3},{8,12},{9,13},{10,... | collective-permute-start | bytes 1179656 | tf_op jit(solution)/shard_map/ppermute | solution.py:179
  148.2 9.5 %collective-permute-start.6 = (f32[1,1,1,1024]{3,2,1,0:T(1,128)S(1)}, f32[1,1,1,1024]{3,2,1,0:T(1,128)S(1)}, u32[]{:S(2)}, u32[]{:S(2)}) collective-permute-start(f32[1,1,1,1024]{3,2,1,0:T(1,128)S(1)} %bitcast.111), channel_id=1, source_target_pairs={{0,4},{1,5},{2,6},{3,7},{4,0},{5,1},{6,2},{7,3},{8,12},{9,13},{10,... | collective-permute-start | bytes 12296 | tf_op jit(solution)/shard_map/ppermute | solution.py:179
  148.3 14.8 %collective-permute-start.1 = (f16[2,2,48,1024]{3,2,1,0:T(8,128)(2,1)S(1)}, f16[2,2,48,1024]{3,2,1,0:T(8,128)(2,1)S(1)}, u32[]{:S(2)}, u32[]{:S(2)}) collective-permute-start(f16[2,2,48,1024]{3,2,1,0:T(8,128)(2,1)S(1)} %fusion.9), channel_id=1, source_target_pairs={{0,2},{1,3},{2,0},{3,1},{4,6},{5,7},{6,4},{7,5},{8,10},{9,11},{10,... | collective-permute-start | bytes 1179656 | tf_op jit(solution)/shard_map/ppermute | solution.py:179
  151.2 9.4 %collective-permute-start.2 = (f32[1,1,1,1024]{3,2,1,0:T(1,128)S(1)}, f32[1,1,1,1024]{3,2,1,0:T(1,128)S(1)}, u32[]{:S(2)}, u32[]{:S(2)}) collective-permute-start(f32[1,1,1,1024]{3,2,1,0:T(1,128)S(1)} %bitcast.112), channel_id=1, source_target_pairs={{0,2},{1,3},{2,0},{3,1},{4,6},{5,7},{6,4},{7,5},{8,10},{9,11},{10,... | collective-permute-start | bytes 12296 | tf_op jit(solution)/shard_map/ppermute | solution.py:179
  161.0 8.3 %collective-permute-start.7 = (f16[2,48,1024]{2,1,0:T(8,128)(2,1)S(1)}, f16[2,48,1024]{2,1,0:T(8,128)(2,1)S(1)}, u32[]{:S(2)}, u32[]{:S(2)}) collective-permute-start(f16[2,48,1024]{2,1,0:T(8,128)(2,1)S(1)} %fusion.17), channel_id=1, source_target_pairs={{0,2},{1,3},{2,0},{3,1},{4,6},{5,7},{6,4},{7,5},{8,10},{9,11},{10,... | collective-permute-start | bytes 589832 | tf_op jit(solution)/shard_map/ppermute | solution.py:179
  162.8 4.7 %collective-permute-start.8 = (f32[1,1,1024]{2,1,0:T(1,128)S(1)}, f32[1,1,1024]{2,1,0:T(1,128)S(1)}, u32[]{:S(2)}, u32[]{:S(2)}) collective-permute-start(f32[1,1,1024]{2,1,0:T(1,128)S(1)} %bitcast.110), channel_id=1, source_target_pairs={{0,2},{1,3},{2,0},{3,1},{4,6},{5,7},{6,4},{7,5},{8,10},{9,11},{10,... | collective-permute-start | bytes 12296 | tf_op jit(solution)/shard_map/ppermute | solution.py:179
  163.3 6.0 %collective-permute-start.3 = (f16[2,48,1024]{2,1,0:T(8,128)(2,1)S(1)}, f16[2,48,1024]{2,1,0:T(8,128)(2,1)S(1)}, u32[]{:S(2)}, u32[]{:S(2)}) collective-permute-start(f16[2,48,1024]{2,1,0:T(8,128)(2,1)S(1)} %fusion.19), channel_id=1, source_target_pairs={{0,4},{1,5},{2,6},{3,7},{4,0},{5,1},{6,2},{7,3},{8,12},{9,13},{10,... | collective-permute-start | bytes 589832 | tf_op jit(solution)/shard_map/ppermute | solution.py:179
  165.1 4.2 %collective-permute-start.4 = (f32[1,1,1024]{2,1,0:T(1,128)S(1)}, f32[1,1,1024]{2,1,0:T(1,128)S(1)}, u32[]{:S(2)}, u32[]{:S(2)}) collective-permute-start(f32[1,1,1024]{2,1,0:T(1,128)S(1)} %bitcast.113), channel_id=1, source_target_pairs={{0,4},{1,5},{2,6},{3,7},{4,0},{5,1},{6,2},{7,3},{8,12},{9,13},{10,... | collective-permute-start | bytes 12296 | tf_op jit(solution)/shard_map/ppermute | solution.py:179
  169.5 6.0 %collective-permute-start.10 = (f32[1,2048]{1,0:T(1,128)S(1)}, f32[1,2048]{1,0:T(1,128)S(1)}, u32[]{:S(2)}, u32[]{:S(2)}) collective-permute-start(f32[1,2048]{1,0:T(1,128)S(1)} %bitcast.109), channel_id=1, source_target_pairs={{0,8},{1,9},{2,10},{3,11},{4,12},{5,13},{6,14},{7,15},{8,0},{9,1},... | collective-permute-start | bytes 24584 | tf_op jit(solution)/shard_map/ppermute | solution.py:179
  172.4 9.1 %collective-permute-start.9 = (f16[48,2048]{1,0:T(8,128)(2,1)S(1)}, f16[48,2048]{1,0:T(8,128)(2,1)S(1)}, u32[]{:S(2)}, u32[]{:S(2)}) collective-permute-start(f16[48,2048]{1,0:T(8,128)(2,1)S(1)} %multiply_convert_fusion), channel_id=1, source_target_pairs={{0,8},{1,9},{2,10},{3,11},{4,12},{5,13},{6,14},{7,15},{8,0},{9,1},... | collective-permute-start | bytes 589832 | tf_op jit(solution)/shard_map/ppermute | solution.py:179
  (5 other events, 5.4 us)

commit v4 on v3

--- a/solution.py
+++ b/solution.py
@@ -11,11 +11,13 @@
 HEADS = 8
 BLOCK = 64
 CHUNK = 256
+GROUP = 512
 DEAD = -1e30
 F32 = jnp.float32
 F16 = jnp.float16
 BF16 = jnp.bfloat16
 VMEM = pl.BlockSpec(memory_space=pltpu.VMEM)
+HBM = pl.BlockSpec(memory_space=pltpu.HBM)
 SMEM = pl.BlockSpec(memory_space=pltpu.SMEM)
 
 
@@ -36,14 +38,9 @@
 
 
 def pick_body(owner_ref, pairs_ref, shares_ref, out_ref):
-    count = shares_ref.shape[0]
-
-    def step(p, carry):
+    for p in range(shares_ref.shape[0]):
         for side in range(2):
             out_ref[p, side] = shares_ref[owner_ref[pairs_ref[2 * p + side]]]
-        return carry
-
-    lax.fori_loop(0, count, step, 0, unroll=4)
 
 
 def pick(owner_slot, pairs, shares):
@@ -59,31 +56,54 @@
 
 
 def pair_body(
-    heads, core_ref, token_ref, qw_ref, kw_ref, vw_ref, aug_ref, hot_ref, gt_ref, g_ref, cot_ref,
-    ctx_ref, keep_ref, send_ref,
-    qn_ref, kn_ref, qt_ref, kt_ref, vt_ref, q_ref, k_ref, v_ref, gq_ref, gk_ref, gv_ref, val_ref,
+    heads, core_ref, token_in, qw_in, kw_in, vw_in, aug_in, hot_in, gt_in, cot_in,
+    ctx_ref, keep_qk_ref, send_qk_ref, keep_vo_ref, send_vo_ref,
+    token_ref, qw_ref, kw_ref, vw_ref, aug_ref, hot_ref, gt_ref, cot_ref,
+    qn_ref, kn_ref, qt_ref, kt_ref, vt_ref, k_ref, v_ref, gq_ref, val_ref,
+    token_sems, in_sems, out_sems,
 ):
     count, _, share, length = token_ref.shape
     att = qw_ref.shape[0]
     hsize = att // heads
     scale = jnp.asarray(1.0 / math.sqrt(hsize), BF16)
-    for c in range(length // CHUNK):
-        cols = pl.ds(c * CHUNK, CHUNK)
+    chunks = [pl.ds(c * CHUNK, CHUNK) for c in range(length // CHUNK)]
+    tokens_here = [
+        pltpu.make_async_copy(
+            token_in.at[:, :, :, cols], token_ref.at[:, :, :, cols], token_sems.at[c]
+        )
+        for c, cols in enumerate(chunks)
+    ]
+    in_pairs = (
+        (qw_in, qw_ref), (kw_in, kw_ref), (vw_in, vw_ref), (aug_in, aug_ref), (hot_in, hot_ref),
+        (gt_in, gt_ref), (cot_in, cot_ref),
+    )
+    others = [
+        pltpu.make_async_copy(source, target, in_sems.at[n])
+        for n, (source, target) in enumerate(in_pairs)
+    ]
+    for copy in tokens_here[:1] + others[:3] + tokens_here[1:] + others[3:]:
+        copy.start()
+    for c, cols in enumerate(chunks):
+        tokens_here[c].wait()
         query_n = norm_columns(token_ref[:, 0, :, cols].reshape(count * share, CHUNK))
         key_n = norm_columns(token_ref[:, 1, :, cols].reshape(count * share, CHUNK))
         qn_ref[:, cols] = query_n
         kn_ref[:, cols] = key_n
+        if c == 0:
+            for copy in others[:3]:
+                copy.wait()
         qt_ref[:, cols] = dot_nn(qw_ref[...], query_n).astype(BF16)
         kt_ref[:, cols] = dot_nn(kw_ref[...], key_n).astype(BF16)
         vt_ref[:, cols] = dot_nn(vw_ref[...], key_n).astype(BF16)
+    for copy in others[3:]:
+        copy.wait()
     for h in range(heads):
         rows = pl.ds(h * hsize, hsize)
-        q_ref[h] = qt_ref[rows, :].T
         k_ref[h] = jnp.concatenate([kt_ref[rows, :].T, aug_ref[...]], axis=1)
         v_ref[h] = vt_ref[rows, :].T
 
     def rows_of(h):
-        return pl.ds(pl.multiple_of(h * hsize, hsize), hsize)
+        return pl.ds(h * hsize, hsize)
 
     def scores_of(h):
         query_aug = jnp.concatenate([qt_ref[rows_of(h), :] * scale, hot_ref[...]], axis=0)
@@ -95,7 +115,7 @@
 
     def context_of(h, low):
         ctx_ref[rows_of(h), :] = dot_nn(vt_ref[rows_of(h), :], low).astype(BF16)
-        return dot_nn(low, g_ref[h]).astype(BF16)
+        return dot_nt(low, gt_ref[rows_of(h), :]).astype(BF16)
 
     def grad_score_of(prob, grad_prob):
         inner = jnp.sum(prob * grad_prob, axis=0, keepdims=True)
@@ -103,75 +123,97 @@
 
     def grads_of(h, grad_score):
         gq_ref[rows_of(h), :] = dot_nn(kt_ref[rows_of(h), :], grad_score).astype(BF16)
-        return dot_nn(grad_score, q_ref[h]).astype(BF16)
-
-    def two_heads(i, carry):
+        return dot_nt(grad_score, qt_ref[rows_of(h), :]).astype(BF16)
+
+    def two_heads(i):
         pair = (2 * i, 2 * i + 1)
-        cols = pl.ds(pl.multiple_of(i * 2 * hsize, 2 * hsize), 2 * hsize)
         scores = [scores_of(h) for h in pair]
         grad_probs = [dot_nn(v_ref[h], gt_ref[rows_of(h), :] * scale) for h in pair]
         probs = [softmax(each) for each in scores]
-        gv_ref[:, cols] = jnp.concatenate(
-            [context_of(h, prob.astype(BF16)) for h, prob in zip(pair, probs)], axis=1
+        grad_values = [context_of(h, prob.astype(BF16)) for h, prob in zip(pair, probs)]
+        grad_scores = [grad_score_of(*each) for each in zip(probs, grad_probs)]
+        return [grads_of(h, each) for h, each in zip(pair, grad_scores)], grad_values
+
+    mine = core_ref[0]
+    blocks, rows_each, _ = keep_qk_ref.shape
+    group = val_ref.shape[-1]
+    per_group = group // hsize
+    outs = ((keep_qk_ref, send_qk_ref), (keep_vo_ref, send_vo_ref))
+
+    def leaving(i, n, m):
+        cols = pl.ds((n % 2) * att + i * group, group)
+        return pltpu.make_async_copy(
+            val_ref.at[i, n, :, mine if m == 0 else 1 - mine],
+            outs[n // 2][m].at[:, :, cols],
+            out_sems.at[i, n, m],
         )
-        grad_scores = [grad_score_of(*each) for each in zip(probs, grad_probs)]
-        gk_ref[:, cols] = jnp.concatenate(
-            [grads_of(h, each) for h, each in zip(pair, grad_scores)], axis=1
-        )
+
+    def one_group(i, carry):
+        grad_keys, grad_values = [], []
+        for j in range(per_group // 2):
+            more_keys, more_values = two_heads(i * (per_group // 2) + j)
+            grad_keys += more_keys
+            grad_values += more_values
+        rows = pl.ds(i * group, group)
+        for n, grad in (
+            (2, lambda: dot_nn(kn_ref[...], jnp.concatenate(grad_values, axis=1))),
+            (3, lambda: dot_nt(cot_ref[...], ctx_ref[rows, :])),
+            (1, lambda: dot_nn(kn_ref[...], jnp.concatenate(grad_keys, axis=1))),
+            (0, lambda: dot_nt(qn_ref[...], gq_ref[rows, :])),
+        ):
+            grad = grad()
+            if rows_each % 8:
+                for b in range(2 * blocks):
+                    block = grad[b * rows_each : (b + 1) * rows_each, :]
+                    val_ref[i, n, b // 2, b % 2] = block
+            else:
+                val_ref[i, n] = grad.reshape(blocks, 2, rows_each, group)
+            for m in range(2):
+                leaving(i, n, m).start()
         return carry
 
-    lax.fori_loop(0, heads // 2, two_heads, 0)
-
-    blocks, rows_each, _ = keep_ref.shape
-    for n, (left, right, dot) in enumerate(
-        (
-            (qn_ref, gq_ref, dot_nt),
-            (kn_ref, gk_ref, dot_nn),
-            (kn_ref, gv_ref, dot_nn),
-            (cot_ref, ctx_ref, dot_nt),
-        )
-    ):
-        cols = pl.ds(n * att, att)
-        val_ref[...] = dot(left[...], right[...])
-        for core, targets in ((0, (keep_ref, send_ref)), (1, (send_ref, keep_ref))):
-
-            @pl.when(core_ref[0] == core)
-            def _():
-                for b in range(2 * blocks):
-                    targets[b % 2][b // 2, :, cols] = val_ref[pl.ds(b * rows_each, rows_each), :]
-
-
-def pair_side(core, arrived, qw, kw, vw, aug, hot, gt, g, cot, heads, rows_each):
+    groups = att // group
+    for i in range(groups):
+        one_group(i, 0)
+    for i in range(groups):
+        for n in range(4):
+            for m in range(2):
+                leaving(i, n, m).wait()
+
+
+def pair_side(core, arrived, qw, kw, vw, aug, hot, gt, cot, heads, rows_each):
     length = arrived.shape[-1]
     width = cot.shape[0]
     att = qw.shape[0]
     hsize = att // heads
-    part = jax.ShapeDtypeStruct((width // rows_each // 2, rows_each, 4 * att), F32)
+    blocks = width // rows_each // 2
+    part = jax.ShapeDtypeStruct((blocks, rows_each, 2 * att), F32)
     flat = pltpu.VMEM((att, length), BF16)
-    each = pltpu.VMEM((heads, length, hsize), BF16)
-    side = pltpu.VMEM((length, att), BF16)
+    square = pltpu.VMEM((width, length), BF16)
+    inputs = (arrived, qw, kw, vw, aug, hot, gt, cot)
     return pl.pallas_call(
         functools.partial(pair_body, heads),
-        out_shape=(jax.ShapeDtypeStruct((att, length), BF16), part, part),
-        in_specs=[SMEM] + [VMEM] * 9,
-        out_specs=(VMEM,) * 3,
-        scratch_shapes=[
-            pltpu.VMEM((width, length), BF16),
-            pltpu.VMEM((width, length), BF16),
+        out_shape=(jax.ShapeDtypeStruct((att, length), BF16), part, part, part, part),
+        in_specs=[SMEM] + [HBM] * len(inputs),
+        out_specs=(VMEM,) + (HBM,) * 4,
+        scratch_shapes=[pltpu.VMEM(array.shape, array.dtype) for array in inputs]
+        + [
+            square,
+            square,
             flat,
             flat,
             flat,
-            each,
             pltpu.VMEM((heads, length, 2 * hsize), BF16),
-            each,
+            pltpu.VMEM((heads, length, hsize), BF16),
             flat,
-            side,
-            side,
-            pltpu.VMEM((width, att), F32),
+            pltpu.VMEM((att // GROUP, 4, blocks, 2, rows_each, GROUP), F32),
+            pltpu.SemaphoreType.DMA((length // CHUNK,)),
+            pltpu.SemaphoreType.DMA((len(inputs) - 1,)),
+            pltpu.SemaphoreType.DMA((att // GROUP, 4, 2)),
         ],
-        compiler_params=pltpu.CompilerParams(vmem_limit_bytes=38 * 2**20),
+        compiler_params=pltpu.CompilerParams(vmem_limit_bytes=56 * 2**20),
         name="pair_pass",
-    )(core, arrived, qw, kw, vw, aug, hot, gt, g, cot)
+    )(core, *inputs)
 
 
 def exchange(array, axis, bit):
@@ -259,21 +301,18 @@
         == lax.broadcasted_iota(jnp.int32, (hsize, length), 1) // BLOCK
     ).astype(BF16)
     grad_context = jnp.dot(cot, out_weight, preferred_element_type=F32).astype(BF16)
-    g = grad_context.reshape(length, HEADS, hsize).transpose(1, 0, 2)
     core = (lax.axis_index("img") % 2).astype(jnp.int32).reshape(1)
 
-    context, keep, send = pair_side(
+    context, keep_qk, send_qk, keep_vo, send_vo = pair_side(
         core, arrived, query_weight.T, key_weight.T, value_weight.T, aug, hot,
-        grad_context.T, g, cot.T, HEADS, share,
+        grad_context.T, cot.T, HEADS, share,
     )
-    part = keep + exchange(send, "img", 0)
-    half = part.shape[-1] // 2
-    dims = (2,) * (bits - 1) + (share, half)
-    parts = [part[:, :, :half].reshape(dims), part[:, :, half:].reshape(dims)]
+    parts = [keep_qk + exchange(send_qk, "img", 0), keep_vo + exchange(send_vo, "img", 0)]
+    dims = (2,) * (bits - 1) + parts[0].shape[1:]
+    parts = [part.reshape(dims) for part in parts]
     left = [list(reversed(range(1, bits))) for _ in parts]
     cut = halve(parts, "img", left, (1, 2))
-    context, *kept = lax.optimization_barrier((context, cut[0][2], cut[1][2]))
-    cut = [(keep, power, scaled) for (keep, power, _), scaled in zip(cut, kept)]
+    context = lax.optimization_barrier((context, cut[0][2], cut[1][2]))[0]
     parts = join(cut, "img", (1, 2))
     attended = out_side(arrived, out_weight, context)
     parts = join(halve(parts, "img", left, (2, 1)), "img", (2, 1))

time: 183 us -> 174 us (0.951)
  local copies, waits for them, and re-layouts: 22.1 us -> 11.2 us
    unnamed x37 -> x25, local copies, waits for them, and re-layouts: 19.7 us -> 10.2 us
    ppermute x11 -> x12, waiting for transfers between devices: 24.3 us -> 21.9 us  [exchange(): return lax.ppermute(array, axis, [(d, d ^ 1 << bit) for d in range(size)])]
    add x1 -> x2, other arithmetic: 3.52 us -> 3.9 us  [the longest x1 2.23 us: per_device(): keep_vo + exchange(send_vo, 'img', 0)]
    ppermute x11 -> x12, starting transfers between devices: 18.4 us -> 18.7 us  [exchange(): return lax.ppermute(array, axis, [(d, d ^ 1 << bit) for d in range(size)])]
  transfers between devices with their start and end apart: 13 -> 14, of which waited for: 9 -> 9; matrix products, arithmetic and copies ran while one was open for 7% -> 9% of each run, Pallas kernels for 2% -> 2%
where the time goes in v4:
time: 174 us; the launch traced here: 173 us
  waiting for transfers between devices  81.9 us (47%)
  starting transfers between devices  33.9 us (19%)
  Pallas kernels  33.2 us (19%)
  local copies, waits for them, and re-layouts  11.2 us (6%)
  other arithmetic  6.45 us (4%)
  matrix products  5.55 us (3%)
    all_to_all x1, waiting for transfers between devices, per_device(): arrived = lax.all_to_all(picked, 'img', 0, 0, tiled=True)  35.1 us
    pallas_call x1, Pallas kernels, pair_side(): pl.pallas_call(functools.partial(pair_body, heads), out_shape=(jax.ShapeD...  28.9 us
    all_to_all x1, waiting for transfers between devices, per_device(): lax.all_to_all(embedded.reshape(devices_img, share, length), 'img', 0, 0,...  24.9 us
    ppermute x12, waiting for transfers between devices, exchange(): return lax.ppermute(array, axis, [(d, d ^ 1 << bit) for d in range(size)])  21.9 us
    ppermute x12, starting transfers between devices, exchange(): return lax.ppermute(array, axis, [(d, d ^ 1 << bit) for d in range(size)])  18.7 us
    unnamed x25, local copies, waits for them, and re-layouts  10.2 us
    all_to_all x1, starting transfers between devices, per_device(): arrived = lax.all_to_all(picked, 'img', 0, 0, tiled=True)  7.66 us
    all_to_all x1, starting transfers between devices, per_device(): lax.all_to_all(embedded.reshape(devices_img, share, length), 'img', 0, 0,...  7.52 us
  transfers between devices with their start and end apart: 14, of which 9 were waited for; matrix products, arithmetic and copies ran while one was open for 9% of the time, Pallas kernels for 2%

profile of v4, /device:TPU:0, one launch (start us, length us, event | category | flops | bytes accessed | tf_op | source)
XLA Modules:
  0.0 173.1 jit_solution(12533911347804000643)
XLA Ops:
  2.0 3.9 %fusion.2 = bf16[768,768]{1,0:T(8,128)(2,1)} fusion(bf16[1024,768]{1,0:T(8,128)(2,1)S(1)} %copy-done, bf16[1,768,1024]{2,1,0:T(8,128)(2,1)} %param.10), kind=kOutput, calls=%fused_computation.2 | convolution fusion | flops 1208549376 | bytes 4325376 | tf_op jit(solution)/shard_map/dot_general | solution.py:286
  5.9 7.5 %all-to-all-start = ((bf16[16,48,768]{2,1,0:T(8,128)(2,1)}), bf16[16,48,768]{2,1,0:T(8,128)(2,1)S(1)}, u32[]{:S(2)}, u32[]{:S(2)}) async-start(bf16[16,48,768]{2,1,0:T(8,128)(2,1)} %bitcast.95), calls=%async_computation | async-start | bytes 2359296 | tf_op jit(solution)/shard_map/all_to_all | solution.py:289
  13.6 24.9 %all-to-all-done.shares_ref = bf16[16,48,768]{2,1,0:T(8,128)(2,1)S(1)} async-done(((bf16[16,48,768]{2,1,0:T(8,128)(2,1)}), bf16[16,48,768]{2,1,0:T(8,128)(2,1)S(1)}, u32[]{:S(2)}, u32[]{:S(2)}) %all-to-all-start) | async-done | bytes 1179680 | tf_op jit(solution)/shard_map/all_to_all | solution.py:289
  40.7 7.7 %all-to-all-start.1 = ((bf16[16,2,48,768]{3,2,1,0:T(8,128)(2,1)}), bf16[16,2,48,768]{3,2,1,0:T(8,128)(2,1)}, u32[]{:S(2)}, u32[]{:S(2)}) async-start(bf16[16,2,48,768]{3,2,1,0:T(8,128)(2,1)} %copy-done.1), calls=%async_computation.1 | async-start | bytes 4718592 | tf_op jit(solution)/shard_map/all_to_all | solution.py:293
  48.4 1.5 copy.23
  51.0 2.4 %copy.20 = bf16[768,512]{0,1:T(8,128)(2,1)} copy(bf16[768,512]{1,0:T(8,128)(2,1)} %param.17) | data formatting | bytes 1572864 | tf_op args[7]
  53.4 2.3 %copy.21 = bf16[768,512]{0,1:T(8,128)(2,1)} copy(bf16[768,512]{1,0:T(8,128)(2,1)} %param.18) | data formatting | bytes 1572864 | tf_op args[8]
  57.2 1.7 convolution_convert_fusion.gt_in
  58.9 35.1 %all-to-all-done.1.token_in.token_ref = bf16[16,2,48,768]{3,2,1,0:T(8,128)(2,1)} async-done(((bf16[16,2,48,768]{3,2,1,0:T(8,128)(2,1)}), bf16[16,2,48,768]{3,2,1,0:T(8,128)(2,1)}, u32[]{:S(2)}, u32[]{:S(2)}) %all-to-all-start.1) | async-done | bytes 2359328 | tf_op jit(solution)/shard_map/all_to_all | solution.py:293
  94.1 28.9 %pair_pass.1 = (bf16[512,768]{1,0:T(8,128)(2,1)}, f32[8,48,1024]{2,1,0:T(8,128)}, f32[8,48,1024]{2,1,0:T(8,128)}, f32[8,48,1024]{2,1,0:T(8,128)}, f32[8,48,1024]{2,1,0:T(8,128)}) custom-call(s32[1]{0:T(128)} %bitcast.2.core_ref, bf16[16,2,48,768]{3,2,1,0:T(8,128)(2,1)} %all-to-all-done.1.token_in.token_ref, bf16[512,768]{1,0:T(8,128)(2,1)} %bitcast.91, ...), custom_call_target="tpu_custom_call" | custom-call | tf_op jit(solution)/shard_map/pair_pass/pallas_call | solution.py:194
  123.9 3.3 %collective-permute-done.1 = f32[8,48,1024]{2,1,0:T(8,128)} collective-permute-done((f32[8,48,1024]{2,1,0:T(8,128)}, f32[8,48,1024]{2,1,0:T(8,128)}, u32[]{:S(2)}, u32[]{:S(2)}) %collective-permute-start.1) | collective-permute-done | bytes 1572896 | tf_op jit(solution)/shard_map/ppermute | solution.py:221
  127.2 2.2 %add.66 = f32[8,48,1024]{2,1,0:T(8,128)S(1)} add(f32[8,48,1024]{2,1,0:T(8,128)} %get-tuple-element.11, f32[8,48,1024]{2,1,0:T(8,128)} %collective-permute-done.1) | non-fusion elementwise | flops 393216 | bytes 4718592 | tf_op jit(solution)/shard_map/add | solution.py:310
  129.6 7.3 %collective-permute-start.6 = (f16[2,2,48,1024]{3,2,1,0:T(8,128)(2,1)S(1)}, f16[2,2,48,1024]{3,2,1,0:T(8,128)(2,1)S(1)}, u32[]{:S(2)}, u32[]{:S(2)}) collective-permute-start(f16[2,2,48,1024]{3,2,1,0:T(8,128)(2,1)S(1)} %fusion.7), channel_id=1, source_target_pairs={{0,4},{1,5},{2,6},{3,7},{4,0},{5,1},{6,2},{7,3},{8,12},{9,13},{10,... | collective-permute-start | bytes 1179656 | tf_op jit(solution)/shard_map/ppermute | solution.py:221
  137.0 1.7 add.64
  138.9 3.0 %collective-permute-start.2 = (f16[2,2,48,1024]{3,2,1,0:T(8,128)(2,1)S(1)}, f16[2,2,48,1024]{3,2,1,0:T(8,128)(2,1)S(1)}, u32[]{:S(2)}, u32[]{:S(2)}) collective-permute-start(f16[2,2,48,1024]{3,2,1,0:T(8,128)(2,1)S(1)} %fusion.9), channel_id=1, source_target_pairs={{0,2},{1,3},{2,0},{3,1},{4,6},{5,7},{6,4},{7,5},{8,10},{9,11},{10,... | collective-permute-start | bytes 1179656 | tf_op jit(solution)/shard_map/ppermute | solution.py:221
  142.0 3.5 %attended_out.1 = bf16[768,768]{1,0:T(8,128)(2,1)} custom-call(bf16[16,2,48,768]{3,2,1,0:T(8,128)(2,1)} %all-to-all-done.1.token_in.token_ref, bf16[768,512]{1,0:T(8,128)(2,1)S(1)} %copy-done.2, bf16[512,768]{1,0:T(8,128)(2,1)S(1)} %copy-done.3), custom_call_target="tpu_custom_call" | custom-call | flops 603979776 | bytes 3538944 | tf_op jit(solution)/shard_map/attended_out/pallas_call | solution.py:236
  146.5 4.8 %collective-permute-done.3 = f32[1,1,1,1024]{3,2,1,0:T(1,128)S(1)} collective-permute-done((f32[1,1,1,1024]{3,2,1,0:T(1,128)S(1)}, f32[1,1,1,1024]{3,2,1,0:T(1,128)S(1)}, u32[]{:S(2)}, u32[]{:S(2)}) %collective-permute-start.3) | collective-permute-done | bytes 4128 | tf_op jit(solution)/shard_map/ppermute | solution.py:221
  151.6 1.8 %collective-permute-start.8 = (f16[2,48,1024]{2,1,0:T(8,128)(2,1)S(1)}, f16[2,48,1024]{2,1,0:T(8,128)(2,1)S(1)}, u32[]{:S(2)}, u32[]{:S(2)}) collective-permute-start(f16[2,48,1024]{2,1,0:T(8,128)(2,1)S(1)} %fusion.17), channel_id=1, source_target_pairs={{0,2},{1,3},{2,0},{3,1},{4,6},{5,7},{6,4},{7,5},{8,10},{9,11},{10,... | collective-permute-start | bytes 589832 | tf_op jit(solution)/shard_map/ppermute | solution.py:221
  154.0 1.7 %collective-permute-start.4 = (f16[2,48,1024]{2,1,0:T(8,128)(2,1)S(1)}, f16[2,48,1024]{2,1,0:T(8,128)(2,1)S(1)}, u32[]{:S(2)}, u32[]{:S(2)}) collective-permute-start(f16[2,48,1024]{2,1,0:T(8,128)(2,1)S(1)} %fusion.19), channel_id=1, source_target_pairs={{0,4},{1,5},{2,6},{3,7},{4,0},{5,1},{6,2},{7,3},{8,12},{9,13},{10,... | collective-permute-start | bytes 589832 | tf_op jit(solution)/shard_map/ppermute | solution.py:221
  156.1 2.0 %collective-permute-done.9 = f32[1,1,1024]{2,1,0:T(1,128)S(1)} collective-permute-done((f32[1,1,1024]{2,1,0:T(1,128)S(1)}, f32[1,1,1024]{2,1,0:T(1,128)S(1)}, u32[]{:S(2)}, u32[]{:S(2)}) %collective-permute-start.9) | collective-permute-done | bytes 4128 | tf_op jit(solution)/shard_map/ppermute | solution.py:221
  158.1 1.8 %collective-permute-done.5 = f32[1,1,1024]{2,1,0:T(1,128)S(1)} collective-permute-done((f32[1,1,1024]{2,1,0:T(1,128)S(1)}, f32[1,1,1024]{2,1,0:T(1,128)S(1)}, u32[]{:S(2)}, u32[]{:S(2)}) %collective-permute-start.5) | collective-permute-done | bytes 4128 | tf_op jit(solution)/shard_map/ppermute | solution.py:221
  160.1 3.0 %collective-permute-start.11 = (f32[1,2048]{1,0:T(1,128)S(1)}, f32[1,2048]{1,0:T(1,128)S(1)}, u32[]{:S(2)}, u32[]{:S(2)}) collective-permute-start(f32[1,2048]{1,0:T(1,128)S(1)} %bitcast.103), channel_id=1, source_target_pairs={{0,8},{1,9},{2,10},{3,11},{4,12},{5,13},{6,14},{7,15},{8,0},{9,1},... | collective-permute-start | bytes 24584 | tf_op jit(solution)/shard_map/ppermute | solution.py:221
  163.2 3.0 %collective-permute-done.11 = f32[1,2048]{1,0:T(1,128)S(1)} collective-permute-done((f32[1,2048]{1,0:T(1,128)S(1)}, f32[1,2048]{1,0:T(1,128)S(1)}, u32[]{:S(2)}, u32[]{:S(2)}) %collective-permute-start.11) | collective-permute-done | bytes 8224 | tf_op jit(solution)/shard_map/ppermute | solution.py:221
  166.3 6.0 %collective-permute-done.10 = f16[48,2048]{1,0:T(8,128)(2,1)S(1)} collective-permute-done((f16[48,2048]{1,0:T(8,128)(2,1)S(1)}, f16[48,2048]{1,0:T(8,128)(2,1)S(1)}, u32[]{:S(2)}, u32[]{:S(2)}) %collective-permute-start.10) | collective-permute-done | bytes 196640 | tf_op jit(solution)/shard_map/ppermute | solution.py:221
  (69 shorter events, 11.1 us)
Async XLA Ops:
  0.6 1.4 copy-start
  5.9 7.5 %copy-start.9 = (s32[16,2]{0,1:T(2,128)S(1)}, s32[16,2]{0,1:T(2,128)}, u32[]{:S(2)}) copy-start(s32[16,2]{0,1:T(2,128)} %param.12) | copy-start | bytes 388
  5.9 32.7 %copy-start.4 = (s32[16]{0:T(128)S(1)}, s32[16]{0:T(128)}, u32[]{:S(2)}) copy-start(s32[16]{0:T(128)} %owner_ref.1) | copy-start | bytes 196
  5.9 32.7 %all-to-all-start = ((bf16[16,48,768]{2,1,0:T(8,128)(2,1)}), bf16[16,48,768]{2,1,0:T(8,128)(2,1)S(1)}, u32[]{:S(2)}, u32[]{:S(2)}) async-start(bf16[16,48,768]{2,1,0:T(8,128)(2,1)} %bitcast.95), calls=%async_computation | async-start | bytes 2359296 | tf_op jit(solution)/shard_map/all_to_all | solution.py:289
  39.3 1.4 copy-start.1
  40.7 7.7 %copy-start.6 = (bf16[1,768,768]{2,1,0:T(8,128)(2,1)S(1)}, bf16[1,768,768]{2,1,0:T(8,128)(2,1)}, u32[]{:S(2)}) copy-start(bf16[1,768,768]{2,1,0:T(8,128)(2,1)} %param.14) | copy-start | bytes 3538948
  40.7 53.4 %all-to-all-start.1 = ((bf16[16,2,48,768]{3,2,1,0:T(8,128)(2,1)}), bf16[16,2,48,768]{3,2,1,0:T(8,128)(2,1)}, u32[]{:S(2)}, u32[]{:S(2)}) async-start(bf16[16,2,48,768]{3,2,1,0:T(8,128)(2,1)} %copy-done.1), calls=%async_computation.1 | async-start | bytes 4718592 | tf_op jit(solution)/shard_map/all_to_all | solution.py:293
  48.3 1.5 copy-start.7
  51.0 4.7 %copy-start.8 = (s32[1,12,12]{2,0,1:T(1,128)S(1)}, s32[1,12,12]{2,0,1:T(1,128)}, u32[]{:S(2)}) copy-start(s32[1,12,12]{2,0,1:T(1,128)} %param.13) | copy-start | bytes 1732
  51.0 6.2 %copy-start.2 = (bf16[768,512]{1,0:T(8,128)(2,1)S(1)}, bf16[768,512]{1,0:T(8,128)(2,1)}, u32[]{:S(2)}) copy-start(bf16[768,512]{1,0:T(8,128)(2,1)} %ow_ref.1) | copy-start | bytes 2359300
  123.0 4.2 %collective-permute-start.1 = (f32[8,48,1024]{2,1,0:T(8,128)}, f32[8,48,1024]{2,1,0:T(8,128)}, u32[]{:S(2)}, u32[]{:S(2)}) collective-permute-start(f32[8,48,1024]{2,1,0:T(8,128)} %get-tuple-element.12), channel_id=1, source_target_pairs={{0,1},{1,0},{2,3},{3,2},{4,5},{5,4},{6,7},{7,6},{8,9},{9,8},{10,11... | collective-permute-start | bytes 4718600 | tf_op jit(solution)/shard_map/ppermute | solution.py:221
  123.8 13.2 %collective-permute-start = (f32[8,48,1024]{2,1,0:T(8,128)}, f32[8,48,1024]{2,1,0:T(8,128)}, u32[]{:S(2)}, u32[]{:S(2)}) collective-permute-start(f32[8,48,1024]{2,1,0:T(8,128)} %get-tuple-element.10), channel_id=1, source_target_pairs={{0,1},{1,0},{2,3},{3,2},{4,5},{5,4},{6,7},{7,6},{8,9},{9,8},{10,11... | collective-permute-start | bytes 4718600 | tf_op jit(solution)/shard_map/ppermute | solution.py:221
  129.5 7.6 %copy-start.5 = (f32[8,48,1024]{2,1,0:T(8,128)S(1)}, f32[8,48,1024]{2,1,0:T(8,128)}, u32[]{:S(2)}) copy-start(f32[8,48,1024]{2,1,0:T(8,128)} %get-tuple-element.9) | copy-start | bytes 4718596
  129.6 21.7 %collective-permute-start.6 = (f16[2,2,48,1024]{3,2,1,0:T(8,128)(2,1)S(1)}, f16[2,2,48,1024]{3,2,1,0:T(8,128)(2,1)S(1)}, u32[]{:S(2)}, u32[]{:S(2)}) collective-permute-start(f16[2,2,48,1024]{3,2,1,0:T(8,128)(2,1)S(1)} %fusion.7), channel_id=1, source_target_pairs={{0,4},{1,5},{2,6},{3,7},{4,0},{5,1},{6,2},{7,3},{8,12},{9,13},{10,... | collective-permute-start | bytes 1179656 | tf_op jit(solution)/shard_map/ppermute | solution.py:221
  137.0 9.5 %collective-permute-start.7 = (f32[1,1,1,1024]{3,2,1,0:T(1,128)S(1)}, f32[1,1,1,1024]{3,2,1,0:T(1,128)S(1)}, u32[]{:S(2)}, u32[]{:S(2)}) collective-permute-start(f32[1,1,1,1024]{3,2,1,0:T(1,128)S(1)} %bitcast.104), channel_id=1, source_target_pairs={{0,4},{1,5},{2,6},{3,7},{4,0},{5,1},{6,2},{7,3},{8,12},{9,13},{10,... | collective-permute-start | bytes 12296 | tf_op jit(solution)/shard_map/ppermute | solution.py:221
  138.7 3.3 %copy-start.3 = (bf16[512,768]{1,0:T(8,128)(2,1)S(1)}, bf16[512,768]{1,0:T(8,128)(2,1)}, u32[]{:S(2)}) copy-start(bf16[512,768]{1,0:T(8,128)(2,1)} %get-tuple-element.13.ctx_ref) | copy-start | bytes 2359300
  138.9 14.8 %collective-permute-start.2 = (f16[2,2,48,1024]{3,2,1,0:T(8,128)(2,1)S(1)}, f16[2,2,48,1024]{3,2,1,0:T(8,128)(2,1)S(1)}, u32[]{:S(2)}, u32[]{:S(2)}) collective-permute-start(f16[2,2,48,1024]{3,2,1,0:T(8,128)(2,1)S(1)} %fusion.9), channel_id=1, source_target_pairs={{0,2},{1,3},{2,0},{3,1},{4,6},{5,7},{6,4},{7,5},{8,10},{9,11},{10,... | collective-permute-start | bytes 1179656 | tf_op jit(solution)/shard_map/ppermute | solution.py:221
  141.9 9.4 %collective-permute-start.3 = (f32[1,1,1,1024]{3,2,1,0:T(1,128)S(1)}, f32[1,1,1,1024]{3,2,1,0:T(1,128)S(1)}, u32[]{:S(2)}, u32[]{:S(2)}) collective-permute-start(f32[1,1,1,1024]{3,2,1,0:T(1,128)S(1)} %bitcast.106), channel_id=1, source_target_pairs={{0,2},{1,3},{2,0},{3,1},{4,6},{5,7},{6,4},{7,5},{8,10},{9,11},{10,... | collective-permute-start | bytes 12296 | tf_op jit(solution)/shard_map/ppermute | solution.py:221
  151.6 8.3 %collective-permute-start.8 = (f16[2,48,1024]{2,1,0:T(8,128)(2,1)S(1)}, f16[2,48,1024]{2,1,0:T(8,128)(2,1)S(1)}, u32[]{:S(2)}, u32[]{:S(2)}) collective-permute-start(f16[2,48,1024]{2,1,0:T(8,128)(2,1)S(1)} %fusion.17), channel_id=1, source_target_pairs={{0,2},{1,3},{2,0},{3,1},{4,6},{5,7},{6,4},{7,5},{8,10},{9,11},{10,... | collective-permute-start | bytes 589832 | tf_op jit(solution)/shard_map/ppermute | solution.py:221
  153.4 4.6 %collective-permute-start.9 = (f32[1,1,1024]{2,1,0:T(1,128)S(1)}, f32[1,1,1024]{2,1,0:T(1,128)S(1)}, u32[]{:S(2)}, u32[]{:S(2)}) collective-permute-start(f32[1,1,1024]{2,1,0:T(1,128)S(1)} %bitcast.105), channel_id=1, source_target_pairs={{0,2},{1,3},{2,0},{3,1},{4,6},{5,7},{6,4},{7,5},{8,10},{9,11},{10,... | collective-permute-start | bytes 12296 | tf_op jit(solution)/shard_map/ppermute | solution.py:221
  154.0 6.0 %collective-permute-start.4 = (f16[2,48,1024]{2,1,0:T(8,128)(2,1)S(1)}, f16[2,48,1024]{2,1,0:T(8,128)(2,1)S(1)}, u32[]{:S(2)}, u32[]{:S(2)}) collective-permute-start(f16[2,48,1024]{2,1,0:T(8,128)(2,1)S(1)} %fusion.19), channel_id=1, source_target_pairs={{0,4},{1,5},{2,6},{3,7},{4,0},{5,1},{6,2},{7,3},{8,12},{9,13},{10,... | collective-permute-start | bytes 589832 | tf_op jit(solution)/shard_map/ppermute | solution.py:221
  155.7 4.2 %collective-permute-start.5 = (f32[1,1,1024]{2,1,0:T(1,128)S(1)}, f32[1,1,1024]{2,1,0:T(1,128)S(1)}, u32[]{:S(2)}, u32[]{:S(2)}) collective-permute-start(f32[1,1,1024]{2,1,0:T(1,128)S(1)} %bitcast.107), channel_id=1, source_target_pairs={{0,4},{1,5},{2,6},{3,7},{4,0},{5,1},{6,2},{7,3},{8,12},{9,13},{10,... | collective-permute-start | bytes 12296 | tf_op jit(solution)/shard_map/ppermute | solution.py:221
  160.1 6.2 %collective-permute-start.11 = (f32[1,2048]{1,0:T(1,128)S(1)}, f32[1,2048]{1,0:T(1,128)S(1)}, u32[]{:S(2)}, u32[]{:S(2)}) collective-permute-start(f32[1,2048]{1,0:T(1,128)S(1)} %bitcast.103), channel_id=1, source_target_pairs={{0,8},{1,9},{2,10},{3,11},{4,12},{5,13},{6,14},{7,15},{8,0},{9,1},... | collective-permute-start | bytes 24584 | tf_op jit(solution)/shard_map/ppermute | solution.py:221
  163.1 9.1 %collective-permute-start.10 = (f16[48,2048]{1,0:T(8,128)(2,1)S(1)}, f16[48,2048]{1,0:T(8,128)(2,1)S(1)}, u32[]{:S(2)}, u32[]{:S(2)}) collective-permute-start(f16[48,2048]{1,0:T(8,128)(2,1)S(1)} %multiply_convert_fusion), channel_id=1, source_target_pairs={{0,8},{1,9},{2,10},{3,11},{4,12},{5,13},{6,14},{7,15},{8,0},{9,1},... | collective-permute-start | bytes 589832 | tf_op jit(solution)/shard_map/ppermute | solution.py:221

commit v5 on v4

--- a/solution.py
+++ b/solution.py
@@ -12,6 +12,7 @@
 BLOCK = 64
 CHUNK = 256
 GROUP = 512
+POWER_ROWS = 8
 DEAD = -1e30
 F32 = jnp.float32
 F16 = jnp.float16
@@ -125,15 +126,6 @@
         gq_ref[rows_of(h), :] = dot_nn(kt_ref[rows_of(h), :], grad_score).astype(BF16)
         return dot_nt(grad_score, qt_ref[rows_of(h), :]).astype(BF16)
 
-    def two_heads(i):
-        pair = (2 * i, 2 * i + 1)
-        scores = [scores_of(h) for h in pair]
-        grad_probs = [dot_nn(v_ref[h], gt_ref[rows_of(h), :] * scale) for h in pair]
-        probs = [softmax(each) for each in scores]
-        grad_values = [context_of(h, prob.astype(BF16)) for h, prob in zip(pair, probs)]
-        grad_scores = [grad_score_of(*each) for each in zip(probs, grad_probs)]
-        return [grads_of(h, each) for h, each in zip(pair, grad_scores)], grad_values
-
     mine = core_ref[0]
     blocks, rows_each, _ = keep_qk_ref.shape
     group = val_ref.shape[-1]
@@ -148,33 +140,37 @@
             out_sems.at[i, n, m],
         )
 
-    def one_group(i, carry):
-        grad_keys, grad_values = [], []
-        for j in range(per_group // 2):
-            more_keys, more_values = two_heads(i * (per_group // 2) + j)
-            grad_keys += more_keys
-            grad_values += more_values
-        rows = pl.ds(i * group, group)
-        for n, grad in (
-            (2, lambda: dot_nn(kn_ref[...], jnp.concatenate(grad_values, axis=1))),
-            (3, lambda: dot_nt(cot_ref[...], ctx_ref[rows, :])),
-            (1, lambda: dot_nn(kn_ref[...], jnp.concatenate(grad_keys, axis=1))),
-            (0, lambda: dot_nt(qn_ref[...], gq_ref[rows, :])),
-        ):
-            grad = grad()
-            if rows_each % 8:
-                for b in range(2 * blocks):
-                    block = grad[b * rows_each : (b + 1) * rows_each, :]
-                    val_ref[i, n, b // 2, b % 2] = block
-            else:
-                val_ref[i, n] = grad.reshape(blocks, 2, rows_each, group)
-            for m in range(2):
-                leaving(i, n, m).start()
-        return carry
-
-    groups = att // group
-    for i in range(groups):
-        one_group(i, 0)
+    def send_out(n, grad):
+        if rows_each % 8:
+            for b in range(2 * blocks):
+                block = grad[b * rows_each : (b + 1) * rows_each, :]
+                val_ref[0, n, b // 2, b % 2] = block
+        else:
+            val_ref[0, n] = grad.reshape(blocks, 2, rows_each, group)
+        for m in range(2):
+            leaving(0, n, m).start()
+
+    def products(some):
+        scores = [scores_of(h) for h in some]
+        return scores, [dot_nn(v_ref[h], gt_ref[rows_of(h), :] * scale) for h in some]
+
+    grad_keys, grad_values = [], []
+    together = [tuple(range(h, h + 1)) for h in range(0, heads, 1)]
+    ahead = products(together[0])
+    for n, some in enumerate(together):
+        scores, grad_probs = ahead
+        probs = [softmax(each) for each in scores]
+        if n + 1 < len(together):
+            ahead = products(together[n + 1])
+        grad_values += [context_of(h, prob.astype(BF16)) for h, prob in zip(some, probs)]
+        if n + 1 == len(together):
+            send_out(2, dot_nn(kn_ref[...], jnp.concatenate(grad_values, axis=1)))
+            send_out(3, dot_nt(cot_ref[...], ctx_ref[...]))
+        grad_scores = [grad_score_of(*each) for each in zip(probs, grad_probs)]
+        grad_keys += [grads_of(h, each) for h, each in zip(some, grad_scores)]
+    send_out(1, dot_nn(kn_ref[...], jnp.concatenate(grad_keys, axis=1)))
+    send_out(0, dot_nt(qn_ref[...], gq_ref[...]))
+    groups = 1
     for i in range(groups):
         for n in range(4):
             for m in range(2):
@@ -257,15 +253,19 @@
         keep = lax.dynamic_index_in_dim(part, mine, at, keepdims=False)
         top = jnp.max(jnp.abs(send), axis=tuple(range(send.ndim - 1)), keepdims=True)
         power = jnp.ceil(jnp.log2(jnp.maximum(top, 1e-30)))
-        cut.append((keep, power, (send * jnp.exp2(8.0 - power)).astype(F16)))
+        cols = send.shape[-1]
+        scaled = (send * jnp.exp2(8.0 - power)).astype(F16).reshape(-1, cols)
+        powers = jnp.broadcast_to(power.astype(F16).reshape(1, cols), (POWER_ROWS, cols))
+        cut.append((keep, jnp.concatenate([scaled, powers], axis=0)))
     return cut
 
 
 def join(cut, axis, bits):
     out = []
-    for (keep, power, scaled), bit in zip(cut, bits):
-        power = exchange(power, axis, bit)
-        out.append(keep + exchange(scaled, axis, bit).astype(F32) * jnp.exp2(power - 8.0))
+    for (keep, message), bit in zip(cut, bits):
+        got = exchange(message, axis, bit).astype(F32)
+        factor = jnp.exp2(got[-1:] - 8.0)
+        out.append(keep + (got[:-POWER_ROWS] * factor).reshape(keep.shape))
     return out
 
 
@@ -307,20 +307,26 @@
         core, arrived, query_weight.T, key_weight.T, value_weight.T, aug, hot,
         grad_context.T, cot.T, HEADS, share,
     )
-    parts = [keep_qk + exchange(send_qk, "img", 0), keep_vo + exchange(send_vo, "img", 0)]
-    dims = (2,) * (bits - 1) + parts[0].shape[1:]
-    parts = [part.reshape(dims) for part in parts]
-    left = [list(reversed(range(1, bits))) for _ in parts]
-    cut = halve(parts, "img", left, (1, 2))
-    context = lax.optimization_barrier((context, cut[0][2], cut[1][2]))[0]
-    parts = join(cut, "img", (1, 2))
+    batches = []
+    for keep, send in ((keep_vo, send_vo), (keep_qk, send_qk)):
+        part = keep + exchange(send, "img", 0)
+        half = part.shape[-1] // 2
+        dims = (2,) * (bits - 1) + (share, half)
+        batches.append([part[:, :, :half].reshape(dims), part[:, :, half:].reshape(dims)])
+    lefts = [[list(reversed(range(1, bits))) for _ in range(2)] for _ in batches]
+    cuts = [halve(parts, "img", left, (1, 2)) for parts, left in zip(batches, lefts)]
+    context = lax.optimization_barrier((context, cuts[1][0][1], cuts[1][1][1]))[0]
     attended = out_side(arrived, out_weight, context)
-    parts = join(halve(parts, "img", left, (2, 1)), "img", (2, 1))
-    parts = [jnp.concatenate(parts, axis=-1)]
-    left = left[:1]
-    for bit in range(3, bits):
-        parts = join(halve(parts, "img", left, (bit,)), "img", (bit,))
-    return (attended[None], parts[0] * (1.0 / devices_img))
+    sums = []
+    for cut, left in zip(cuts, lefts):
+        parts = join(cut, "img", (1, 2))
+        parts = join(halve(parts, "img", left, (2, 1)), "img", (2, 1))
+        parts = [jnp.concatenate(parts, axis=-1)]
+        for bit in range(3, bits):
+            parts = join(halve(parts, "img", left[:1], (bit,)), "img", (bit,))
+        sums.append(parts[0])
+    summed = jnp.concatenate([sums[1], sums[0]], axis=-1)
+    return (attended[None], summed * (1.0 / devices_img))
 
 
 def solution(mesh):

time: 174 us -> 167 us (0.960)
  waiting for transfers between devices: 81.9 us -> 71.7 us
  starting transfers between devices: 33.9 us -> 36.9 us
    ppermute x12, waiting for transfers between devices: 21.9 us -> 11.6 us  [exchange(): return lax.ppermute(array, axis, [(d, d ^ 1 << bit) for d in range(size)])]
    ppermute x12, starting transfers between devices: 18.7 us -> 21.7 us  [exchange(): return lax.ppermute(array, axis, [(d, d ^ 1 << bit) for d in range(size)])]
    add x6 -> x12, other arithmetic: 4.3 us -> 2.98 us  [the longest x2 2.49 us: per_device(): part = keep + exchange(send, 'img', 0)]
  transfers between devices with their start and end apart: 14 -> 14, of which waited for: 9 -> 8; matrix products, arithmetic and copies ran while one was open for 9% -> 10% of each run, Pallas kernels for 2% -> 2%
where the time goes in v5:
time: 167 us; the launch traced here: 166 us
  waiting for transfers between devices  71.7 us (43%)
  starting transfers between devices  36.9 us (22%)
  Pallas kernels  32.8 us (20%)
  local copies, waits for them, and re-layouts  11.8 us (7%)
  other arithmetic  6.28 us (4%)
  matrix products  5.57 us (3%)
    all_to_all x1, waiting for transfers between devices, per_device(): arrived = lax.all_to_all(picked, 'img', 0, 0, tiled=True)  35.1 us
    pallas_call x1, Pallas kernels, pair_side(): pl.pallas_call(functools.partial(pair_body, heads), out_shape=(jax.ShapeD...  28.5 us
    all_to_all x1, waiting for transfers between devices, per_device(): lax.all_to_all(embedded.reshape(devices_img, share, length), 'img', 0, 0,...  24.9 us
    ppermute x12, starting transfers between devices, exchange(): return lax.ppermute(array, axis, [(d, d ^ 1 << bit) for d in range(size)])  21.7 us
    ppermute x12, waiting for transfers between devices, exchange(): return lax.ppermute(array, axis, [(d, d ^ 1 << bit) for d in range(size)])  11.6 us
    unnamed x25, local copies, waits for them, and re-layouts  10.2 us
    all_to_all x1, starting transfers between devices, per_device(): arrived = lax.all_to_all(picked, 'img', 0, 0, tiled=True)  7.66 us
    all_to_all x1, starting transfers between devices, per_device(): lax.all_to_all(embedded.reshape(devices_img, share, length), 'img', 0, 0,...  7.52 us
  transfers between devices with their start and end apart: 14, of which 8 were waited for; matrix products, arithmetic and copies ran while one was open for 10% of the time, Pallas kernels for 2%

profile of v5, /device:TPU:0, one launch (start us, length us, event | category | flops | bytes accessed | tf_op | source)
XLA Modules:
  0.0 166.3 jit_solution(17650370909686774578)
XLA Ops:
  0.6 1.4 copy-done
  2.0 3.9 %fusion.2 = bf16[768,768]{1,0:T(8,128)(2,1)} fusion(bf16[1024,768]{1,0:T(8,128)(2,1)S(1)} %copy-done, bf16[1,768,1024]{2,1,0:T(8,128)(2,1)} %param.10), kind=kOutput, calls=%fused_computation.2 | convolution fusion | flops 1208549376 | bytes 4325376 | tf_op jit(solution)/shard_map/dot_general | solution.py:286
  5.9 7.5 %all-to-all-start = ((bf16[16,48,768]{2,1,0:T(8,128)(2,1)}), bf16[16,48,768]{2,1,0:T(8,128)(2,1)S(1)}, u32[]{:S(2)}, u32[]{:S(2)}) async-start(bf16[16,48,768]{2,1,0:T(8,128)(2,1)} %bitcast.131), calls=%async_computation | async-start | bytes 2359296 | tf_op jit(solution)/shard_map/all_to_all | solution.py:289
  13.6 24.9 %all-to-all-done.shares_ref = bf16[16,48,768]{2,1,0:T(8,128)(2,1)S(1)} async-done(((bf16[16,48,768]{2,1,0:T(8,128)(2,1)}), bf16[16,48,768]{2,1,0:T(8,128)(2,1)S(1)}, u32[]{:S(2)}, u32[]{:S(2)}) %all-to-all-start) | async-done | bytes 1179680 | tf_op jit(solution)/shard_map/all_to_all | solution.py:289
  39.3 1.4 copy-done.1
  40.7 7.7 %all-to-all-start.1 = ((bf16[16,2,48,768]{3,2,1,0:T(8,128)(2,1)}), bf16[16,2,48,768]{3,2,1,0:T(8,128)(2,1)}, u32[]{:S(2)}, u32[]{:S(2)}) async-start(bf16[16,2,48,768]{3,2,1,0:T(8,128)(2,1)} %copy-done.1), calls=%async_computation.1 | async-start | bytes 4718592 | tf_op jit(solution)/shard_map/all_to_all | solution.py:293
  48.4 1.5 copy.23
  49.8 1.2 copy.19
  51.0 2.4 %copy.20 = bf16[768,512]{0,1:T(8,128)(2,1)} copy(bf16[768,512]{1,0:T(8,128)(2,1)} %param.17) | data formatting | bytes 1572864 | tf_op args[7]
  53.4 2.3 %copy.21 = bf16[768,512]{0,1:T(8,128)(2,1)} copy(bf16[768,512]{1,0:T(8,128)(2,1)} %param.18) | data formatting | bytes 1572864 | tf_op args[8]
  57.2 1.7 %convolution_convert_fusion.gt_in = bf16[512,768]{1,0:T(8,128)(2,1)} fusion(bf16[768,512]{1,0:T(8,128)(2,1)S(1)} %copy-done.2, bf16[1,768,768]{2,1,0:T(8,128)(2,1)S(1)} %copy-done.6), kind=kOutput, calls=%fused_computation.3 | convolution fusion | flops 604372992 | bytes 2752512 | tf_op jit(solution)/shard_map/dot_general | solution.py:303
  58.9 35.1 %all-to-all-done.1.token_in.token_ref = bf16[16,2,48,768]{3,2,1,0:T(8,128)(2,1)} async-done(((bf16[16,2,48,768]{3,2,1,0:T(8,128)(2,1)}), bf16[16,2,48,768]{3,2,1,0:T(8,128)(2,1)}, u32[]{:S(2)}, u32[]{:S(2)}) %all-to-all-start.1) | async-done | bytes 2359328 | tf_op jit(solution)/shard_map/all_to_all | solution.py:293
  94.1 28.5 %pair_pass.1 = (bf16[512,768]{1,0:T(8,128)(2,1)}, f32[8,48,1024]{2,1,0:T(8,128)}, f32[8,48,1024]{2,1,0:T(8,128)}, f32[8,48,1024]{2,1,0:T(8,128)}, f32[8,48,1024]{2,1,0:T(8,128)}) custom-call(s32[1]{0:T(128)} %bitcast.2.core_ref, bf16[16,2,48,768]{3,2,1,0:T(8,128)(2,1)} %all-to-all-done.1.token_in.token_ref, bf16[512,768]{1,0:T(8,128)(2,1)} %bitcast.123, ...), custom_call_target="tpu_custom_call" | custom-call | tf_op jit(solution)/shard_map/pair_pass/pallas_call | solution.py:190
  123.5 4.6 %collective-permute-done = f32[8,48,1024]{2,1,0:T(8,128)} collective-permute-done((f32[8,48,1024]{2,1,0:T(8,128)}, f32[8,48,1024]{2,1,0:T(8,128)}, u32[]{:S(2)}, u32[]{:S(2)}) %collective-permute-start) | collective-permute-done | bytes 1572896 | tf_op jit(solution)/shard_map/ppermute | solution.py:217
  128.2 2.1 %add.94 = f32[8,48,1024]{2,1,0:T(8,128)S(1)} add(f32[8,48,1024]{2,1,0:T(8,128)} %get-tuple-element.9, f32[8,48,1024]{2,1,0:T(8,128)} %collective-permute-done) | non-fusion elementwise | flops 393216 | bytes 4718592 | tf_op jit(solution)/shard_map/add | solution.py:312
  130.7 7.3 %collective-permute-start.3 = (f16[200,512]{1,0:T(8,128)(2,1)S(1)}, f16[200,512]{1,0:T(8,128)(2,1)S(1)}, u32[]{:S(2)}, u32[]{:S(2)}) collective-permute-start(f16[200,512]{1,0:T(8,128)(2,1)S(1)} %pad_maximum_fusion.1), channel_id=1, source_target_pairs={{0,4},{1,5},{2,6},{3,7},{4,0},{5,1},{6,2},{7,3},{8,12},{9,13},{10,... | collective-permute-start | bytes 614408 | tf_op jit(solution)/shard_map/ppermute | solution.py:217
  138.2 1.7 %collective-permute-start.1 = (f16[200,512]{1,0:T(8,128)(2,1)S(1)}, f16[200,512]{1,0:T(8,128)(2,1)S(1)}, u32[]{:S(2)}, u32[]{:S(2)}) collective-permute-start(f16[200,512]{1,0:T(8,128)(2,1)S(1)} %pad_maximum_fusion), channel_id=1, source_target_pairs={{0,2},{1,3},{2,0},{3,1},{4,6},{5,7},{6,4},{7,5},{8,10},{9,11},{10,... | collective-permute-start | bytes 614408 | tf_op jit(solution)/shard_map/ppermute | solution.py:217
  142.1 3.5 %attended_out.1 = bf16[768,768]{1,0:T(8,128)(2,1)} custom-call(bf16[16,2,48,768]{3,2,1,0:T(8,128)(2,1)} %all-to-all-done.1.token_in.token_ref, bf16[768,512]{1,0:T(8,128)(2,1)S(1)} %copy-done.2, bf16[512,768]{1,0:T(8,128)(2,1)S(1)} %copy-done.3), custom_call_target="tpu_custom_call" | custom-call | flops 603979776 | bytes 3538944 | tf_op jit(solution)/shard_map/attended_out/pallas_call | solution.py:232
  147.5 2.1 %collective-permute-start.2 = (f16[104,512]{1,0:T(8,128)(2,1)S(1)}, f16[104,512]{1,0:T(8,128)(2,1)S(1)}, u32[]{:S(2)}, u32[]{:S(2)}) collective-permute-start(f16[104,512]{1,0:T(8,128)(2,1)S(1)} %pad_maximum_fusion.6), channel_id=1, source_target_pairs={{0,4},{1,5},{2,6},{3,7},{4,0},{5,1},{6,2},{7,3},{8,12},{9,13},{10,... | collective-permute-start | bytes 319496 | tf_op jit(solution)/shard_map/ppermute | solution.py:217
  150.9 1.2 collective-permute-start.8
  152.8 3.4 %collective-permute-start.5 = (f16[56,1024]{1,0:T(8,128)(2,1)S(1)}, f16[56,1024]{1,0:T(8,128)(2,1)S(1)}, u32[]{:S(2)}, u32[]{:S(2)}) collective-permute-start(f16[56,1024]{1,0:T(8,128)(2,1)S(1)} %pad_maximum_fusion.4), channel_id=1, source_target_pairs={{0,8},{1,9},{2,10},{3,11},{4,12},{5,13},{6,14},{7,15},{8,0},{9,1},... | collective-permute-start | bytes 344072 | tf_op jit(solution)/shard_map/ppermute | solution.py:217
  157.1 2.4 %collective-permute-start.11 = (f16[56,1024]{1,0:T(8,128)(2,1)S(1)}, f16[56,1024]{1,0:T(8,128)(2,1)S(1)}, u32[]{:S(2)}, u32[]{:S(2)}) collective-permute-start(f16[56,1024]{1,0:T(8,128)(2,1)S(1)} %pad_maximum_fusion.5), channel_id=1, source_target_pairs={{0,8},{1,9},{2,10},{3,11},{4,12},{5,13},{6,14},{7,15},{8,0},{9,1},... | collective-permute-start | bytes 344072 | tf_op jit(solution)/shard_map/ppermute | solution.py:217
  159.5 4.6 %collective-permute-done.5 = f16[56,1024]{1,0:T(8,128)(2,1)S(1)} collective-permute-done((f16[56,1024]{1,0:T(8,128)(2,1)S(1)}, f16[56,1024]{1,0:T(8,128)(2,1)S(1)}, u32[]{:S(2)}, u32[]{:S(2)}) %collective-permute-start.5) | collective-permute-done | bytes 114720 | tf_op jit(solution)/shard_map/ppermute | solution.py:217
  164.2 1.2 collective-permute-done.11
  (135 shorter events, 11.3 us)
Async XLA Ops:
  0.6 1.4 copy-start
  5.9 7.5 %copy-start.9 = (s32[16,2]{0,1:T(2,128)S(1)}, s32[16,2]{0,1:T(2,128)}, u32[]{:S(2)}) copy-start(s32[16,2]{0,1:T(2,128)} %param.12) | copy-start | bytes 388
  5.9 32.7 %copy-start.4 = (s32[16]{0:T(128)S(1)}, s32[16]{0:T(128)}, u32[]{:S(2)}) copy-start(s32[16]{0:T(128)} %owner_ref.1) | copy-start | bytes 196
  5.9 32.7 %all-to-all-start = ((bf16[16,48,768]{2,1,0:T(8,128)(2,1)}), bf16[16,48,768]{2,1,0:T(8,128)(2,1)S(1)}, u32[]{:S(2)}, u32[]{:S(2)}) async-start(bf16[16,48,768]{2,1,0:T(8,128)(2,1)} %bitcast.131), calls=%async_computation | async-start | bytes 2359296 | tf_op jit(solution)/shard_map/all_to_all | solution.py:289
  39.3 1.4 copy-start.1
  40.7 7.7 %copy-start.6 = (bf16[1,768,768]{2,1,0:T(8,128)(2,1)S(1)}, bf16[1,768,768]{2,1,0:T(8,128)(2,1)}, u32[]{:S(2)}) copy-start(bf16[1,768,768]{2,1,0:T(8,128)(2,1)} %param.14) | copy-start | bytes 3538948
  40.7 53.4 %all-to-all-start.1 = ((bf16[16,2,48,768]{3,2,1,0:T(8,128)(2,1)}), bf16[16,2,48,768]{3,2,1,0:T(8,128)(2,1)}, u32[]{:S(2)}, u32[]{:S(2)}) async-start(bf16[16,2,48,768]{3,2,1,0:T(8,128)(2,1)} %copy-done.1), calls=%async_computation.1 | async-start | bytes 4718592 | tf_op jit(solution)/shard_map/all_to_all | solution.py:293
  48.3 1.5 copy-start.7
  51.0 4.6 %copy-start.8 = (s32[1,12,12]{2,0,1:T(1,128)S(1)}, s32[1,12,12]{2,0,1:T(1,128)}, u32[]{:S(2)}) copy-start(s32[1,12,12]{2,0,1:T(1,128)} %param.13) | copy-start | bytes 1732
  51.0 6.2 %copy-start.2 = (bf16[768,512]{1,0:T(8,128)(2,1)S(1)}, bf16[768,512]{1,0:T(8,128)(2,1)}, u32[]{:S(2)}) copy-start(bf16[768,512]{1,0:T(8,128)(2,1)} %ow_ref.1) | copy-start | bytes 2359300
  122.6 5.6 %collective-permute-start = (f32[8,48,1024]{2,1,0:T(8,128)}, f32[8,48,1024]{2,1,0:T(8,128)}, u32[]{:S(2)}, u32[]{:S(2)}) collective-permute-start(f32[8,48,1024]{2,1,0:T(8,128)} %get-tuple-element.10), channel_id=1, source_target_pairs={{0,1},{1,0},{2,3},{3,2},{4,5},{5,4},{6,7},{7,6},{8,9},{9,8},{10,11... | collective-permute-start | bytes 4718600 | tf_op jit(solution)/shard_map/ppermute | solution.py:217
  123.4 16.4 %collective-permute-start.6 = (f32[8,48,1024]{2,1,0:T(8,128)}, f32[8,48,1024]{2,1,0:T(8,128)S(1)}, u32[]{:S(2)}, u32[]{:S(2)}) collective-permute-start(f32[8,48,1024]{2,1,0:T(8,128)} %get-tuple-element.13), channel_id=1, source_target_pairs={{0,1},{1,0},{2,3},{3,2},{4,5},{5,4},{6,7},{7,6},{8,9},{9,8},{10,11... | collective-permute-start | bytes 4718600 | tf_op jit(solution)/shard_map/ppermute | solution.py:217
  130.5 9.3 %copy-start.5 = (f32[8,48,1024]{2,1,0:T(8,128)S(1)}, f32[8,48,1024]{2,1,0:T(8,128)}, u32[]{:S(2)}) copy-start(f32[8,48,1024]{2,1,0:T(8,128)} %get-tuple-element.12) | copy-start | bytes 4718596
  130.7 15.0 %collective-permute-start.3 = (f16[200,512]{1,0:T(8,128)(2,1)S(1)}, f16[200,512]{1,0:T(8,128)(2,1)S(1)}, u32[]{:S(2)}, u32[]{:S(2)}) collective-permute-start(f16[200,512]{1,0:T(8,128)(2,1)S(1)} %pad_maximum_fusion.1), channel_id=1, source_target_pairs={{0,4},{1,5},{2,6},{3,7},{4,0},{5,1},{6,2},{7,3},{8,12},{9,13},{10,... | collective-permute-start | bytes 614408 | tf_op jit(solution)/shard_map/ppermute | solution.py:217
  138.2 9.0 %collective-permute-start.1 = (f16[200,512]{1,0:T(8,128)(2,1)S(1)}, f16[200,512]{1,0:T(8,128)(2,1)S(1)}, u32[]{:S(2)}, u32[]{:S(2)}) collective-permute-start(f16[200,512]{1,0:T(8,128)(2,1)S(1)} %pad_maximum_fusion), channel_id=1, source_target_pairs={{0,2},{1,3},{2,0},{3,1},{4,6},{5,7},{6,4},{7,5},{8,10},{9,11},{10,... | collective-permute-start | bytes 614408 | tf_op jit(solution)/shard_map/ppermute | solution.py:217
  140.7 1.4 copy-start.3
  140.8 8.7 %collective-permute-start.9 = (f16[200,512]{1,0:T(8,128)(2,1)S(1)}, f16[200,512]{1,0:T(8,128)(2,1)S(1)}, u32[]{:S(2)}, u32[]{:S(2)}) collective-permute-start(f16[200,512]{1,0:T(8,128)(2,1)S(1)} %pad_maximum_fusion.3), channel_id=1, source_target_pairs={{0,4},{1,5},{2,6},{3,7},{4,0},{5,1},{6,2},{7,3},{8,12},{9,13},{10,... | collective-permute-start | bytes 614408 | tf_op jit(solution)/shard_map/ppermute | solution.py:217
  141.1 9.5 %collective-permute-start.7 = (f16[200,512]{1,0:T(8,128)(2,1)S(1)}, f16[200,512]{1,0:T(8,128)(2,1)S(1)}, u32[]{:S(2)}, u32[]{:S(2)}) collective-permute-start(f16[200,512]{1,0:T(8,128)(2,1)S(1)} %pad_maximum_fusion.2), channel_id=1, source_target_pairs={{0,2},{1,3},{2,0},{3,1},{4,6},{5,7},{6,4},{7,5},{8,10},{9,11},{10,... | collective-permute-start | bytes 614408 | tf_op jit(solution)/shard_map/ppermute | solution.py:217
  146.0 6.5 %collective-permute-start.4 = (f16[104,512]{1,0:T(8,128)(2,1)S(1)}, f16[104,512]{1,0:T(8,128)(2,1)S(1)}, u32[]{:S(2)}, u32[]{:S(2)}) collective-permute-start(f16[104,512]{1,0:T(8,128)(2,1)S(1)} %pad_maximum_fusion.7), channel_id=1, source_target_pairs={{0,2},{1,3},{2,0},{3,1},{4,6},{5,7},{6,4},{7,5},{8,10},{9,11},{10,... | collective-permute-start | bytes 319496 | tf_op jit(solution)/shard_map/ppermute | solution.py:217
  147.5 5.1 %collective-permute-start.2 = (f16[104,512]{1,0:T(8,128)(2,1)S(1)}, f16[104,512]{1,0:T(8,128)(2,1)S(1)}, u32[]{:S(2)}, u32[]{:S(2)}) collective-permute-start(f16[104,512]{1,0:T(8,128)(2,1)S(1)} %pad_maximum_fusion.6), channel_id=1, source_target_pairs={{0,4},{1,5},{2,6},{3,7},{4,0},{5,1},{6,2},{7,3},{8,12},{9,13},{10,... | collective-permute-start | bytes 319496 | tf_op jit(solution)/shard_map/ppermute | solution.py:217
  149.9 6.4 %collective-permute-start.10 = (f16[104,512]{1,0:T(8,128)(2,1)S(1)}, f16[104,512]{1,0:T(8,128)(2,1)S(1)}, u32[]{:S(2)}, u32[]{:S(2)}) collective-permute-start(f16[104,512]{1,0:T(8,128)(2,1)S(1)} %pad_maximum_fusion.9), channel_id=1, source_target_pairs={{0,2},{1,3},{2,0},{3,1},{4,6},{5,7},{6,4},{7,5},{8,10},{9,11},{10,... | collective-permute-start | bytes 319496 | tf_op jit(solution)/shard_map/ppermute | solution.py:217
  150.9 6.0 %collective-permute-start.8 = (f16[104,512]{1,0:T(8,128)(2,1)S(1)}, f16[104,512]{1,0:T(8,128)(2,1)S(1)}, u32[]{:S(2)}, u32[]{:S(2)}) collective-permute-start(f16[104,512]{1,0:T(8,128)(2,1)S(1)} %pad_maximum_fusion.8), channel_id=1, source_target_pairs={{0,4},{1,5},{2,6},{3,7},{4,0},{5,1},{6,2},{7,3},{8,12},{9,13},{10,... | collective-permute-start | bytes 319496 | tf_op jit(solution)/shard_map/ppermute | solution.py:217
  152.8 11.3 %collective-permute-start.5 = (f16[56,1024]{1,0:T(8,128)(2,1)S(1)}, f16[56,1024]{1,0:T(8,128)(2,1)S(1)}, u32[]{:S(2)}, u32[]{:S(2)}) collective-permute-start(f16[56,1024]{1,0:T(8,128)(2,1)S(1)} %pad_maximum_fusion.4), channel_id=1, source_target_pairs={{0,8},{1,9},{2,10},{3,11},{4,12},{5,13},{6,14},{7,15},{8,0},{9,1},... | collective-permute-start | bytes 344072 | tf_op jit(solution)/shard_map/ppermute | solution.py:217
  157.1 8.2 %collective-permute-start.11 = (f16[56,1024]{1,0:T(8,128)(2,1)S(1)}, f16[56,1024]{1,0:T(8,128)(2,1)S(1)}, u32[]{:S(2)}, u32[]{:S(2)}) collective-permute-start(f16[56,1024]{1,0:T(8,128)(2,1)S(1)} %pad_maximum_fusion.5), channel_id=1, source_target_pairs={{0,8},{1,9},{2,10},{3,11},{4,12},{5,13},{6,14},{7,15},{8,0},{9,1},... | collective-permute-start | bytes 344072 | tf_op jit(solution)/shard_map/ppermute | solution.py:217

commit v6 on v5

--- a/solution.py
+++ b/solution.py
@@ -315,16 +315,17 @@
         batches.append([part[:, :, :half].reshape(dims), part[:, :, half:].reshape(dims)])
     lefts = [[list(reversed(range(1, bits))) for _ in range(2)] for _ in batches]
     cuts = [halve(parts, "img", left, (1, 2)) for parts, left in zip(batches, lefts)]
-    context = lax.optimization_barrier((context, cuts[1][0][1], cuts[1][1][1]))[0]
-    attended = out_side(arrived, out_weight, context)
     sums = []
     for cut, left in zip(cuts, lefts):
         parts = join(cut, "img", (1, 2))
-        parts = join(halve(parts, "img", left, (2, 1)), "img", (2, 1))
+        second = halve(parts, "img", left, (2, 1))
+        parts = join(second, "img", (2, 1))
         parts = [jnp.concatenate(parts, axis=-1)]
         for bit in range(3, bits):
             parts = join(halve(parts, "img", left[:1], (bit,)), "img", (bit,))
         sums.append(parts[0])
+    context = lax.optimization_barrier((context, second[0][1], second[1][1]))[0]
+    attended = out_side(arrived, out_weight, context)
     summed = jnp.concatenate([sums[1], sums[0]], axis=-1)
     return (attended[None], summed * (1.0 / devices_img))
 

time: 167 us -> 170 us (1.018)
  waiting for transfers between devices: 71.7 us -> 74.7 us
    ppermute x12, waiting for transfers between devices: 11.6 us -> 14.6 us  [exchange(): return lax.ppermute(array, axis, [(d, d ^ 1 << bit) for d in range(size)])]
  transfers between devices with their start and end apart: 14 -> 14, of which waited for: 8 -> 8; matrix products, arithmetic and copies ran while one was open for 10% -> 9% of each run, Pallas kernels for 2% -> 2%
where the time goes in v6:
time: 170 us; the launch traced here: 169 us
  waiting for transfers between devices  74.7 us (44%)
  starting transfers between devices  36.9 us (22%)
  Pallas kernels  32.8 us (19%)
  local copies, waits for them, and re-layouts  11.8 us (7%)
  other arithmetic  6.29 us (4%)
  matrix products  5.57 us (3%)
    all_to_all x1, waiting for transfers between devices, per_device(): arrived = lax.all_to_all(picked, 'img', 0, 0, tiled=True)  35.1 us
    pallas_call x1, Pallas kernels, pair_side(): pl.pallas_call(functools.partial(pair_body, heads), out_shape=(jax.ShapeD...  28.5 us
    all_to_all x1, waiting for transfers between devices, per_device(): lax.all_to_all(embedded.reshape(devices_img, share, length), 'img', 0, 0,...  24.9 us
    ppermute x12, starting transfers between devices, exchange(): return lax.ppermute(array, axis, [(d, d ^ 1 << bit) for d in range(size)])  21.7 us
    ppermute x12, waiting for transfers between devices, exchange(): return lax.ppermute(array, axis, [(d, d ^ 1 << bit) for d in range(size)])  14.6 us
    unnamed x25, local copies, waits for them, and re-layouts  10.2 us
    all_to_all x1, starting transfers between devices, per_device(): arrived = lax.all_to_all(picked, 'img', 0, 0, tiled=True)  7.66 us
    all_to_all x1, starting transfers between devices, per_device(): lax.all_to_all(embedded.reshape(devices_img, share, length), 'img', 0, 0,...  7.52 us
  transfers between devices with their start and end apart: 14, of which 8 were waited for; matrix products, arithmetic and copies ran while one was open for 9% of the time, Pallas kernels for 2%

profile of v6, /device:TPU:0, one launch (start us, length us, event | category | flops | bytes accessed | tf_op | source)
XLA Modules:
  0.0 169.3 jit_solution(11708311698268872961)
XLA Ops:
  0.6 1.4 copy-done
  2.0 3.9 %fusion.2 = bf16[768,768]{1,0:T(8,128)(2,1)} fusion(bf16[1024,768]{1,0:T(8,128)(2,1)S(1)} %copy-done, bf16[1,768,1024]{2,1,0:T(8,128)(2,1)} %param.10), kind=kOutput, calls=%fused_computation.2 | convolution fusion | flops 1208549376 | bytes 4325376 | tf_op jit(solution)/shard_map/dot_general | solution.py:286
  5.9 7.5 %all-to-all-start = ((bf16[16,48,768]{2,1,0:T(8,128)(2,1)}), bf16[16,48,768]{2,1,0:T(8,128)(2,1)S(1)}, u32[]{:S(2)}, u32[]{:S(2)}) async-start(bf16[16,48,768]{2,1,0:T(8,128)(2,1)} %bitcast.131), calls=%async_computation | async-start | bytes 2359296 | tf_op jit(solution)/shard_map/all_to_all | solution.py:289
  13.6 24.9 %all-to-all-done.shares_ref = bf16[16,48,768]{2,1,0:T(8,128)(2,1)S(1)} async-done(((bf16[16,48,768]{2,1,0:T(8,128)(2,1)}), bf16[16,48,768]{2,1,0:T(8,128)(2,1)S(1)}, u32[]{:S(2)}, u32[]{:S(2)}) %all-to-all-start) | async-done | bytes 1179680 | tf_op jit(solution)/shard_map/all_to_all | solution.py:289
  39.3 1.4 copy-done.1
  40.7 7.7 %all-to-all-start.1 = ((bf16[16,2,48,768]{3,2,1,0:T(8,128)(2,1)}), bf16[16,2,48,768]{3,2,1,0:T(8,128)(2,1)}, u32[]{:S(2)}, u32[]{:S(2)}) async-start(bf16[16,2,48,768]{3,2,1,0:T(8,128)(2,1)} %copy-done.1), calls=%async_computation.1 | async-start | bytes 4718592 | tf_op jit(solution)/shard_map/all_to_all | solution.py:293
  48.4 1.5 copy.23
  51.0 2.4 %copy.20 = bf16[768,512]{0,1:T(8,128)(2,1)} copy(bf16[768,512]{1,0:T(8,128)(2,1)} %param.17) | data formatting | bytes 1572864 | tf_op args[7]
  53.4 2.3 %copy.21 = bf16[768,512]{0,1:T(8,128)(2,1)} copy(bf16[768,512]{1,0:T(8,128)(2,1)} %param.18) | data formatting | bytes 1572864 | tf_op args[8]
  57.2 1.7 %convolution_convert_fusion.gt_in = bf16[512,768]{1,0:T(8,128)(2,1)} fusion(bf16[768,512]{1,0:T(8,128)(2,1)S(1)} %copy-done.2, bf16[1,768,768]{2,1,0:T(8,128)(2,1)S(1)} %copy-done.6), kind=kOutput, calls=%fused_computation.3 | convolution fusion | flops 604372992 | bytes 2752512 | tf_op jit(solution)/shard_map/dot_general | solution.py:303
  58.9 35.1 %all-to-all-done.1.token_in.token_ref = bf16[16,2,48,768]{3,2,1,0:T(8,128)(2,1)} async-done(((bf16[16,2,48,768]{3,2,1,0:T(8,128)(2,1)}), bf16[16,2,48,768]{3,2,1,0:T(8,128)(2,1)}, u32[]{:S(2)}, u32[]{:S(2)}) %all-to-all-start.1) | async-done | bytes 2359328 | tf_op jit(solution)/shard_map/all_to_all | solution.py:293
  94.1 28.5 %pair_pass.1 = (bf16[512,768]{1,0:T(8,128)(2,1)}, f32[8,48,1024]{2,1,0:T(8,128)}, f32[8,48,1024]{2,1,0:T(8,128)}, f32[8,48,1024]{2,1,0:T(8,128)}, f32[8,48,1024]{2,1,0:T(8,128)}) custom-call(s32[1]{0:T(128)} %bitcast.2.core_ref, bf16[16,2,48,768]{3,2,1,0:T(8,128)(2,1)} %all-to-all-done.1.token_in.token_ref, bf16[512,768]{1,0:T(8,128)(2,1)} %bitcast.123, ...), custom_call_target="tpu_custom_call" | custom-call | tf_op jit(solution)/shard_map/pair_pass/pallas_call | solution.py:190
  123.5 4.6 %collective-permute-done = f32[8,48,1024]{2,1,0:T(8,128)} collective-permute-done((f32[8,48,1024]{2,1,0:T(8,128)}, f32[8,48,1024]{2,1,0:T(8,128)}, u32[]{:S(2)}, u32[]{:S(2)}) %collective-permute-start) | collective-permute-done | bytes 1572896 | tf_op jit(solution)/shard_map/ppermute | solution.py:217
  128.2 2.1 %add.94 = f32[8,48,1024]{2,1,0:T(8,128)S(1)} add(f32[8,48,1024]{2,1,0:T(8,128)} %get-tuple-element.9, f32[8,48,1024]{2,1,0:T(8,128)} %collective-permute-done) | non-fusion elementwise | flops 393216 | bytes 4718592 | tf_op jit(solution)/shard_map/add | solution.py:312
  130.7 7.3 %collective-permute-start.2 = (f16[200,512]{1,0:T(8,128)(2,1)S(1)}, f16[200,512]{1,0:T(8,128)(2,1)S(1)}, u32[]{:S(2)}, u32[]{:S(2)}) collective-permute-start(f16[200,512]{1,0:T(8,128)(2,1)S(1)} %pad_maximum_fusion.1), channel_id=1, source_target_pairs={{0,4},{1,5},{2,6},{3,7},{4,0},{5,1},{6,2},{7,3},{8,12},{9,13},{10,... | collective-permute-start | bytes 614408 | tf_op jit(solution)/shard_map/ppermute | solution.py:217
  138.2 1.7 collective-permute-start.1
  142.1 1.3 collective-permute-done.2
  143.8 2.2 %collective-permute-start.4 = (f16[104,512]{1,0:T(8,128)(2,1)S(1)}, f16[104,512]{1,0:T(8,128)(2,1)S(1)}, u32[]{:S(2)}, u32[]{:S(2)}) collective-permute-start(f16[104,512]{1,0:T(8,128)(2,1)S(1)} %pad_maximum_fusion.7), channel_id=1, source_target_pairs={{0,2},{1,3},{2,0},{3,1},{4,6},{5,7},{6,4},{7,5},{8,10},{9,11},{10,... | collective-permute-start | bytes 319496 | tf_op jit(solution)/shard_map/ppermute | solution.py:217
  146.5 1.8 %collective-permute-start.3 = (f16[104,512]{1,0:T(8,128)(2,1)S(1)}, f16[104,512]{1,0:T(8,128)(2,1)S(1)}, u32[]{:S(2)}, u32[]{:S(2)}) collective-permute-start(f16[104,512]{1,0:T(8,128)(2,1)S(1)} %pad_maximum_fusion.6), channel_id=1, source_target_pairs={{0,4},{1,5},{2,6},{3,7},{4,0},{5,1},{6,2},{7,3},{8,12},{9,13},{10,... | collective-permute-start | bytes 319496 | tf_op jit(solution)/shard_map/ppermute | solution.py:217
  148.6 1.7 %collective-permute-start.10 = (f16[104,512]{1,0:T(8,128)(2,1)S(1)}, f16[104,512]{1,0:T(8,128)(2,1)S(1)}, u32[]{:S(2)}, u32[]{:S(2)}) collective-permute-start(f16[104,512]{1,0:T(8,128)(2,1)S(1)} %pad_maximum_fusion.9), channel_id=1, source_target_pairs={{0,2},{1,3},{2,0},{3,1},{4,6},{5,7},{6,4},{7,5},{8,10},{9,11},{10,... | collective-permute-start | bytes 319496 | tf_op jit(solution)/shard_map/ppermute | solution.py:217
  150.9 1.8 %collective-permute-start.8 = (f16[104,512]{1,0:T(8,128)(2,1)S(1)}, f16[104,512]{1,0:T(8,128)(2,1)S(1)}, u32[]{:S(2)}, u32[]{:S(2)}) collective-permute-start(f16[104,512]{1,0:T(8,128)(2,1)S(1)} %pad_maximum_fusion.8), channel_id=1, source_target_pairs={{0,4},{1,5},{2,6},{3,7},{4,0},{5,1},{6,2},{7,3},{8,12},{9,13},{10,... | collective-permute-start | bytes 319496 | tf_op jit(solution)/shard_map/ppermute | solution.py:217
  152.7 3.5 %attended_out.1 = bf16[768,768]{1,0:T(8,128)(2,1)} custom-call(bf16[16,2,48,768]{3,2,1,0:T(8,128)(2,1)} %all-to-all-done.1.token_in.token_ref, bf16[768,512]{1,0:T(8,128)(2,1)S(1)} %copy-done.2, bf16[512,768]{1,0:T(8,128)(2,1)S(1)} %copy-done.3), custom_call_target="tpu_custom_call" | custom-call | flops 603979776 | bytes 3538944 | tf_op jit(solution)/shard_map/attended_out/pallas_call | solution.py:232
  156.6 3.2 %collective-permute-start.5 = (f16[56,1024]{1,0:T(8,128)(2,1)S(1)}, f16[56,1024]{1,0:T(8,128)(2,1)S(1)}, u32[]{:S(2)}, u32[]{:S(2)}) collective-permute-start(f16[56,1024]{1,0:T(8,128)(2,1)S(1)} %pad_maximum_fusion.4), channel_id=1, source_target_pairs={{0,8},{1,9},{2,10},{3,11},{4,12},{5,13},{6,14},{7,15},{8,0},{9,1},... | collective-permute-start | bytes 344072 | tf_op jit(solution)/shard_map/ppermute | solution.py:217
  160.2 6.9 %collective-permute-done.5 = f16[56,1024]{1,0:T(8,128)(2,1)S(1)} collective-permute-done((f16[56,1024]{1,0:T(8,128)(2,1)S(1)}, f16[56,1024]{1,0:T(8,128)(2,1)S(1)}, u32[]{:S(2)}, u32[]{:S(2)}) %collective-permute-start.5) | collective-permute-done | bytes 114720 | tf_op jit(solution)/shard_map/ppermute | solution.py:217
  (135 shorter events, 11.6 us)
Async XLA Ops:
  0.6 1.4 copy-start
  5.9 7.5 %copy-start.9 = (s32[16,2]{0,1:T(2,128)S(1)}, s32[16,2]{0,1:T(2,128)}, u32[]{:S(2)}) copy-start(s32[16,2]{0,1:T(2,128)} %param.12) | copy-start | bytes 388
  5.9 32.7 %copy-start.4 = (s32[16]{0:T(128)S(1)}, s32[16]{0:T(128)}, u32[]{:S(2)}) copy-start(s32[16]{0:T(128)} %owner_ref.1) | copy-start | bytes 196
  5.9 32.7 %all-to-all-start = ((bf16[16,48,768]{2,1,0:T(8,128)(2,1)}), bf16[16,48,768]{2,1,0:T(8,128)(2,1)S(1)}, u32[]{:S(2)}, u32[]{:S(2)}) async-start(bf16[16,48,768]{2,1,0:T(8,128)(2,1)} %bitcast.131), calls=%async_computation | async-start | bytes 2359296 | tf_op jit(solution)/shard_map/all_to_all | solution.py:289
  39.3 1.4 copy-start.1
  40.7 7.7 %copy-start.6 = (bf16[1,768,768]{2,1,0:T(8,128)(2,1)S(1)}, bf16[1,768,768]{2,1,0:T(8,128)(2,1)}, u32[]{:S(2)}) copy-start(bf16[1,768,768]{2,1,0:T(8,128)(2,1)} %param.14) | copy-start | bytes 3538948
  40.7 53.4 %all-to-all-start.1 = ((bf16[16,2,48,768]{3,2,1,0:T(8,128)(2,1)}), bf16[16,2,48,768]{3,2,1,0:T(8,128)(2,1)}, u32[]{:S(2)}, u32[]{:S(2)}) async-start(bf16[16,2,48,768]{3,2,1,0:T(8,128)(2,1)} %copy-done.1), calls=%async_computation.1 | async-start | bytes 4718592 | tf_op jit(solution)/shard_map/all_to_all | solution.py:293
  48.3 1.5 copy-start.7
  51.0 4.6 %copy-start.8 = (s32[1,12,12]{2,0,1:T(1,128)S(1)}, s32[1,12,12]{2,0,1:T(1,128)}, u32[]{:S(2)}) copy-start(s32[1,12,12]{2,0,1:T(1,128)} %param.13) | copy-start | bytes 1732
  51.0 6.2 %copy-start.2 = (bf16[768,512]{1,0:T(8,128)(2,1)S(1)}, bf16[768,512]{1,0:T(8,128)(2,1)}, u32[]{:S(2)}) copy-start(bf16[768,512]{1,0:T(8,128)(2,1)} %ow_ref.1) | copy-start | bytes 2359300
  122.6 5.6 %collective-permute-start = (f32[8,48,1024]{2,1,0:T(8,128)}, f32[8,48,1024]{2,1,0:T(8,128)}, u32[]{:S(2)}, u32[]{:S(2)}) collective-permute-start(f32[8,48,1024]{2,1,0:T(8,128)} %get-tuple-element.10), channel_id=1, source_target_pairs={{0,1},{1,0},{2,3},{3,2},{4,5},{5,4},{6,7},{7,6},{8,9},{9,8},{10,11... | collective-permute-start | bytes 4718600 | tf_op jit(solution)/shard_map/ppermute | solution.py:217
  123.4 16.4 %collective-permute-start.6 = (f32[8,48,1024]{2,1,0:T(8,128)}, f32[8,48,1024]{2,1,0:T(8,128)S(1)}, u32[]{:S(2)}, u32[]{:S(2)}) collective-permute-start(f32[8,48,1024]{2,1,0:T(8,128)} %get-tuple-element.13), channel_id=1, source_target_pairs={{0,1},{1,0},{2,3},{3,2},{4,5},{5,4},{6,7},{7,6},{8,9},{9,8},{10,11... | collective-permute-start | bytes 4718600 | tf_op jit(solution)/shard_map/ppermute | solution.py:217
  130.5 9.3 %copy-start.5 = (f32[8,48,1024]{2,1,0:T(8,128)S(1)}, f32[8,48,1024]{2,1,0:T(8,128)}, u32[]{:S(2)}) copy-start(f32[8,48,1024]{2,1,0:T(8,128)} %get-tuple-element.12) | copy-start | bytes 4718596
  130.7 12.8 %collective-permute-start.2 = (f16[200,512]{1,0:T(8,128)(2,1)S(1)}, f16[200,512]{1,0:T(8,128)(2,1)S(1)}, u32[]{:S(2)}, u32[]{:S(2)}) collective-permute-start(f16[200,512]{1,0:T(8,128)(2,1)S(1)} %pad_maximum_fusion.1), channel_id=1, source_target_pairs={{0,4},{1,5},{2,6},{3,7},{4,0},{5,1},{6,2},{7,3},{8,12},{9,13},{10,... | collective-permute-start | bytes 614408 | tf_op jit(solution)/shard_map/ppermute | solution.py:217
  138.2 8.0 %collective-permute-start.1 = (f16[200,512]{1,0:T(8,128)(2,1)S(1)}, f16[200,512]{1,0:T(8,128)(2,1)S(1)}, u32[]{:S(2)}, u32[]{:S(2)}) collective-permute-start(f16[200,512]{1,0:T(8,128)(2,1)S(1)} %pad_maximum_fusion), channel_id=1, source_target_pairs={{0,2},{1,3},{2,0},{3,1},{4,6},{5,7},{6,4},{7,5},{8,10},{9,11},{10,... | collective-permute-start | bytes 614408 | tf_op jit(solution)/shard_map/ppermute | solution.py:217
  140.8 7.5 %collective-permute-start.9 = (f16[200,512]{1,0:T(8,128)(2,1)S(1)}, f16[200,512]{1,0:T(8,128)(2,1)S(1)}, u32[]{:S(2)}, u32[]{:S(2)}) collective-permute-start(f16[200,512]{1,0:T(8,128)(2,1)S(1)} %pad_maximum_fusion.3), channel_id=1, source_target_pairs={{0,4},{1,5},{2,6},{3,7},{4,0},{5,1},{6,2},{7,3},{8,12},{9,13},{10,... | collective-permute-start | bytes 614408 | tf_op jit(solution)/shard_map/ppermute | solution.py:217
  141.1 9.5 %collective-permute-start.7 = (f16[200,512]{1,0:T(8,128)(2,1)S(1)}, f16[200,512]{1,0:T(8,128)(2,1)S(1)}, u32[]{:S(2)}, u32[]{:S(2)}) collective-permute-start(f16[200,512]{1,0:T(8,128)(2,1)S(1)} %pad_maximum_fusion.2), channel_id=1, source_target_pairs={{0,2},{1,3},{2,0},{3,1},{4,6},{5,7},{6,4},{7,5},{8,10},{9,11},{10,... | collective-permute-start | bytes 614408 | tf_op jit(solution)/shard_map/ppermute | solution.py:217
  143.8 12.5 %collective-permute-start.4 = (f16[104,512]{1,0:T(8,128)(2,1)S(1)}, f16[104,512]{1,0:T(8,128)(2,1)S(1)}, u32[]{:S(2)}, u32[]{:S(2)}) collective-permute-start(f16[104,512]{1,0:T(8,128)(2,1)S(1)} %pad_maximum_fusion.7), channel_id=1, source_target_pairs={{0,2},{1,3},{2,0},{3,1},{4,6},{5,7},{6,4},{7,5},{8,10},{9,11},{10,... | collective-permute-start | bytes 319496 | tf_op jit(solution)/shard_map/ppermute | solution.py:217
  146.5 9.8 %collective-permute-start.3 = (f16[104,512]{1,0:T(8,128)(2,1)S(1)}, f16[104,512]{1,0:T(8,128)(2,1)S(1)}, u32[]{:S(2)}, u32[]{:S(2)}) collective-permute-start(f16[104,512]{1,0:T(8,128)(2,1)S(1)} %pad_maximum_fusion.6), channel_id=1, source_target_pairs={{0,4},{1,5},{2,6},{3,7},{4,0},{5,1},{6,2},{7,3},{8,12},{9,13},{10,... | collective-permute-start | bytes 319496 | tf_op jit(solution)/shard_map/ppermute | solution.py:217
  148.6 11.1 %collective-permute-start.10 = (f16[104,512]{1,0:T(8,128)(2,1)S(1)}, f16[104,512]{1,0:T(8,128)(2,1)S(1)}, u32[]{:S(2)}, u32[]{:S(2)}) collective-permute-start(f16[104,512]{1,0:T(8,128)(2,1)S(1)} %pad_maximum_fusion.9), channel_id=1, source_target_pairs={{0,2},{1,3},{2,0},{3,1},{4,6},{5,7},{6,4},{7,5},{8,10},{9,11},{10,... | collective-permute-start | bytes 319496 | tf_op jit(solution)/shard_map/ppermute | solution.py:217
  150.6 2.1 %copy-start.3 = (bf16[512,768]{1,0:T(8,128)(2,1)S(1)}, bf16[512,768]{1,0:T(8,128)(2,1)}, u32[]{:S(2)}) copy-start(bf16[512,768]{1,0:T(8,128)(2,1)} %get-tuple-element.11.ctx_ref) | copy-start | bytes 2359300
  150.9 9.0 %collective-permute-start.8 = (f16[104,512]{1,0:T(8,128)(2,1)S(1)}, f16[104,512]{1,0:T(8,128)(2,1)S(1)}, u32[]{:S(2)}, u32[]{:S(2)}) collective-permute-start(f16[104,512]{1,0:T(8,128)(2,1)S(1)} %pad_maximum_fusion.8), channel_id=1, source_target_pairs={{0,4},{1,5},{2,6},{3,7},{4,0},{5,1},{6,2},{7,3},{8,12},{9,13},{10,... | collective-permute-start | bytes 319496 | tf_op jit(solution)/shard_map/ppermute | solution.py:217
  156.6 10.6 %collective-permute-start.5 = (f16[56,1024]{1,0:T(8,128)(2,1)S(1)}, f16[56,1024]{1,0:T(8,128)(2,1)S(1)}, u32[]{:S(2)}, u32[]{:S(2)}) collective-permute-start(f16[56,1024]{1,0:T(8,128)(2,1)S(1)} %pad_maximum_fusion.4), channel_id=1, source_target_pairs={{0,8},{1,9},{2,10},{3,11},{4,12},{5,13},{6,14},{7,15},{8,0},{9,1},... | collective-permute-start | bytes 344072 | tf_op jit(solution)/shard_map/ppermute | solution.py:217
  160.1 8.3 %collective-permute-start.11 = (f16[56,1024]{1,0:T(8,128)(2,1)S(1)}, f16[56,1024]{1,0:T(8,128)(2,1)S(1)}, u32[]{:S(2)}, u32[]{:S(2)}) collective-permute-start(f16[56,1024]{1,0:T(8,128)(2,1)S(1)} %pad_maximum_fusion.5), channel_id=1, source_target_pairs={{0,8},{1,9},{2,10},{3,11},{4,12},{5,13},{6,14},{7,15},{8,0},{9,1},... | collective-permute-start | bytes 344072 | tf_op jit(solution)/shard_map/ppermute | solution.py:217
